TPU v7x, 32 devices: a whole 2x2x4 slice. The times are simulated.
32 devices in a mesh: dp: 8 (over z, y), tensor: 4 (over x, core).
Axes of the slice: x: 2, y: 2, z: 4, core: 2. Of those that a mesh axis runs over, the one named last changes fastest.
Arguments:
- hidden_in: bfloat16 [8, 1024, 2048], P('dp', 'tensor'), may hold values from -6 to 6
- out_grad: bfloat16 [8, 1024, 2048], P('dp', 'tensor'), may hold values from -6 to 6
- segment_ids: int32 [8, 1024], P('dp'), may hold values from 0 to 3, never falling along the last dimension, each value on 1 to 512 neighbouring positions
- norm1_gain: bfloat16 [2048], P('dp'), may hold values from 0.5 to 1.5
- w_query: bfloat16 [2048, 2048], P('dp', 'tensor'), may hold values from -0.125 to 0.125
- w_key: bfloat16 [2048, 2048], P('dp', 'tensor'), may hold values from -0.125 to 0.125
- w_value: bfloat16 [2048, 3456], P('dp', 'tensor'), may hold values from -0.125 to 0.125
- w_gate: bfloat16 [2048, 3456], P('dp', 'tensor'), may hold values from -0.125 to 0.125
- w_out: bfloat16 [3456, 2048], P('tensor', 'dp'), may hold values from -0.109375 to 0.109375
- norm2_gain: bfloat16 [2048], P('dp'), may hold values from 0.5 to 1.5
- w_mlp_gate: bfloat16 [2048, 3456], P('dp', 'tensor'), may hold values from -0.125 to 0.125
- w_mlp_up: bfloat16 [2048, 3456], P('dp', 'tensor'), may hold values from -0.125 to 0.125
- w_mlp_down: bfloat16 [3456, 2048], P('tensor', 'dp'), may hold values from -0.109375 to 0.109375
Outputs:
- hidden_out: bfloat16 [8, 1024, 2048], P('dp', 'tensor')
- in_grad: float32 [8, 1024, 2048], P('dp', 'tensor')
- norm1_gain_grad: float32 [2048], P('dp')
- w_query_grad: float32 [2048, 2048], P('dp', 'tensor')
- w_key_grad: float32 [2048, 2048], P('dp', 'tensor')
- w_value_grad: float32 [2048, 3456], P('dp', 'tensor')
- w_gate_grad: float32 [2048, 3456], P('dp', 'tensor')
- w_out_grad: float32 [3456, 2048], P('tensor', 'dp')
- norm2_gain_grad: float32 [2048], P('dp')
- w_mlp_gate_grad: float32 [2048, 3456], P('dp', 'tensor')
- w_mlp_up_grad: float32 [2048, 3456], P('dp', 'tensor')
- w_mlp_down_grad: float32 [3456, 2048], P('tensor', 'dp')
Inputs may be any that keep to these rules, and one draw needn't show every extreme that they name: `segment_ids`: along a sequence segment numbers never fall; each number marks one document of at most 512 tokens, and some document has exactly that many.
All inputs are finite; a program needn't handle non-finite values.
Results may differ from a plain program's by a relative error of at most 0.015.
Values may be sent and summed in bfloat16 or wider, within the bound.
A program may use at most 192 MiB of HBM per device.

v0:
```python
import jax
import jax.numpy as jnp
from jax import lax
from jax.sharding import PartitionSpec as P

KEY = 256
VAL = 432


def multiply(left, right):
    return jnp.dot(left, right, preferred_element_type=jnp.float32)


def multiply_left(left, right):
    return lax.dot_general(
        left, right, (((0,), (0,)), ((), ())), preferred_element_type=jnp.float32
    )


def multiply_right(left, right):
    return lax.dot_general(
        left, right, (((1,), (1,)), ((), ())), preferred_element_type=jnp.float32
    )


def rms_scale(values, gain):
    return values * lax.rsqrt(jnp.mean(values * values, axis=-1, keepdims=True) + 1e-06) * gain


def group_norm(values):
    centred = values - jnp.mean(values, axis=-1, keepdims=True)
    return centred * lax.rsqrt(jnp.mean(centred * centred, axis=-1, keepdims=True) + 1.0)


def rotary_tables(length, width):
    half = width // 2
    frequency = 10000.0 ** (-2.0 * jnp.arange(half, dtype=jnp.int32).astype(jnp.float32) / width)
    angle = jnp.arange(length, dtype=jnp.int32).astype(jnp.float32)[:, None] * frequency[None, :]
    return (jnp.cos(angle), jnp.sin(angle))


def rotate(values, cosine, sine):
    half = values.shape[-1] // 2
    first = values[..., :half]
    second = values[..., half:]
    return jnp.concatenate(
        [first * cosine - second * sine, second * cosine + first * sine], axis=-1
    )


def decay_mask(segments, first_head, count):
    length = segments.shape[-1]
    position = jnp.arange(length, dtype=jnp.int32)
    distance = position[:, None] - position[None, :]
    same = (distance >= 0) & (segments[..., :, None] == segments[..., None, :])
    heads = (jnp.arange(count, dtype=jnp.int32) + first_head).astype(jnp.float32)
    rates = jnp.log1p(-jnp.exp2(-5.0 - heads))
    steps_back = jnp.maximum(distance, 0).astype(jnp.float32)
    decay = jnp.exp(rates[:, None, None] * steps_back[None, :, :])
    return jnp.where(same[..., None, :, :], decay, jnp.zeros((), jnp.float32))


def on_device(
    hidden_in,
    out_grad,
    segment_ids,
    norm1_gain,
    w_query,
    w_key,
    w_value,
    w_gate,
    w_out,
    norm2_gain,
    w_mlp_gate,
    w_mlp_up,
    w_mlp_down,
):
    seqs_here, local_len, width = hidden_in.shape
    length = local_len * lax.axis_size("tensor")
    rows = local_len * seqs_here
    rows_full = length * seqs_here
    attention_set = (
        lax.all_gather(norm1_gain, "dp", axis=0, tiled=True),
        lax.all_gather(w_query, "dp", axis=0, tiled=True),
        lax.all_gather(w_key, "dp", axis=0, tiled=True),
        lax.all_gather(w_value, "dp", axis=0, tiled=True),
        lax.all_gather(w_gate, "dp", axis=0, tiled=True),
        lax.all_gather(w_out, "dp", axis=1, tiled=True),
    )
    gain_one, query_weight, key_weight, value_weight, gate_weight, out_weight = attention_set
    heads_here = query_weight.shape[1] // KEY
    first_head = lax.axis_index("tensor") * heads_here
    resid_in = jnp.swapaxes(hidden_in, 0, 1).reshape(rows, width).astype(jnp.float32)
    gain_first = gain_one.astype(jnp.float32)
    normed_local = rms_scale(resid_in, gain_first).astype(jnp.bfloat16)
    normed_full = lax.all_gather(normed_local, "tensor", axis=0, tiled=True)
    cosine, sine = rotary_tables(length, KEY)
    cosine = cosine[:, None, None, :]
    sine = sine[:, None, None, :]
    query_pre = multiply(normed_full, query_weight)
    key_pre = multiply(normed_full, key_weight)
    values = multiply(normed_full, value_weight).astype(jnp.bfloat16)
    gate_pre = multiply(normed_full, gate_weight)
    key_shape = (length, seqs_here, heads_here, KEY)
    query = (rotate(query_pre.reshape(key_shape), cosine, sine) * KEY ** (-0.5)).astype(
        jnp.bfloat16
    )
    keys = rotate(key_pre.reshape(key_shape), cosine, sine).astype(jnp.bfloat16)
    value_four = values.reshape(length, seqs_here, heads_here, VAL)

    def retention_scores():
        mask = decay_mask(segment_ids, first_head, heads_here)
        raw = jnp.einsum("nshk,mshk->shnm", query, keys, preferred_element_type=jnp.float32)
        return (raw * mask, mask)

    weighted, mask = retention_scores()
    scores_low = weighted.astype(jnp.bfloat16)
    retained = jnp.einsum(
        "shnm,mshv->nshv", scores_low, value_four, preferred_element_type=jnp.float32
    ).reshape(rows_full, heads_here * VAL)

    def gate_mix(retained_in, gate_in):
        grouped = group_norm(retained_in.reshape(retained_in.shape[0], heads_here, VAL)).reshape(
            retained_in.shape
        )
        return grouped * jax.nn.silu(gate_in)

    mixed = gate_mix(retained, gate_pre).astype(jnp.bfloat16)
    resid_mid = resid_in + lax.psum_scatter(
        multiply(mixed, out_weight), "tensor", scatter_dimension=0, tiled=True
    )
    feed_set = (
        lax.all_gather(norm2_gain, "dp", axis=0, tiled=True),
        lax.all_gather(w_mlp_gate, "dp", axis=0, tiled=True),
        lax.all_gather(w_mlp_up, "dp", axis=0, tiled=True),
        lax.all_gather(w_mlp_down, "dp", axis=1, tiled=True),
    )
    gain_two, mlp_gate_weight, mlp_up_weight, mlp_down_weight = feed_set
    gain_second = gain_two.astype(jnp.float32)
    normed_mid = rms_scale(resid_mid, gain_second).astype(jnp.bfloat16)
    normed_mid_full = lax.all_gather(normed_mid, "tensor", axis=0, tiled=True)
    gate_hidden = multiply(normed_mid_full, mlp_gate_weight)
    up_hidden = multiply(normed_mid_full, mlp_up_weight)

    def gelu_mix(gate_in, up_in):
        return jax.nn.gelu(gate_in, approximate=True) * up_in

    hidden = gelu_mix(gate_hidden, up_hidden).astype(jnp.bfloat16)
    resid_out = resid_mid + lax.psum_scatter(
        multiply(hidden, mlp_down_weight), "tensor", scatter_dimension=0, tiled=True
    )
    hidden_out = jnp.swapaxes(resid_out.reshape(local_len, seqs_here, width), 0, 1).astype(
        jnp.bfloat16
    )
    grad_local = jnp.swapaxes(out_grad, 0, 1).reshape(rows, width)
    grad_full = lax.all_gather(grad_local, "tensor", axis=0, tiled=True)
    down_weight_grad = multiply_left(hidden, grad_full)
    hidden_grad = multiply_right(grad_full, mlp_down_weight)
    _, pull_mix = jax.vjp(gelu_mix, gate_hidden, up_hidden)
    gate_hidden_grad, up_hidden_grad = pull_mix(hidden_grad)
    gate_low = gate_hidden_grad.astype(jnp.bfloat16)
    up_low = up_hidden_grad.astype(jnp.bfloat16)
    mlp_gate_grad = multiply_left(normed_mid_full, gate_low)
    mlp_up_grad = multiply_left(normed_mid_full, up_low)
    normed_mid_grad = lax.psum_scatter(
        multiply_right(gate_low, mlp_gate_weight) + multiply_right(up_low, mlp_up_weight),
        "tensor",
        scatter_dimension=0,
        tiled=True,
    )
    _, pull_second = jax.vjp(rms_scale, resid_mid, gain_second)
    mid_from_norm, gain_second_part = pull_second(normed_mid_grad)
    resid_mid_grad = grad_local.astype(jnp.float32) + mid_from_norm
    mid_low = resid_mid_grad.astype(jnp.bfloat16)
    mid_full = lax.all_gather(mid_low, "tensor", axis=0, tiled=True)
    out_weight_grad = multiply_left(mixed, mid_full)
    mixed_grad = multiply_right(mid_full, out_weight)
    _, pull_gate = jax.vjp(gate_mix, retained, gate_pre)
    retained_grad, gate_pre_grad = pull_gate(mixed_grad)
    retained_low = retained_grad.astype(jnp.bfloat16).reshape(length, seqs_here, heads_here, VAL)
    gate_pre_low = gate_pre_grad.astype(jnp.bfloat16)
    weighted, mask = retention_scores()
    scores_low = weighted.astype(jnp.bfloat16)
    score_grad = jnp.einsum(
        "nshv,mshv->shnm", retained_low, value_four, preferred_element_type=jnp.float32
    )
    raw_grad = (score_grad * mask).astype(jnp.bfloat16)
    query_grad = jnp.einsum("shnm,mshk->nshk", raw_grad, keys, preferred_element_type=jnp.float32)
    key_grad = jnp.einsum("shnm,nshk->mshk", raw_grad, query, preferred_element_type=jnp.float32)
    value_grad = (
        jnp.einsum("shnm,nshv->mshv", scores_low, retained_low, preferred_element_type=jnp.float32)
        .astype(jnp.bfloat16)
        .reshape(rows_full, heads_here * VAL)
    )
    query_pre_grad = (
        (rotate(query_grad, cosine, -sine) * KEY ** (-0.5))
        .astype(jnp.bfloat16)
        .reshape(rows_full, heads_here * KEY)
    )
    key_pre_grad = (
        rotate(key_grad, cosine, -sine).astype(jnp.bfloat16).reshape(rows_full, heads_here * KEY)
    )
    query_weight_grad = multiply_left(normed_full, query_pre_grad)
    key_weight_grad = multiply_left(normed_full, key_pre_grad)
    value_weight_grad = multiply_left(normed_full, value_grad)
    gate_weight_grad = multiply_left(normed_full, gate_pre_low)
    total = multiply_right(query_pre_grad, query_weight)
    total = total + multiply_right(key_pre_grad, key_weight)
    total = total + multiply_right(value_grad, value_weight)
    normed_grad = lax.psum_scatter(
        total + multiply_right(gate_pre_low, gate_weight), "tensor", scatter_dimension=0, tiled=True
    )
    _, pull_first = jax.vjp(rms_scale, resid_in, gain_first)
    in_from_norm, gain_first_part = pull_first(normed_grad)
    in_rows = resid_mid_grad + in_from_norm
    in_grad = jnp.swapaxes(in_rows.reshape(local_len, seqs_here, width), 0, 1)
    collected = (
        lax.psum_scatter(gain_first_part, "dp", scatter_dimension=0, tiled=True),
        lax.psum_scatter(query_weight_grad, "dp", scatter_dimension=0, tiled=True),
        lax.psum_scatter(key_weight_grad, "dp", scatter_dimension=0, tiled=True),
        lax.psum_scatter(value_weight_grad, "dp", scatter_dimension=0, tiled=True),
        lax.psum_scatter(gate_weight_grad, "dp", scatter_dimension=0, tiled=True),
        lax.psum_scatter(out_weight_grad, "dp", scatter_dimension=1, tiled=True),
        lax.psum_scatter(gain_second_part, "dp", scatter_dimension=0, tiled=True),
        lax.psum_scatter(mlp_gate_grad, "dp", scatter_dimension=0, tiled=True),
        lax.psum_scatter(mlp_up_grad, "dp", scatter_dimension=0, tiled=True),
        lax.psum_scatter(down_weight_grad, "dp", scatter_dimension=1, tiled=True),
    )
    gain_first_total, gain_second_total = lax.psum((collected[0], collected[6]), "tensor")
    return (
        hidden_out,
        in_grad,
        gain_first_total,
        collected[1],
        collected[2],
        collected[3],
        collected[4],
        collected[5],
        gain_second_total,
        collected[7],
        collected[8],
        collected[9],
    )


def solution(mesh):
    return jax.shard_map(
        on_device,
        mesh=mesh,
        in_specs=(
            P("dp", "tensor", None),
            P("dp", "tensor", None),
            P("dp", None),
            P("dp"),
            P("dp", "tensor"),
            P("dp", "tensor"),
            P("dp", "tensor"),
            P("dp", "tensor"),
            P("tensor", "dp"),
            P("dp"),
            P("dp", "tensor"),
            P("dp", "tensor"),
            P("tensor", "dp"),
        ),
        out_specs=(
            P("dp", "tensor", None),
            P("dp", "tensor", None),
            P("dp"),
            P("dp", "tensor"),
            P("dp", "tensor"),
            P("dp", "tensor"),
            P("dp", "tensor"),
            P("tensor", "dp"),
            P("dp"),
            P("dp", "tensor"),
            P("dp", "tensor"),
            P("tensor", "dp"),
        ),
        check_vma=False,
    )
```

profile of v0, /device:TPU:8, one launch (start us, length us, event | category | flops | bytes accessed | tf_op | source)
XLA Modules:
  0.0 2044.3 jit_solution(3336040535537134835)
XLA Ops:
  8.6 18.0 all-gather.1
  29.3 2.5 fusion.22
  34.4 2.5 maximum_convert_fusion
  36.9 2.9 fusion.35
  41.5 19.2 all-gather.22.cloned.1.call-done
  60.6 35.1 %all-gather.16.cloned.1.call-done = bf16[1024,2048]{1,0:T(8,128)(2,1)} async-done(((bf16[256,2048]{1,0:T(8,128)(2,1)}), bf16[1024,2048]{1,0:T(8,128)(2,1)}) %all-gather.16.cloned.1.call-update) | async-done | bytes 4194320 | tf_op jit(solution)/shard_map/all_gather | solution.py:96
  95.8 5.2 fusion.51
  103.9 43.4 %all-gather.20.cloned.1.call-done = bf16[2048,512]{1,0:T(8,128)(2,1)} async-done(((bf16[256,512]{1,0:T(8,128)(2,1)}), bf16[2048,512]{1,0:T(8,128)(2,1)}) %all-gather.20.cloned.1.call-update) | async-done | bytes 2097168 | tf_op jit(solution)/shard_map/all_gather | solution.py:84
  147.2 5.2 fusion.50
  154.3 2.8 subtract_bitcast_fusion
  158.4 4.2 multiply_convert_fusion.1
  162.6 50.7 %all-gather.18.cloned.1.call-done = bf16[2048,864]{0,1:T(8,128)(2,1)} async-done(((bf16[256,864]{0,1:T(8,128)(2,1)}), bf16[2048,864]{0,1:T(8,128)(2,1)}) %all-gather.18.cloned.1.call-update) | async-done | bytes 3538960 | tf_op jit(solution)/shard_map/all_gather | solution.py:86
  213.4 7.3 convolution_convert_fusion.1
  220.7 2.1 bitcast_reduce_fusion
  223.8 57.2 %all-gather.24.cloned.1.call-done = bf16[2048,864]{0,1:T(8,128)(2,1)} async-done(((bf16[256,864]{0,1:T(8,128)(2,1)}), bf16[2048,864]{0,1:T(8,128)(2,1)}) %all-gather.24.cloned.1.call-update) | async-done | bytes 3538960 | tf_op jit(solution)/shard_map/all_gather | solution.py:87
  281.0 10.1 multiply_convert_fusion.4
  291.1 57.6 %all-gather.26.cloned.1.call-done = bf16[864,2048]{1,0:T(8,128)(2,1)} async-done(((bf16[864,256]{1,0:T(8,128)(2,1)}), bf16[864,2048]{1,0:T(8,128)(2,1)}) %all-gather.26.cloned.1.call-update) | async-done | bytes 3538960 | tf_op jit(solution)/shard_map/all_gather | solution.py:88
  348.7 10.9 fusion.52
  360.4 16.8 all-gather.2
  377.3 54.2 %reduce-scatter.13.cloned.1.call-done = f32[256,2048]{1,0:T(8,128)} async-done(((f32[1024,2048]{1,0:T(8,128)}), f32[256,2048]{1,0:T(8,128)}) %reduce-scatter.13.cloned.1.call-update) | async-done | bytes 2097168 | tf_op jit(solution)/shard_map/reduce_scatter | solution.py:129
  431.5 2.2 multiply_reduce_fusion.4
  438.2 61.3 %all-gather.32.cloned.1.call-done = bf16[2048,864]{0,1:T(8,128)(2,1)} async-done(((bf16[256,864]{0,1:T(8,128)(2,1)}), bf16[2048,864]{0,1:T(8,128)(2,1)}) %all-gather.32.cloned.1.call-update) | async-done | bytes 3538960 | tf_op jit(solution)/shard_map/all_gather | solution.py:135
  499.5 36.8 %all-gather.28.cloned.1.call-done = bf16[1024,2048]{1,0:T(8,128)(2,1)} async-done(((bf16[256,2048]{1,0:T(8,128)(2,1)}), bf16[1024,2048]{1,0:T(8,128)(2,1)}) %all-gather.28.cloned.1.call-update) | async-done | bytes 4194320 | tf_op jit(solution)/shard_map/all_gather | solution.py:141
  536.3 8.9 fusion.54
  545.1 59.0 %all-gather.30.cloned.1.call-done = bf16[2048,864]{0,1:T(8,128)(2,1)} async-done(((bf16[256,864]{0,1:T(8,128)(2,1)}), bf16[2048,864]{0,1:T(8,128)(2,1)}) %all-gather.30.cloned.1.call-update) | async-done | bytes 3538960 | tf_op jit(solution)/shard_map/all_gather | solution.py:134
  604.1 8.9 fusion.53
  613.0 59.2 %all-gather.34.cloned.1.call-done = bf16[864,2048]{1,0:T(8,128)(2,1)} async-done(((bf16[864,256]{1,0:T(8,128)(2,1)}), bf16[864,2048]{1,0:T(8,128)(2,1)}) %all-gather.34.cloned.1.call-update) | async-done | bytes 3538960 | tf_op jit(solution)/shard_map/all_gather | solution.py:136
  672.1 36.0 %all-gather.38.cloned.1.call-done = bf16[1,1024,2048]{2,1,0:T(8,128)(2,1)} async-done(((bf16[1,256,2048]{2,1,0:T(8,128)(2,1)}), bf16[1,1024,2048]{2,1,0:T(8,128)(2,1)}) %all-gather.38.cloned.1.call-update) | async-done | bytes 4194320 | tf_op jit(solution)/shard_map/all_gather | solution.py:156
  708.1 12.0 multiply_convert_fusion.2
  720.2 4.6 fusion.56
  724.8 7.1 convolution_add_fusion
  732.1 71.8 %reduce-scatter.17.cloned.1.call-done = f32[256,2048]{1,0:T(8,128)} async-done(((f32[1024,2048]{1,0:T(8,128)}), f32[256,2048]{1,0:T(8,128)}) %reduce-scatter.17.cloned.1.call-update) | async-done | bytes 2097168 | tf_op jit(solution)/shard_map/reduce_scatter | solution.py:165
  803.9 3.5 multiply_reduce_fusion.2
  808.0 3.0 fusion.47
  811.3 34.4 %all-gather.36.cloned.1.call-done = bf16[1024,2048]{1,0:T(8,128)(2,1)} async-done(((bf16[256,2048]{1,0:T(8,128)(2,1)}), bf16[1024,2048]{1,0:T(8,128)(2,1)}) %all-gather.36.cloned.1.call-update) | async-done | bytes 4194320 | tf_op jit(solution)/shard_map/all_gather | solution.py:175
  845.6 10.6 fusion.32
  861.1 4.1 multiply_convert_fusion
  865.2 3.3 convolution_convert_fusion
  876.6 7.3 fusion.58
  884.0 6.9 fusion.59
  890.9 5.7 fusion.57
  896.6 12.1 add_add_fusion
  908.9 12.0 fusion.55
  921.2 10.4 fusion
  931.6 10.2 fusion.66
  941.9 9.5 fusion.65
  951.5 7.1 fusion.60
  958.9 6.6 fusion.61
  967.1 7.9 fusion.62
  975.1 8.0 fusion.64
  984.5 8.4 fusion.63
  995.4 2.8 fusion.23
  998.2 34.3 %all-reduce.2 = (f32[2048]{0:T(1024)S(1)}, f32[2048]{0:T(1024)S(1)}) all-reduce(f32[2048]{0:T(1024)S(1)} %get-tuple-element.14, f32[2048]{0:T(1024)S(1)} %copy-done.31), channel_id=7, replica_groups=mesh['dp'=8,'tensor'=4] {'dp'}, use_global_device_ids=true, to_apply=%region_13.14.clone | all-reduce | flops 4096 | bytes 32768
  1032.7 6.7 all-reduce.3
  1039.4 15.8 reduce-scatter.15.cloned.1.call-done
  1055.2 5.9 fusion.26
  1061.2 126.7 %reduce-scatter.35.cloned.1.call-done = f32[864,256]{1,0:T(8,128)} async-done(((f32[864,2048]{1,0:T(8,128)}), f32[864,256]{1,0:T(8,128)}) %reduce-scatter.35.cloned.1.call-update) | async-done | bytes 884752 | tf_op jit(solution)/shard_map/reduce_scatter | solution.py:227
  1187.9 133.1 %reduce-scatter.33.cloned.1.call-done = f32[256,864]{0,1:T(8,128)} async-done(((f32[2048,864]{0,1:T(8,128)}), f32[256,864]{0,1:T(8,128)}) %reduce-scatter.33.cloned.1.call-update) | async-done | bytes 884752 | tf_op jit(solution)/shard_map/reduce_scatter | solution.py:226
  1321.0 132.8 %reduce-scatter.31.cloned.1.call-done = f32[256,864]{0,1:T(8,128)} async-done(((f32[2048,864]{0,1:T(8,128)}), f32[256,864]{0,1:T(8,128)}) %reduce-scatter.31.cloned.1.call-update) | async-done | bytes 884752 | tf_op jit(solution)/shard_map/reduce_scatter | solution.py:225
  1453.7 92.6 %reduce-scatter.21.cloned.1.call-done = f32[256,512]{1,0:T(8,128)} async-done(((f32[2048,512]{1,0:T(8,128)}), f32[256,512]{1,0:T(8,128)}) %reduce-scatter.21.cloned.1.call-update) | async-done | bytes 524304 | tf_op jit(solution)/shard_map/reduce_scatter | solution.py:219
  1546.4 91.9 %reduce-scatter.23.cloned.1.call-done = f32[256,512]{1,0:T(8,128)} async-done(((f32[2048,512]{1,0:T(8,128)}), f32[256,512]{1,0:T(8,128)}) %reduce-scatter.23.cloned.1.call-update) | async-done | bytes 524304 | tf_op jit(solution)/shard_map/reduce_scatter | solution.py:220
  1638.3 132.8 %reduce-scatter.29.cloned.1.call-done = f32[864,256]{1,0:T(8,128)} async-done(((f32[864,2048]{1,0:T(8,128)}), f32[864,256]{1,0:T(8,128)}) %reduce-scatter.29.cloned.1.call-update) | async-done | bytes 884752 | tf_op jit(solution)/shard_map/reduce_scatter | solution.py:223
  1771.1 132.8 %reduce-scatter.27.cloned.1.call-done = f32[256,864]{0,1:T(8,128)} async-done(((f32[2048,864]{0,1:T(8,128)}), f32[256,864]{0,1:T(8,128)}) %reduce-scatter.27.cloned.1.call-update) | async-done | bytes 884752 | tf_op jit(solution)/shard_map/reduce_scatter | solution.py:222
  1903.9 133.1 %reduce-scatter.25.cloned.1.call-done = f32[256,864]{0,1:T(8,128)} async-done(((f32[2048,864]{0,1:T(8,128)}), f32[256,864]{0,1:T(8,128)}) %reduce-scatter.25.cloned.1.call-update) | async-done | bytes 884752 | tf_op jit(solution)/shard_map/reduce_scatter | solution.py:221
  (203 shorter events, 39.4 us)
Async XLA Ops:
  7.2 53.5 %all-gather.22.cloned.1.call-start = ((), (), s32[]{:S(2)}) async-start(), calls=%async_computation.15 | async-start | bytes 2359296 | tf_op jit(solution)/shard_map/all_gather | solution.py:85
  7.9 87.9 %all-gather.16.cloned.1.call-start = ((), (), s32[]{:S(2)}) async-start(), calls=%async_computation.12 | async-start | bytes 5242880 | tf_op jit(solution)/shard_map/all_gather | solution.py:96
  26.6 2.1 copy-start.27
  31.8 115.4 %all-gather.20.cloned.1.call-start = ((), (), s32[]{:S(2)}) async-start(), calls=%async_computation.14 | async-start | bytes 2359296 | tf_op jit(solution)/shard_map/all_gather | solution.py:84
  32.6 7.3 copy-start.35
  32.6 180.8 %all-gather.18.cloned.1.call-start = ((), (), s32[]{:S(2)}) async-start(), calls=%async_computation.13 | async-start | bytes 3981312 | tf_op jit(solution)/shard_map/all_gather | solution.py:86
  33.2 247.9 %all-gather.24.cloned.1.call-start = ((), (), s32[]{:S(2)}) async-start(), calls=%async_computation.16 | async-start | bytes 3981312 | tf_op jit(solution)/shard_map/all_gather | solution.py:87
  33.8 315.0 %all-gather.26.cloned.1.call-start = ((), (), s32[]{:S(2)}) async-start(), calls=%async_computation.17 | async-start | bytes 3981312 | tf_op jit(solution)/shard_map/all_gather | solution.py:88
  34.3 397.2 %reduce-scatter.13.cloned.1.call-start = ((), (), s32[]{:S(2)}) async-start(), calls=%async_computation.18 | async-start | bytes 10485760 | tf_op jit(solution)/shard_map/reduce_scatter | solution.py:129
  34.4 122.7 %copy-start.52 = (f32[2]{0:T(128)}, f32[2]{0:T(128)S(1)}, u32[]{:S(2)}) copy-start(f32[2]{0:T(128)S(1)} %negate_log-plus-one_fusion) | copy-start | bytes 28
  39.9 114.4 %copy-start.5 = (f32[1024,128]{1,0:T(8,128)}, f32[1024,128]{1,0:T(8,128)S(1)}, u32[]{:S(2)}) copy-start(f32[1024,128]{1,0:T(8,128)S(1)} %get-tuple-element.47) | copy-start | bytes 1572868
  154.3 4.1 copy-start.7
  154.3 4.1 copy-start.18
  157.1 5.5 copy-start.9
  213.4 7.3 copy-start.55
  220.6 2.1 copy-start.48
  223.8 67.3 %copy-start.25 = (f32[1024,2]{0,1:T(2,128)}, f32[1024,2]{0,1:T(2,128)S(1)}, u32[]{:S(2)}) copy-start(f32[1024,2]{0,1:T(2,128)S(1)} %fusion.38) | copy-start | bytes 24580
  359.6 139.9 %all-gather.32.cloned.1.call-start = ((), (), s32[]{:S(2)}) async-start(), calls=%async_computation.21 | async-start | bytes 3981312 | tf_op jit(solution)/shard_map/all_gather | solution.py:135
  360.3 175.9 %all-gather.28.cloned.1.call-start = ((), (), s32[]{:S(2)}) async-start(), calls=%async_computation.19 | async-start | bytes 5242880 | tf_op jit(solution)/shard_map/all_gather | solution.py:141
  436.3 167.8 %all-gather.30.cloned.1.call-start = ((), (), s32[]{:S(2)}) async-start(), calls=%async_computation.20 | async-start | bytes 3981312 | tf_op jit(solution)/shard_map/all_gather | solution.py:134
  436.9 235.2 %all-gather.34.cloned.1.call-start = ((), (), s32[]{:S(2)}) async-start(), calls=%async_computation.22 | async-start | bytes 3981312 | tf_op jit(solution)/shard_map/all_gather | solution.py:136
  437.6 270.5 %all-gather.38.cloned.1.call-start = ((), (), s32[]{:S(2)}) async-start(), calls=%async_computation.35 | async-start | bytes 5242880 | tf_op jit(solution)/shard_map/all_gather | solution.py:156
  438.2 365.7 %reduce-scatter.17.cloned.1.call-start = ((), (), s32[]{:S(2)}) async-start(), calls=%async_computation.24 | async-start | bytes 10485760 | tf_op jit(solution)/shard_map/reduce_scatter | solution.py:165
  708.1 12.0 copy-start.45
  720.1 4.7 copy-start.54
  720.2 4.7 copy-start.57
  720.2 4.7 copy-start.44
  732.0 113.6 %all-gather.36.cloned.1.call-start = ((), (), s32[]{:S(2)}) async-start(), calls=%async_computation.25 | async-start | bytes 5242880 | tf_op jit(solution)/shard_map/all_gather | solution.py:175
  803.9 3.5 copy-start.43
  803.9 4.1 copy-start.1
  803.9 4.1 copy-start.4
  803.9 4.1 copy-start.33
  811.0 184.4 %reduce-scatter.19.cloned.1.call-start = ((), (), s32[]{:S(2)}) async-start(), calls=%async_computation.26 | async-start | bytes 10485760 | tf_op jit(solution)/shard_map/reduce_scatter | solution.py:210
  858.0 2.2 copy-start.8
  858.0 2.5 copy-start.19
  858.0 3.0 copy-start.49
  858.0 3.0 copy-start.53
  861.1 4.1 copy-start.56
  865.2 3.3 copy-start.10
  865.2 3.3 copy-start.12
  868.5 1.9 copy-start.22
  868.5 1.9 copy-start.24
  876.6 7.4 copy-start.13
  876.6 7.4 copy-start.17
  884.0 6.9 copy-start.20
  884.0 6.9 copy-start.46
  890.9 5.7 copy-start.14
  908.8 146.4 %reduce-scatter.15.cloned.1.call-start = ((), (), s32[]{:S(2)}) async-start(), calls=%async_computation.23 | async-start | bytes 10485760 | tf_op jit(solution)/shard_map/reduce_scatter | solution.py:149
  920.9 267.0 %reduce-scatter.35.cloned.1.call-start = ((), (), s32[]{:S(2)}) async-start(), calls=%async_computation.34 | async-start | bytes 7962624 | tf_op jit(solution)/shard_map/reduce_scatter | solution.py:227
  931.6 389.4 %reduce-scatter.33.cloned.1.call-start = ((), (), s32[]{:S(2)}) async-start(), calls=%async_computation.33 | async-start | bytes 7962624 | tf_op jit(solution)/shard_map/reduce_scatter | solution.py:226
  941.8 511.9 %reduce-scatter.31.cloned.1.call-start = ((), (), s32[]{:S(2)}) async-start(), calls=%async_computation.32 | async-start | bytes 7962624 | tf_op jit(solution)/shard_map/reduce_scatter | solution.py:225
  951.4 595.0 %reduce-scatter.21.cloned.1.call-start = ((), (), s32[]{:S(2)}) async-start(), calls=%async_computation.27 | async-start | bytes 4718592 | tf_op jit(solution)/shard_map/reduce_scatter | solution.py:219
  958.6 679.6 %reduce-scatter.23.cloned.1.call-start = ((), (), s32[]{:S(2)}) async-start(), calls=%async_computation.28 | async-start | bytes 4718592 | tf_op jit(solution)/shard_map/reduce_scatter | solution.py:220
  965.6 805.5 %reduce-scatter.29.cloned.1.call-start = ((), (), s32[]{:S(2)}) async-start(), calls=%async_computation.31 | async-start | bytes 7962624 | tf_op jit(solution)/shard_map/reduce_scatter | solution.py:223
  975.0 928.9 %reduce-scatter.27.cloned.1.call-start = ((), (), s32[]{:S(2)}) async-start(), calls=%async_computation.30 | async-start | bytes 7962624 | tf_op jit(solution)/shard_map/reduce_scatter | solution.py:222
  983.0 1053.9 %reduce-scatter.25.cloned.1.call-start = ((), (), s32[]{:S(2)}) async-start(), calls=%async_computation.29 | async-start | bytes 7962624 | tf_op jit(solution)/shard_map/reduce_scatter | solution.py:221
  992.9 2.5 copy-start.3
  992.9 2.5 copy-start.28
  992.9 2.5 copy-start.37
  992.9 5.3 copy-start.31
  992.9 46.5 %copy-start.41 = (f32[256]{0:T(256)S(1)}, f32[256]{0:T(256)}, u32[]{:S(2)}) copy-start(f32[256]{0:T(256)} %copy-done.40) | copy-start | bytes 3076
  992.9 62.3 %copy-start.2 = (f32[256,2048]{1,0:T(8,128)S(1)}, f32[256,2048]{1,0:T(8,128)}, u32[]{:S(2)}) copy-start(f32[256,2048]{1,0:T(8,128)} %copy-done) | copy-start | bytes 6291460
  992.9 62.3 %copy-start.34 = (f32[256]{0:T(256)S(1)}, f32[256]{0:T(256)}, u32[]{:S(2)}) copy-start(f32[256]{0:T(256)} %copy-done.32) | copy-start | bytes 3076
  992.9 62.3 %copy-start.39 = (f32[256]{0:T(256)S(1)}, f32[256]{0:T(256)}, u32[]{:S(2)}) copy-start(f32[256]{0:T(256)} %copy-done.38) | copy-start | bytes 3076
  (18 other events, 17.1 us)
Sparse Core Ops, SparseCore 0:
  10.1 50.4 all-gather.21
  62.8 32.9 all-gather.15
  97.9 49.2 all-gather.19
  149.1 64.1 all-gather.17
  215.3 65.7 all-gather.23
  282.9 65.7 all-gather.25
  359.7 71.7 reduce-scatter.12
  433.7 65.7 all-gather.31
  501.7 34.4 all-gather.27
  538.3 65.7 all-gather.29
  606.3 65.7 all-gather.33
  673.6 34.4 all-gather.37
  732.1 71.6 reduce-scatter.16
  811.1 34.4 all-gather.35
  908.9 71.7 reduce-scatter.18
  983.3 71.8 reduce-scatter.14
  1059.4 128.4 reduce-scatter.34
  1192.5 128.4 reduce-scatter.32
  1325.2 128.4 reduce-scatter.30
  1458.2 88.1 reduce-scatter.20
  1550.6 87.6 reduce-scatter.22
  1643.0 128.0 reduce-scatter.28
  1775.4 128.4 reduce-scatter.26
  1908.5 128.4 reduce-scatter.24
where the time goes:
time: 2050 us; the launch traced here: 2040 us
  waiting for transfers between devices  1670 us (81%)
  matrix products  220 us (11%)
  blocking collectives  75.9 us (4%)
  other arithmetic  38.7 us (2%)
    reduce_scatter x1, waiting for transfers between devices, on_device(): lax.psum_scatter(value_weight_grad, 'dp', scatter_dimension=0, tiled=True)  133 us
    reduce_scatter x1, waiting for transfers between devices, on_device(): lax.psum_scatter(mlp_up_grad, 'dp', scatter_dimension=0, tiled=True)  133 us
    reduce_scatter x1, waiting for transfers between devices, on_device(): lax.psum_scatter(out_weight_grad, 'dp', scatter_dimension=1, tiled=True)  133 us
    reduce_scatter x1, waiting for transfers between devices, on_device(): lax.psum_scatter(gate_weight_grad, 'dp', scatter_dimension=0, tiled=True)  133 us
    reduce_scatter x1, waiting for transfers between devices, on_device(): lax.psum_scatter(mlp_gate_grad, 'dp', scatter_dimension=0, tiled=True)  133 us
    reduce_scatter x1, waiting for transfers between devices, on_device(): lax.psum_scatter(down_weight_grad, 'dp', scatter_dimension=1, tiled=True)  127 us
    reduce_scatter x1, waiting for transfers between devices, on_device(): lax.psum_scatter(query_weight_grad, 'dp', scatter_dimension=0, tiled=True)  92.6 us
    reduce_scatter x1, waiting for transfers between devices, on_device(): lax.psum_scatter(key_weight_grad, 'dp', scatter_dimension=0, tiled=True)  91.9 us
  transfers between devices with their start and end apart: 24, of which 23 were waited for; matrix products, arithmetic and copies ran while one was open for 8% of the time, Pallas kernels for 0%

commit v1 on v0

v1 whole, which is shorter than its diff:
```python
import jax
import jax.numpy as jnp
from jax import lax
from jax.sharding import PartitionSpec as P

KEY = 256
VAL = 432
LOW = jnp.bfloat16
WIDE = jnp.float32


def multiply(left, right):
    return jnp.dot(left, right, preferred_element_type=WIDE)


def multiply_left(left, right):
    return lax.dot_general(left, right, (((0,), (0,)), ((), ())), preferred_element_type=WIDE)


def multiply_right(left, right):
    return lax.dot_general(left, right, (((1,), (1,)), ((), ())), preferred_element_type=WIDE)


def rms_scale(values, gain):
    return values * lax.rsqrt(jnp.mean(values * values, axis=-1, keepdims=True) + 1e-06) * gain


def group_norm(values):
    centred = values - jnp.mean(values, axis=-1, keepdims=True)
    return centred * lax.rsqrt(jnp.mean(centred * centred, axis=-1, keepdims=True) + 1.0)


def rotary_tables(position, width):
    half = width // 2
    frequency = 10000.0 ** (-2.0 * jnp.arange(half, dtype=jnp.int32).astype(WIDE) / width)
    angle = position.astype(WIDE)[:, None] * frequency[None, :]
    return (jnp.cos(angle), jnp.sin(angle))


def rotate(values, cosine, sine):
    half = values.shape[-1] // 2
    first = values[..., :half]
    second = values[..., half:]
    return jnp.concatenate(
        [first * cosine - second * sine, second * cosine + first * sine], axis=-1
    )


def decay_mask(position, segments, first_head, count):
    distance = position[:, None] - position[None, :]
    same = (distance >= 0) & (segments[:, None] == segments[None, :])
    heads = (jnp.arange(count, dtype=jnp.int32) + first_head).astype(WIDE)
    rates = jnp.log1p(-jnp.exp2(-5.0 - heads))
    steps_back = jnp.maximum(distance, 0).astype(WIDE)
    decay = jnp.exp(rates[:, None, None] * steps_back[None, :, :])
    return jnp.where(same[None, :, :], decay, jnp.zeros((), WIDE))


def swap_side(value):
    count = lax.axis_size("dp")
    return lax.ppermute(value, "dp", [(i, i ^ 1) for i in range(count)])


def shift_line(value, step):
    count = lax.axis_size("dp")
    lines = count // 2
    pairs = [(i, 2 * ((i // 2 + step) % lines) + i % 2) for i in range(count)]
    return lax.ppermute(value, "dp", pairs)


def swap_tensor(value, bit):
    count = lax.axis_size("tensor")
    return lax.ppermute(value, "tensor", [(i, i ^ bit) for i in range(count)])


def gather_dp(shard, axis):
    lines = lax.axis_size("dp") // 2
    near = [shard] + [shift_line(shard, step) for step in range(1, lines)]
    far = [swap_side(block) for block in near]
    return jnp.concatenate(near + far, axis=axis)


def gather_tensor(block):
    beside = swap_tensor(block, 1)
    across = swap_tensor(block, 2)
    beyond = swap_tensor(across, 1)
    return jnp.concatenate([block, beside, across, beyond], axis=0)


def scatter_tensor(partial):
    rows = partial.shape[0] // 4
    one, two, three, four = [partial[k * rows : (k + 1) * rows] for k in range(4)]
    got = swap_tensor(jnp.concatenate([two, four], axis=0).astype(LOW), 1).astype(WIDE)
    across = swap_tensor((three + got[rows:]).astype(LOW), 2).astype(WIDE)
    return (one + got[:rows]) + across


def scatter_dp(near_product, far_product, axis):
    lines = lax.axis_size("dp") // 2
    got = swap_side(far_product().astype(LOW)).astype(WIDE)
    total = near_product() + got
    width = total.shape[axis] // lines
    parts = [lax.slice_in_dim(total, k * width, (k + 1) * width, axis=axis) for k in range(lines)]
    result = parts[0]
    for step in range(1, lines):
        result = result + shift_line(parts[step].astype(LOW), -step).astype(WIDE)
    return result


def on_device(
    hidden_in,
    out_grad,
    segment_ids,
    norm1_gain,
    w_query,
    w_key,
    w_value,
    w_gate,
    w_out,
    norm2_gain,
    w_mlp_gate,
    w_mlp_up,
    w_mlp_down,
):
    _, rows, width = hidden_in.shape
    parts = lax.axis_size("dp")
    lines = parts // 2
    slice_width = width // parts
    half = width // 2
    me = lax.axis_index("dp")
    line, side = me // 2, me % 2
    own = lax.axis_index("tensor")
    members = lax.axis_size("tensor")
    length = rows * members

    def to_own_order(value):
        owners = [
            2 * ((line + lines - step) % lines) + (side ^ flip)
            for flip in range(2)
            for step in range(lines)
        ]
        return jnp.concatenate(
            [
                lax.dynamic_slice_in_dim(value, owner * slice_width, slice_width, axis=1)
                for owner in owners
            ],
            axis=1,
        )

    def from_own_order(value):
        places = [
            (side ^ (k % 2)) * lines + (line + lines - k // 2) % lines for k in range(parts)
        ]
        return jnp.concatenate(
            [
                lax.dynamic_slice_in_dim(value, place * slice_width, slice_width, axis=1)
                for place in places
            ],
            axis=1,
        )

    gains = gather_dp(jnp.stack([norm1_gain, norm2_gain]), 1).astype(WIDE)
    gain_first, gain_second = gains[0], gains[1]
    heads_here = w_query.shape[1] // KEY
    first_head = own * heads_here
    key_columns = w_query.shape[1]
    value_columns = w_value.shape[1]
    feed_columns = w_mlp_gate.shape[1]

    qk_weight = gather_dp(jnp.concatenate([w_query, w_key], axis=1), 0)
    vg_weight = gather_dp(jnp.concatenate([w_value, w_gate], axis=1), 0)
    out_weight = gather_dp(w_out, 1)
    gu_weight = gather_dp(jnp.concatenate([w_mlp_gate, w_mlp_up], axis=1), 0)
    down_weight = gather_dp(w_mlp_down, 1)

    resid_in = to_own_order(hidden_in.reshape(rows, width)).astype(WIDE)
    grad_local = to_own_order(out_grad.reshape(rows, width))
    normed = gather_tensor(rms_scale(resid_in, gain_first).astype(LOW))
    grad_full = gather_tensor(grad_local)

    position = jnp.concatenate(
        [(own ^ k) * rows + jnp.arange(rows, dtype=jnp.int32) for k in range(members)]
    )
    segments = jnp.concatenate(
        [
            lax.dynamic_slice_in_dim(segment_ids.reshape(length), (own ^ k) * rows, rows)
            for k in range(members)
        ]
    )
    cosine, sine = rotary_tables(position, KEY)
    cosine = cosine[:, None, :]
    sine = sine[:, None, :]

    qk_pre = multiply(normed, qk_weight).reshape(length, 2 * heads_here, KEY)
    turned = rotate(qk_pre, cosine, sine)
    query = (turned[:, :heads_here] * KEY ** (-0.5)).astype(LOW)
    keys = turned[:, heads_here:].astype(LOW)
    vg_pre = multiply(normed, vg_weight)
    values = vg_pre[:, :value_columns].astype(LOW).reshape(length, heads_here, VAL)
    gate_pre = vg_pre[:, value_columns:]

    def retention_scores():
        mask = decay_mask(position, segments, first_head, heads_here)
        raw = jnp.einsum("nhk,mhk->hnm", query, keys, preferred_element_type=WIDE)
        return (raw * mask, mask)

    weighted, mask = retention_scores()
    scores_low = weighted.astype(LOW)
    retained = jnp.einsum(
        "hnm,mhv->nhv", scores_low, values, preferred_element_type=WIDE
    ).reshape(length, value_columns)

    def gate_mix(retained_in, gate_in):
        grouped = group_norm(retained_in.reshape(length, heads_here, VAL)).reshape(
            retained_in.shape
        )
        return grouped * jax.nn.silu(gate_in)

    mixed = gate_mix(retained, gate_pre).astype(LOW)
    resid_mid = resid_in + scatter_tensor(multiply(mixed, out_weight))
    normed_mid = gather_tensor(rms_scale(resid_mid, gain_second).astype(LOW))
    gu_hidden = multiply(normed_mid, gu_weight)
    gate_hidden = gu_hidden[:, :feed_columns]
    up_hidden = gu_hidden[:, feed_columns:]

    def gelu_mix(gate_in, up_in):
        return jax.nn.gelu(gate_in, approximate=True) * up_in

    hidden = gelu_mix(gate_hidden, up_hidden).astype(LOW)
    down_grad = scatter_dp(
        lambda: multiply_left(hidden, grad_full[:, :half]),
        lambda: multiply_left(hidden, grad_full[:, half:]),
        1,
    )
    resid_out = resid_mid + scatter_tensor(multiply(hidden, down_weight))
    hidden_out = from_own_order(resid_out.astype(LOW)).reshape(hidden_in.shape)

    hidden_grad = multiply_right(grad_full, down_weight)
    _, pull_mix = jax.vjp(gelu_mix, gate_hidden, up_hidden)
    gate_hidden_grad, up_hidden_grad = pull_mix(hidden_grad)
    gu_low = jnp.concatenate([gate_hidden_grad.astype(LOW), up_hidden_grad.astype(LOW)], axis=1)
    gu_grad = scatter_dp(
        lambda: multiply_left(normed_mid[:, :half], gu_low),
        lambda: multiply_left(normed_mid[:, half:], gu_low),
        0,
    )
    normed_mid_grad = scatter_tensor(multiply_right(gu_low, gu_weight))
    _, pull_second = jax.vjp(rms_scale, resid_mid, gain_second)
    mid_from_norm, gain_second_part = pull_second(normed_mid_grad)
    resid_mid_grad = grad_local.astype(WIDE) + mid_from_norm
    mid_full = gather_tensor(resid_mid_grad.astype(LOW))
    out_weight_grad = scatter_dp(
        lambda: multiply_left(mixed, mid_full[:, :half]),
        lambda: multiply_left(mixed, mid_full[:, half:]),
        1,
    )
    mixed_grad = multiply_right(mid_full, out_weight)
    _, pull_gate = jax.vjp(gate_mix, retained, gate_pre)
    retained_grad, gate_pre_grad = pull_gate(mixed_grad)
    retained_low = retained_grad.astype(LOW).reshape(length, heads_here, VAL)
    gate_pre_low = gate_pre_grad.astype(LOW)
    score_grad = jnp.einsum("nhv,mhv->hnm", retained_low, values, preferred_element_type=WIDE)
    raw_grad = (score_grad * mask).astype(LOW)
    query_grad = jnp.einsum("hnm,mhk->nhk", raw_grad, keys, preferred_element_type=WIDE)
    key_grad = jnp.einsum("hnm,nhk->mhk", raw_grad, query, preferred_element_type=WIDE)
    value_grad = (
        jnp.einsum("hnm,nhv->mhv", scores_low, retained_low, preferred_element_type=WIDE)
        .astype(LOW)
        .reshape(length, value_columns)
    )
    query_pre_grad = (
        (rotate(query_grad, cosine, -sine) * KEY ** (-0.5)).astype(LOW).reshape(length, key_columns)
    )
    key_pre_grad = rotate(key_grad, cosine, -sine).astype(LOW).reshape(length, key_columns)
    vg_low = jnp.concatenate([value_grad, gate_pre_low], axis=1)
    qk_low = jnp.concatenate([query_pre_grad, key_pre_grad], axis=1)
    vg_grad = scatter_dp(
        lambda: multiply_left(normed[:, :half], vg_low),
        lambda: multiply_left(normed[:, half:], vg_low),
        0,
    )
    qk_grad = scatter_dp(
        lambda: multiply_left(normed[:, :half], qk_low),
        lambda: multiply_left(normed[:, half:], qk_low),
        0,
    )
    normed_grad = scatter_tensor(
        multiply_right(vg_low, vg_weight) + multiply_right(qk_low, qk_weight)
    )
    _, pull_first = jax.vjp(rms_scale, resid_in, gain_first)
    in_from_norm, gain_first_part = pull_first(normed_grad)
    in_grad = from_own_order(resid_mid_grad + in_from_norm).reshape(hidden_in.shape)

    gain_part = jnp.stack([gain_first_part, gain_second_part])
    gain_part = gain_part + swap_tensor(gain_part, 1)
    gain_part = gain_part + swap_tensor(gain_part, 2)
    gain_part = gain_part[:, :half] + swap_side(gain_part[:, half:])
    gain_total = gain_part[:, :slice_width]
    for step in range(1, lines):
        gain_total = gain_total + shift_line(
            gain_part[:, step * slice_width : (step + 1) * slice_width], -step
        )
    return (
        hidden_out,
        in_grad,
        gain_total[0],
        qk_grad[:, :key_columns],
        qk_grad[:, key_columns:],
        vg_grad[:, :value_columns],
        vg_grad[:, value_columns:],
        out_weight_grad,
        gain_total[1],
        gu_grad[:, :feed_columns],
        gu_grad[:, feed_columns:],
        down_grad,
    )


def solution(mesh):
    return jax.shard_map(
        on_device,
        mesh=mesh,
        in_specs=(
            P("dp", "tensor", None),
            P("dp", "tensor", None),
            P("dp", None),
            P("dp"),
            P("dp", "tensor"),
            P("dp", "tensor"),
            P("dp", "tensor"),
            P("dp", "tensor"),
            P("tensor", "dp"),
            P("dp"),
            P("dp", "tensor"),
            P("dp", "tensor"),
            P("tensor", "dp"),
        ),
        out_specs=(
            P("dp", "tensor", None),
            P("dp", "tensor", None),
            P("dp"),
            P("dp", "tensor"),
            P("dp", "tensor"),
            P("dp", "tensor"),
            P("dp", "tensor"),
            P("tensor", "dp"),
            P("dp"),
            P("dp", "tensor"),
            P("dp", "tensor"),
            P("tensor", "dp"),
        ),
        check_vma=False,
    )
```

time: 2050 us -> 1060 us (0.52)
  waiting for transfers between devices: 1670 us -> 652 us
  starting transfers between devices: 1.64 us -> 84.5 us
  local copies, waits for them, and re-layouts: 18.4 us -> 94.6 us
  blocking collectives: 75.9 us -> 0 us
  matrix products: 220 us -> 173 us
    reduce_scatter x12 -> x0, waiting for transfers between devices: 1120 us -> none  [the longest x1 133 us: on_device(): lax.psum_scatter(value_weight_grad, 'dp', scatter_dimension=0, tiled=True)]
    ppermute x0 -> x88, waiting for transfers between devices: none -> 652 us  [the longest x36 321 us: shift_line(): return lax.ppermute(value, 'dp', pairs)]
    all_gather x12 -> x0, waiting for transfers between devices: 550 us -> none  [the longest x1 61.3 us: on_device(): lax.all_gather(w_mlp_up, 'dp', axis=0, tiled=True)]
    ppermute x0 -> x88, starting transfers between devices: none -> 84.5 us  [the longest x36 51.7 us: shift_line(): return lax.ppermute(value, 'dp', pairs)]
    unnamed x125 -> x264, local copies, waits for them, and re-layouts: 16.3 us -> 72.8 us
    all_gather x2 -> x0, blocking collectives: 34.8 us -> none  [the longest x1 18 us: on_device(): lax.all_gather(norm1_gain, 'dp', axis=0, tiled=True)]
    unnamed x1 -> x0, blocking collectives: 34.3 us -> none
    dot_general x14 -> x11, matrix products: 85.1 us -> 58 us  [the longest x5 43 us: multiply(): return jnp.dot(left, right, preferred_element_type=WIDE)]
  transfers between devices with their start and end apart: 24 -> 88, of which waited for: 23 -> 41; matrix products, arithmetic and copies ran while one was open for 8% -> 20% of each run, Pallas kernels for 0% -> 0%
where the time goes in v1:
time: 1060 us
  waiting for transfers between devices  652 us (62%)
  matrix products  173 us (16%)
  local copies, waits for them, and re-layouts  94.6 us (9%)
  starting transfers between devices  84.5 us (8%)
  other arithmetic  51.4 us (5%)
    ppermute x36, waiting for transfers between devices, shift_line(): return lax.ppermute(value, 'dp', pairs)  321 us
    ppermute x30, waiting for transfers between devices, swap_side(): return lax.ppermute(value, 'dp', [(i, i ^ 1) for i in range(count)])  317 us
    unnamed x264, local copies, waits for them, and re-layouts  72.8 us
    dot_general x5, matrix products, multiply_right(): lax.dot_general(left, right, (((1,), (1,)), ((), ())), preferred_element_...  59.2 us
    dot_general x10, matrix products, multiply_left(): lax.dot_general(left, right, (((0,), (0,)), ((), ())), preferred_element_...  55.9 us
    ppermute x36, starting transfers between devices, shift_line(): return lax.ppermute(value, 'dp', pairs)  51.7 us
    dot_general x5, matrix products, multiply(): return jnp.dot(left, right, preferred_element_type=WIDE)  43 us
    ppermute x30, starting transfers between devices, swap_side(): return lax.ppermute(value, 'dp', [(i, i ^ 1) for i in range(count)])  21.6 us
  transfers between devices with their start and end apart: 88, of which 41 were waited for; matrix products, arithmetic and copies ran while one was open for 20% of the time, Pallas kernels for 0%

profile of v1, /device:TPU:8, one launch (start us, length us, event | category | flops | bytes accessed | tf_op | source)
XLA Modules:
  0.0 1057.9 jit_solution(2133225965742061470)
XLA Ops:
  31.7 3.6 collective-permute-start.18
  50.0 44.4 %collective-permute-done.24 = bf16[864,256]{1,0:T(8,128)(2,1)S(1)} collective-permute-done((bf16[864,256]{1,0:T(8,128)(2,1)}, bf16[864,256]{1,0:T(8,128)(2,1)S(1)}, u32[]{:S(2)}, u32[]{:S(2)}) %collective-permute-start.24) | collective-permute-done | bytes 442400 | tf_op jit(solution)/shard_map/ppermute | solution.py:68
  94.5 9.4 collective-permute-done.25
  109.2 7.0 collective-permute-done.27
  116.7 3.3 collective-permute-start.11
  125.4 5.8 collective-permute-done.20
  133.6 33.5 %collective-permute-done.10 = bf16[256,1728]{0,1:T(8,128)(2,1)S(1)} collective-permute-done((bf16[256,1728]{0,1:T(8,128)(2,1)S(1)}, bf16[256,1728]{0,1:T(8,128)(2,1)S(1)}, u32[]{:S(2)}, u32[]{:S(2)}) %collective-permute-start.10) | collective-permute-done | bytes 884768 | tf_op jit(solution)/shard_map/ppermute | solution.py:68
  168.6 15.4 %collective-permute-done.11 = bf16[256,1728]{0,1:T(8,128)(2,1)S(1)} collective-permute-done((bf16[256,1728]{0,1:T(8,128)(2,1)S(1)}, bf16[256,1728]{0,1:T(8,128)(2,1)S(1)}, u32[]{:S(2)}, u32[]{:S(2)}) %collective-permute-start.11) | collective-permute-done | bytes 884768 | tf_op jit(solution)/shard_map/ppermute | solution.py:68
  190.6 6.6 collective-permute-done.29
  197.7 9.0 collective-permute-done.30
  208.2 9.7 collective-permute-done.21
  218.5 10.6 %collective-permute-done.22 = bf16[256,1024]{1,0:T(8,128)(2,1)S(1)} collective-permute-done((bf16[256,1024]{1,0:T(8,128)(2,1)S(1)}, bf16[256,1024]{1,0:T(8,128)(2,1)S(1)}, u32[]{:S(2)}, u32[]{:S(2)}) %collective-permute-start.22) | collective-permute-done | bytes 524320 | tf_op jit(solution)/shard_map/ppermute | solution.py:61
  229.7 10.7 %collective-permute-done.23 = bf16[256,1024]{1,0:T(8,128)(2,1)S(1)} collective-permute-done((bf16[256,1024]{1,0:T(8,128)(2,1)S(1)}, bf16[256,1024]{1,0:T(8,128)(2,1)S(1)}, u32[]{:S(2)}, u32[]{:S(2)}) %collective-permute-start.23) | collective-permute-done | bytes 524320 | tf_op jit(solution)/shard_map/ppermute | solution.py:61
  243.5 15.9 %collective-permute-done.14 = bf16[256,1728]{0,1:T(8,128)(2,1)S(1)} collective-permute-done((bf16[256,1728]{0,1:T(8,128)(2,1)S(1)}, bf16[256,1728]{0,1:T(8,128)(2,1)S(1)}, u32[]{:S(2)}, u32[]{:S(2)}) %collective-permute-start.14) | collective-permute-done | bytes 884768 | tf_op jit(solution)/shard_map/ppermute | solution.py:61
  260.4 17.9 %collective-permute-done.15 = bf16[256,1728]{0,1:T(8,128)(2,1)S(1)} collective-permute-done((bf16[256,1728]{0,1:T(8,128)(2,1)S(1)}, bf16[256,1728]{0,1:T(8,128)(2,1)S(1)}, u32[]{:S(2)}, u32[]{:S(2)}) %collective-permute-start.15) | collective-permute-done | bytes 884768 | tf_op jit(solution)/shard_map/ppermute | solution.py:61
  279.4 15.0 %collective-permute-done.16 = bf16[256,1728]{0,1:T(8,128)(2,1)S(1)} collective-permute-done((bf16[256,1728]{0,1:T(8,128)(2,1)S(1)}, bf16[256,1728]{0,1:T(8,128)(2,1)S(1)}, u32[]{:S(2)}, u32[]{:S(2)}) %collective-permute-start.16) | collective-permute-done | bytes 884768 | tf_op jit(solution)/shard_map/ppermute | solution.py:61
  295.4 7.7 fusion.95
  315.2 10.2 fusion.96
  336.2 4.6 fusion.115
  344.8 3.4 collective-permute-start.37
  348.7 3.8 collective-permute-start.44
  362.1 69.4 %collective-permute-done.43 = bf16[864,256]{1,0:T(8,128)(2,1)} collective-permute-done((bf16[864,256]{1,0:T(8,128)(2,1)}, bf16[864,256]{1,0:T(8,128)(2,1)}, u32[]{:S(2)}, u32[]{:S(2)}) %collective-permute-start.43) | collective-permute-done | bytes 442400 | tf_op jit(solution)/shard_map/ppermute | solution.py:68
  432.1 7.3 collective-permute-done.44
  456.1 9.7 collective-permute-done.32
  471.2 8.3 collective-permute-done.47
  480.0 9.0 collective-permute-done.48
  491.5 7.0 collective-permute-done.49
  499.8 17.6 %collective-permute-done.40 = bf16[256,1728]{0,1:T(8,128)(2,1)S(1)} collective-permute-done((bf16[256,1728]{0,1:T(8,128)(2,1)}, bf16[256,1728]{0,1:T(8,128)(2,1)S(1)}, u32[]{:S(2)}, u32[]{:S(2)}) %collective-permute-start.40) | collective-permute-done | bytes 884768 | tf_op jit(solution)/shard_map/ppermute | solution.py:61
  520.3 16.1 %collective-permute-done.41 = bf16[256,1728]{0,1:T(8,128)(2,1)S(1)} collective-permute-done((bf16[256,1728]{0,1:T(8,128)(2,1)}, bf16[256,1728]{0,1:T(8,128)(2,1)S(1)}, u32[]{:S(2)}, u32[]{:S(2)}) %collective-permute-start.41) | collective-permute-done | bytes 884768 | tf_op jit(solution)/shard_map/ppermute | solution.py:61
  537.9 14.6 %collective-permute-done.42 = bf16[256,1728]{0,1:T(8,128)(2,1)S(1)} collective-permute-done((bf16[256,1728]{0,1:T(8,128)(2,1)S(1)}, bf16[256,1728]{0,1:T(8,128)(2,1)S(1)}, u32[]{:S(2)}, u32[]{:S(2)}) %collective-permute-start.42) | collective-permute-done | bytes 884768 | tf_op jit(solution)/shard_map/ppermute | solution.py:61
  560.3 11.6 %fusion.94 = f32[1024,1728]{0,1:T(8,128)} fusion(bf16[2048,1728]{0,1:T(8,128)(2,1)} %constant_dynamic-update-slice_fusion.48, bf16[256,2048]{1,0:T(8,128)(2,1)S(1)} %collective-permute-done.35, bf16[256,2048]{1,0:T(8,128)(2,1)S(1)} %collective-permute-done.34, bf16[256,2048]{1,0:T(8,128)(2,1)S(1)} %collective-permute-done.33, ...), kind=kOutput, calls=%fused_computation.280 | convolution fusion | flops 7264534528 | bytes 18350080 | tf_op jit(solution)/shard_map/dot_general | solution.py:13
  571.9 12.9 %fusion.8 = (bf16[1024,864]{0,1:T(8,128)(2,1)S(1)}, bf16[1024,864]{0,1:T(8,128)(2,1)}, bf16[1024,864]{0,1:T(8,128)(2,1)}) fusion(f32[1024,1728]{0,1:T(8,128)} %fusion.94, bf16[864,2048]{1,0:T(8,128)(2,1)} %constant_dynamic-update-slice_fusion.57, bf16[256,2048]{1,0:T(8,128)(2,1)S(1)} %collective-permute-done.54, ...), kind=kOutput, calls=%fused_computation.34 | convolution fusion | flops 3663659008 | bytes 20119552 | tf_op jit(solution)/shard_map/dot_general | solution.py:21
  584.7 12.0 %fusion.116 = (bf16[1024,2048]{1,0:T(8,128)(2,1)S(1)}, f32[1024,2048]{1,0:T(8,128)S(1)}) fusion(bf16[2048,1728]{0,1:T(8,128)(2,1)} %constant_dynamic-update-slice_fusion.48, bf16[1024,864]{0,1:T(8,128)(2,1)} %get-tuple-element.25, bf16[1024,864]{0,1:T(8,128)(2,1)S(1)} %get-tuple-element.24), kind=kOutput, calls=%fused_computation.300 | convolution fusion | flops 7256932352 | bytes 23199744 | tf_op jit(solution)/shard_map/dot_general | solution.py:21
  602.2 8.9 fusion.118
  611.1 7.3 convolution_convert_fusion
  622.0 19.8 %collective-permute-done.84 = bf16[864,1024]{1,0:T(8,128)(2,1)S(1)} collective-permute-done((bf16[864,1024]{1,0:T(8,128)(2,1)S(1)}, bf16[864,1024]{1,0:T(8,128)(2,1)S(1)}, u32[]{:S(2)}, u32[]{:S(2)}) %collective-permute-start.84) | collective-permute-done | bytes 1769504 | tf_op jit(solution)/shard_map/ppermute | solution.py:61
  641.8 4.3 fusion.123
  651.7 3.9 collective-permute-start.85
  658.0 4.4 fusion.40
  662.4 21.5 %collective-permute-done.85 = bf16[864,256]{1,0:T(8,128)(2,1)S(1)} collective-permute-done((bf16[864,256]{1,0:T(8,128)(2,1)S(1)}, bf16[864,256]{1,0:T(8,128)(2,1)S(1)}, u32[]{:S(2)}, u32[]{:S(2)}) %collective-permute-start.85) | collective-permute-done | bytes 442400 | tf_op jit(solution)/shard_map/ppermute | solution.py:68
  683.9 6.2 collective-permute-done.87
  692.9 23.2 %collective-permute-done.80 = bf16[1024,1728]{0,1:T(8,128)(2,1)} collective-permute-done((bf16[1024,1728]{0,1:T(8,128)(2,1)}, bf16[1024,1728]{0,1:T(8,128)(2,1)}, u32[]{:S(2)}, u32[]{:S(2)}) %collective-permute-start.80) | collective-permute-done | bytes 3538976 | tf_op jit(solution)/shard_map/ppermute | solution.py:61
  716.1 9.4 fusion.122
  727.2 4.6 collective-permute-start.81
  733.5 12.9 %fusion.11 = (bf16[1024,864]{0,1:T(8,128)(2,1)}, f32[1024,864]{0,1:T(8,128)S(1)}) fusion(f32[1024,2,432]{0,2,1:T(8,128)S(1)} %copy-done.12, f32[1024,1728]{0,1:T(8,128)} %copy-done.27, bf16[864,2048]{1,0:T(8,128)(2,1)S(1)} %copy-done.76, bf16[256,2048]{1,0:T(8,128)(2,1)S(1)} %collective-permute-done.59, bf16[256,2048]{1,0:T(8,128)(2,1)S(1)} %collective-permute-done.58, ...), kind=kOutput, calls=%fused_computation.37 | convolution fusion | flops 3652157440 | bytes 20119552 | tf_op jit(solution)/shard_map/dot_general | solution.py:21
  750.5 3.3 convolution_convert_fusion.3
  753.8 3.7 multiply_convert_fusion
  762.1 3.2 fusion.60
  768.8 9.1 fusion.74
  777.9 5.4 convolution_convert_fusion.2
  784.8 12.4 %fusion.117 = (bf16[1024,2048]{1,0:T(8,128)(2,1)S(1)}, f32[1024,2048]{1,0:T(8,128)S(1)}) fusion(f32[1024,2048]{1,0:T(8,128)} %fusion.74, bf16[2048,1728]{0,1:T(8,128)(2,1)} %constant_dynamic-update-slice_fusion.18, bf16[1024,864]{0,1:T(8,128)(2,1)S(1)} %copy-done.35, bf16[1024,864]{0,1:T(8,128)(2,1)} %bitcast.112), kind=kOutput, calls=%fused_computation.301 | convolution fusion | flops 7259029504 | bytes 31588352 | tf_op jit(solution)/shard_map/dot_general | solution.py:21
  797.7 8.6 collective-permute-done.83
  810.9 5.4 fusion.121
  816.4 3.9 collective-permute-start.78
  820.4 28.4 %collective-permute-done.68 = bf16[1024,1024]{1,0:T(8,128)(2,1)} collective-permute-done((bf16[1024,1024]{1,0:T(8,128)(2,1)}, bf16[1024,1024]{1,0:T(8,128)(2,1)}, u32[]{:S(2)}, u32[]{:S(2)}) %collective-permute-start.68) | collective-permute-done | bytes 2097184 | tf_op jit(solution)/shard_map/ppermute | solution.py:61
  848.8 6.1 fusion.119
  860.9 6.8 convolution_convert_fusion.1
  871.5 20.8 %collective-permute-done.69 = bf16[256,1024]{1,0:T(8,128)(2,1)S(1)} collective-permute-done((bf16[256,1024]{1,0:T(8,128)(2,1)S(1)}, bf16[256,1024]{1,0:T(8,128)(2,1)S(1)}, u32[]{:S(2)}, u32[]{:S(2)}) %collective-permute-start.69) | collective-permute-done | bytes 524320 | tf_op jit(solution)/shard_map/ppermute | solution.py:68
  892.9 6.6 collective-permute-done.71
  905.6 3.3 fusion.20
  913.8 55.7 %collective-permute-done.64 = f32[2,1024]{1,0:T(2,128)S(1)} collective-permute-done((f32[2,1024]{1,0:T(2,128)S(1)}, f32[2,1024]{1,0:T(2,128)S(1)}, u32[]{:S(2)}, u32[]{:S(2)}) %collective-permute-start.64) | collective-permute-done | bytes 8224 | tf_op jit(solution)/shard_map/ppermute | solution.py:61
  969.5 6.0 fusion.120
  981.7 70.1 %collective-permute-done.65 = f32[2,256]{1,0:T(2,128)S(1)} collective-permute-done((f32[2,256]{1,0:T(2,128)S(1)}, f32[2,256]{1,0:T(2,128)S(1)}, u32[]{:S(2)}, u32[]{:S(2)}) %collective-permute-start.65) | collective-permute-done | bytes 2080 | tf_op jit(solution)/shard_map/ppermute | solution.py:68
  1051.8 3.5 collective-permute-done.67
  (502 shorter events, 223.7 us)
Async XLA Ops:
  2.0 29.7 %collective-permute-start = (bf16[2,256]{1,0:T(2,128)(2,1)S(1)}, bf16[2,256]{1,0:T(2,128)(2,1)S(1)}, u32[]{:S(2)}, u32[]{:S(2)}) collective-permute-start(bf16[2,256]{1,0:T(2,128)(2,1)S(1)} %get-tuple-element.21), channel_id=1, source_target_pairs={{0,8},{4,12},{8,16},{12,20},{16,24},{20,28},{24,0},{28,4},{1,9},{5... | collective-permute-start | bytes 3080 | tf_op jit(solution)/shard_map/ppermute | solution.py:68
  3.6 31.7 %collective-permute-start.1 = (bf16[2,256]{1,0:T(2,128)(2,1)S(1)}, bf16[2,256]{1,0:T(2,128)(2,1)S(1)}, u32[]{:S(2)}, u32[]{:S(2)}) collective-permute-start(bf16[2,256]{1,0:T(2,128)(2,1)S(1)} %get-tuple-element.21), channel_id=1, source_target_pairs={{0,16},{4,20},{8,24},{12,28},{16,0},{20,4},{24,8},{28,12},{1,17},{... | collective-permute-start | bytes 3080 | tf_op jit(solution)/shard_map/ppermute | solution.py:68
  4.7 30.6 %collective-permute-start.2 = (bf16[2,256]{1,0:T(2,128)(2,1)S(1)}, bf16[2,256]{1,0:T(2,128)(2,1)S(1)}, u32[]{:S(2)}, u32[]{:S(2)}) collective-permute-start(bf16[2,256]{1,0:T(2,128)(2,1)S(1)} %get-tuple-element.21), channel_id=1, source_target_pairs={{0,24},{4,28},{8,0},{12,4},{16,8},{20,12},{24,16},{28,20},{1,25},{... | collective-permute-start | bytes 3080 | tf_op jit(solution)/shard_map/ppermute | solution.py:68
  6.6 30.8 %collective-permute-start.3 = (bf16[2,256]{1,0:T(2,128)(2,1)S(1)}, bf16[2,256]{1,0:T(2,128)(2,1)S(1)}, u32[]{:S(2)}, u32[]{:S(2)}) collective-permute-start(bf16[2,256]{1,0:T(2,128)(2,1)S(1)} %get-tuple-element.21), channel_id=1, source_target_pairs={{0,4},{4,0},{8,12},{12,8},{16,20},{20,16},{24,28},{28,24},{1,5},{5... | collective-permute-start | bytes 3080 | tf_op jit(solution)/shard_map/ppermute | solution.py:61
  11.8 104.9 %collective-permute-start.17 = (bf16[256,1024]{1,0:T(8,128)(2,1)}, bf16[256,1024]{1,0:T(8,128)(2,1)}, u32[]{:S(2)}, u32[]{:S(2)}) collective-permute-start(bf16[256,1024]{1,0:T(8,128)(2,1)} %get-tuple-element.76), channel_id=1, source_target_pairs={{0,8},{4,12},{8,16},{12,20},{16,24},{20,28},{24,0},{28,4},{1,9},{5... | collective-permute-start | bytes 1572872 | tf_op jit(solution)/shard_map/ppermute | solution.py:68
  31.7 88.3 %collective-permute-start.18 = (bf16[256,1024]{1,0:T(8,128)(2,1)}, bf16[256,1024]{1,0:T(8,128)(2,1)S(1)}, u32[]{:S(2)}, u32[]{:S(2)}) collective-permute-start(bf16[256,1024]{1,0:T(8,128)(2,1)} %get-tuple-element.76), channel_id=1, source_target_pairs={{0,16},{4,20},{8,24},{12,28},{16,0},{20,4},{24,8},{28,12},{1,17},{... | collective-permute-start | bytes 1572872 | tf_op jit(solution)/shard_map/ppermute | solution.py:68
  35.3 84.9 %collective-permute-start.19 = (bf16[256,1024]{1,0:T(8,128)(2,1)}, bf16[256,1024]{1,0:T(8,128)(2,1)S(1)}, u32[]{:S(2)}, u32[]{:S(2)}) collective-permute-start(bf16[256,1024]{1,0:T(8,128)(2,1)} %get-tuple-element.76), channel_id=1, source_target_pairs={{0,24},{4,28},{8,0},{12,4},{16,8},{20,12},{24,16},{28,20},{1,25},{... | collective-permute-start | bytes 1572872 | tf_op jit(solution)/shard_map/ppermute | solution.py:68
  35.3 59.1 %collective-permute-start.24 = (bf16[864,256]{1,0:T(8,128)(2,1)}, bf16[864,256]{1,0:T(8,128)(2,1)S(1)}, u32[]{:S(2)}, u32[]{:S(2)}) collective-permute-start(bf16[864,256]{1,0:T(8,128)(2,1)} %param.21), channel_id=1, source_target_pairs={{0,8},{4,12},{8,16},{12,20},{16,24},{20,28},{24,0},{28,4},{1,9},{5... | collective-permute-start | bytes 1327112 | tf_op jit(solution)/shard_map/ppermute | solution.py:68
  48.2 55.7 %collective-permute-start.25 = (bf16[864,256]{1,0:T(8,128)(2,1)}, bf16[864,256]{1,0:T(8,128)(2,1)S(1)}, u32[]{:S(2)}, u32[]{:S(2)}) collective-permute-start(bf16[864,256]{1,0:T(8,128)(2,1)} %param.21), channel_id=1, source_target_pairs={{0,16},{4,20},{8,24},{12,28},{16,0},{20,4},{24,8},{28,12},{1,17},{... | collective-permute-start | bytes 1327112 | tf_op jit(solution)/shard_map/ppermute | solution.py:68
  107.3 59.8 %collective-permute-start.10 = (bf16[256,1728]{0,1:T(8,128)(2,1)S(1)}, bf16[256,1728]{0,1:T(8,128)(2,1)S(1)}, u32[]{:S(2)}, u32[]{:S(2)}) collective-permute-start(bf16[256,1728]{0,1:T(8,128)(2,1)S(1)} %get-tuple-element.72), channel_id=1, source_target_pairs={{0,8},{4,12},{8,16},{12,20},{16,24},{20,28},{24,0},{28,4},{1,9},{5... | collective-permute-start | bytes 2654216 | tf_op jit(solution)/shard_map/ppermute | solution.py:68
  116.7 67.4 %collective-permute-start.11 = (bf16[256,1728]{0,1:T(8,128)(2,1)S(1)}, bf16[256,1728]{0,1:T(8,128)(2,1)S(1)}, u32[]{:S(2)}, u32[]{:S(2)}) collective-permute-start(bf16[256,1728]{0,1:T(8,128)(2,1)S(1)} %get-tuple-element.72), channel_id=1, source_target_pairs={{0,16},{4,20},{8,24},{12,28},{16,0},{20,4},{24,8},{28,12},{1,17},{... | collective-permute-start | bytes 2654216 | tf_op jit(solution)/shard_map/ppermute | solution.py:68
  120.0 66.0 %collective-permute-start.12 = (bf16[256,1728]{0,1:T(8,128)(2,1)S(1)}, bf16[256,1728]{0,1:T(8,128)(2,1)S(1)}, u32[]{:S(2)}, u32[]{:S(2)}) collective-permute-start(bf16[256,1728]{0,1:T(8,128)(2,1)S(1)} %get-tuple-element.72), channel_id=1, source_target_pairs={{0,24},{4,28},{8,0},{12,4},{16,8},{20,12},{24,16},{28,20},{1,25},{... | collective-permute-start | bytes 2654216 | tf_op jit(solution)/shard_map/ppermute | solution.py:68
  120.1 66.3 %collective-permute-start.13 = (bf16[256,1728]{0,1:T(8,128)(2,1)S(1)}, bf16[256,1728]{0,1:T(8,128)(2,1)S(1)}, u32[]{:S(2)}, u32[]{:S(2)}) collective-permute-start(bf16[256,1728]{0,1:T(8,128)(2,1)S(1)} %get-tuple-element.72), channel_id=1, source_target_pairs={{0,4},{4,0},{8,12},{12,8},{16,20},{20,16},{24,28},{28,24},{1,5},{5... | collective-permute-start | bytes 2654216 | tf_op jit(solution)/shard_map/ppermute | solution.py:61
  131.2 109.1 %collective-permute-start.8 = (bf16[256,2048]{1,0:T(8,128)(2,1)S(1)}, bf16[256,2048]{1,0:T(8,128)(2,1)S(1)}, u32[]{:S(2)}, u32[]{:S(2)}) collective-permute-start(bf16[256,2048]{1,0:T(8,128)(2,1)S(1)} %fusion.17), channel_id=1, source_target_pairs={{0,2},{1,3},{2,0},{3,1},{4,6},{5,7},{6,4},{7,5},{8,10},{9,11},{10,... | collective-permute-start | bytes 3145736 | tf_op jit(solution)/shard_map/ppermute | solution.py:73
  186.5 31.4 %collective-permute-start.21 = (bf16[256,1024]{1,0:T(8,128)(2,1)}, bf16[256,1024]{1,0:T(8,128)(2,1)S(1)}, u32[]{:S(2)}, u32[]{:S(2)}) collective-permute-start(bf16[256,1024]{1,0:T(8,128)(2,1)} %collective-permute-done.17), channel_id=1, source_target_pairs={{0,4},{4,0},{8,12},{12,8},{16,20},{20,16},{24,28},{28,24},{1,5},{5... | collective-permute-start | bytes 1572872 | tf_op jit(solution)/shard_map/ppermute | solution.py:61
  189.0 40.1 %collective-permute-start.22 = (bf16[256,1024]{1,0:T(8,128)(2,1)S(1)}, bf16[256,1024]{1,0:T(8,128)(2,1)S(1)}, u32[]{:S(2)}, u32[]{:S(2)}) collective-permute-start(bf16[256,1024]{1,0:T(8,128)(2,1)S(1)} %collective-permute-done.18), channel_id=1, source_target_pairs={{0,4},{4,0},{8,12},{12,8},{16,20},{20,16},{24,28},{28,24},{1,5},{5... | collective-permute-start | bytes 1572872 | tf_op jit(solution)/shard_map/ppermute | solution.py:61
  197.2 43.2 %collective-permute-start.23 = (bf16[256,1024]{1,0:T(8,128)(2,1)S(1)}, bf16[256,1024]{1,0:T(8,128)(2,1)S(1)}, u32[]{:S(2)}, u32[]{:S(2)}) collective-permute-start(bf16[256,1024]{1,0:T(8,128)(2,1)S(1)} %collective-permute-done.19), channel_id=1, source_target_pairs={{0,4},{4,0},{8,12},{12,8},{16,20},{20,16},{24,28},{28,24},{1,5},{5... | collective-permute-start | bytes 1572872 | tf_op jit(solution)/shard_map/ppermute | solution.py:61
  206.7 52.7 %collective-permute-start.14 = (bf16[256,1728]{0,1:T(8,128)(2,1)S(1)}, bf16[256,1728]{0,1:T(8,128)(2,1)S(1)}, u32[]{:S(2)}, u32[]{:S(2)}) collective-permute-start(bf16[256,1728]{0,1:T(8,128)(2,1)S(1)} %collective-permute-done.10), channel_id=1, source_target_pairs={{0,4},{4,0},{8,12},{12,8},{16,20},{20,16},{24,28},{28,24},{1,5},{5... | collective-permute-start | bytes 2654216 | tf_op jit(solution)/shard_map/ppermute | solution.py:61
  217.9 60.4 %collective-permute-start.15 = (bf16[256,1728]{0,1:T(8,128)(2,1)S(1)}, bf16[256,1728]{0,1:T(8,128)(2,1)S(1)}, u32[]{:S(2)}, u32[]{:S(2)}) collective-permute-start(bf16[256,1728]{0,1:T(8,128)(2,1)S(1)} %collective-permute-done.11), channel_id=1, source_target_pairs={{0,4},{4,0},{8,12},{12,8},{16,20},{20,16},{24,28},{28,24},{1,5},{5... | collective-permute-start | bytes 2654216 | tf_op jit(solution)/shard_map/ppermute | solution.py:61
  229.1 65.2 %collective-permute-start.16 = (bf16[256,1728]{0,1:T(8,128)(2,1)S(1)}, bf16[256,1728]{0,1:T(8,128)(2,1)S(1)}, u32[]{:S(2)}, u32[]{:S(2)}) collective-permute-start(bf16[256,1728]{0,1:T(8,128)(2,1)S(1)} %collective-permute-done.12), channel_id=1, source_target_pairs={{0,4},{4,0},{8,12},{12,8},{16,20},{20,16},{24,28},{28,24},{1,5},{5... | collective-permute-start | bytes 2654216 | tf_op jit(solution)/shard_map/ppermute | solution.py:61
  240.4 55.0 %collective-permute-start.7 = (bf16[256,2048]{1,0:T(8,128)(2,1)S(1)}, bf16[256,2048]{1,0:T(8,128)(2,1)S(1)}, u32[]{:S(2)}, u32[]{:S(2)}) collective-permute-start(bf16[256,2048]{1,0:T(8,128)(2,1)S(1)} %fusion.17), channel_id=1, source_target_pairs={{0,1},{1,0},{2,3},{3,2},{4,5},{5,4},{6,7},{7,6},{8,9},{9,8},{10,11... | collective-permute-start | bytes 3145736 | tf_op jit(solution)/shard_map/ppermute | solution.py:73
  240.4 55.0 %collective-permute-start.9 = (bf16[256,2048]{1,0:T(8,128)(2,1)S(1)}, bf16[256,2048]{1,0:T(8,128)(2,1)S(1)}, u32[]{:S(2)}, u32[]{:S(2)}) collective-permute-start(bf16[256,2048]{1,0:T(8,128)(2,1)S(1)} %collective-permute-done.8), channel_id=1, source_target_pairs={{0,1},{1,0},{2,3},{3,2},{4,5},{5,4},{6,7},{7,6},{8,9},{9,8},{10,11... | collective-permute-start | bytes 3145736 | tf_op jit(solution)/shard_map/ppermute | solution.py:73
  344.8 104.8 %collective-permute-start.36 = (bf16[256,1728]{0,1:T(8,128)(2,1)}, bf16[256,1728]{0,1:T(8,128)(2,1)}, u32[]{:S(2)}, u32[]{:S(2)}) collective-permute-start(bf16[256,1728]{0,1:T(8,128)(2,1)} %get-tuple-element.68), channel_id=1, source_target_pairs={{0,8},{4,12},{8,16},{12,20},{16,24},{20,28},{24,0},{28,4},{1,9},{5... | collective-permute-start | bytes 2654216 | tf_op jit(solution)/shard_map/ppermute | solution.py:68
  344.8 107.6 %collective-permute-start.37 = (bf16[256,1728]{0,1:T(8,128)(2,1)}, bf16[256,1728]{0,1:T(8,128)(2,1)}, u32[]{:S(2)}, u32[]{:S(2)}) collective-permute-start(bf16[256,1728]{0,1:T(8,128)(2,1)} %get-tuple-element.68), channel_id=1, source_target_pairs={{0,16},{4,20},{8,24},{12,28},{16,0},{20,4},{24,8},{28,12},{1,17},{... | collective-permute-start | bytes 2654216 | tf_op jit(solution)/shard_map/ppermute | solution.py:68
  348.1 83.4 %collective-permute-start.43 = (bf16[864,256]{1,0:T(8,128)(2,1)}, bf16[864,256]{1,0:T(8,128)(2,1)}, u32[]{:S(2)}, u32[]{:S(2)}) collective-permute-start(bf16[864,256]{1,0:T(8,128)(2,1)} %param.25), channel_id=1, source_target_pairs={{0,8},{4,12},{8,16},{12,20},{16,24},{20,28},{24,0},{28,4},{1,9},{5... | collective-permute-start | bytes 1327112 | tf_op jit(solution)/shard_map/ppermute | solution.py:68
  348.7 90.7 %collective-permute-start.44 = (bf16[864,256]{1,0:T(8,128)(2,1)}, bf16[864,256]{1,0:T(8,128)(2,1)}, u32[]{:S(2)}, u32[]{:S(2)}) collective-permute-start(bf16[864,256]{1,0:T(8,128)(2,1)} %param.25), channel_id=1, source_target_pairs={{0,16},{4,20},{8,24},{12,28},{16,0},{20,4},{24,8},{28,12},{1,17},{... | collective-permute-start | bytes 1327112 | tf_op jit(solution)/shard_map/ppermute | solution.py:68
  358.4 87.0 %collective-permute-start.45 = (bf16[864,256]{1,0:T(8,128)(2,1)}, bf16[864,256]{1,0:T(8,128)(2,1)}, u32[]{:S(2)}, u32[]{:S(2)}) collective-permute-start(bf16[864,256]{1,0:T(8,128)(2,1)} %param.25), channel_id=1, source_target_pairs={{0,24},{4,28},{8,0},{12,4},{16,8},{20,12},{24,16},{28,20},{1,25},{... | collective-permute-start | bytes 1327112 | tf_op jit(solution)/shard_map/ppermute | solution.py:68
  449.6 50.2 %collective-permute-start.53 = (bf16[256,2048]{1,0:T(8,128)(2,1)}, bf16[256,2048]{1,0:T(8,128)(2,1)S(1)}, u32[]{:S(2)}, u32[]{:S(2)}) collective-permute-start(bf16[256,2048]{1,0:T(8,128)(2,1)} %constant_dynamic-update-slice_fusion.73), channel_id=1, source_target_pairs={{0,2},{1,3},{2,0},{3,1},{4,6},{5,7},{6,4},{7,5},{8,10},{9,11},{10,... | collective-permute-start | bytes 3145736 | tf_op jit(solution)/shard_map/ppermute | solution.py:73
  468.9 29.6 %collective-permute-start.49 = (bf16[864,256]{1,0:T(8,128)(2,1)}, bf16[864,256]{1,0:T(8,128)(2,1)S(1)}, u32[]{:S(2)}, u32[]{:S(2)}) collective-permute-start(bf16[864,256]{1,0:T(8,128)(2,1)} %collective-permute-done.45), channel_id=1, source_target_pairs={{0,4},{4,0},{8,12},{12,8},{16,20},{20,16},{24,28},{28,24},{1,5},{5... | collective-permute-start | bytes 1327112 | tf_op jit(solution)/shard_map/ppermute | solution.py:61
  470.4 47.0 %collective-permute-start.40 = (bf16[256,1728]{0,1:T(8,128)(2,1)}, bf16[256,1728]{0,1:T(8,128)(2,1)S(1)}, u32[]{:S(2)}, u32[]{:S(2)}) collective-permute-start(bf16[256,1728]{0,1:T(8,128)(2,1)} %collective-permute-done.36), channel_id=1, source_target_pairs={{0,4},{4,0},{8,12},{12,8},{16,20},{20,16},{24,28},{28,24},{1,5},{5... | collective-permute-start | bytes 2654216 | tf_op jit(solution)/shard_map/ppermute | solution.py:61
  479.5 56.9 %collective-permute-start.41 = (bf16[256,1728]{0,1:T(8,128)(2,1)}, bf16[256,1728]{0,1:T(8,128)(2,1)S(1)}, u32[]{:S(2)}, u32[]{:S(2)}) collective-permute-start(bf16[256,1728]{0,1:T(8,128)(2,1)} %collective-permute-done.37), channel_id=1, source_target_pairs={{0,4},{4,0},{8,12},{12,8},{16,20},{20,16},{24,28},{28,24},{1,5},{5... | collective-permute-start | bytes 2654216 | tf_op jit(solution)/shard_map/ppermute | solution.py:61
  489.0 47.4 %collective-permute-start.34 = (bf16[256,2048]{1,0:T(8,128)(2,1)S(1)}, bf16[256,2048]{1,0:T(8,128)(2,1)S(1)}, u32[]{:S(2)}, u32[]{:S(2)}) collective-permute-start(bf16[256,2048]{1,0:T(8,128)(2,1)S(1)} %multiply_convert_fusion.4), channel_id=1, source_target_pairs={{0,2},{1,3},{2,0},{3,1},{4,6},{5,7},{6,4},{7,5},{8,10},{9,11},{10,... | collective-permute-start | bytes 3145736 | tf_op jit(solution)/shard_map/ppermute | solution.py:73
  498.5 54.0 %collective-permute-start.42 = (bf16[256,1728]{0,1:T(8,128)(2,1)S(1)}, bf16[256,1728]{0,1:T(8,128)(2,1)S(1)}, u32[]{:S(2)}, u32[]{:S(2)}) collective-permute-start(bf16[256,1728]{0,1:T(8,128)(2,1)S(1)} %collective-permute-done.38), channel_id=1, source_target_pairs={{0,4},{4,0},{8,12},{12,8},{16,20},{20,16},{24,28},{28,24},{1,5},{5... | collective-permute-start | bytes 2654216 | tf_op jit(solution)/shard_map/ppermute | solution.py:61
  499.8 53.7 %collective-permute-start.52 = (bf16[256,2048]{1,0:T(8,128)(2,1)}, bf16[256,2048]{1,0:T(8,128)(2,1)S(1)}, u32[]{:S(2)}, u32[]{:S(2)}) collective-permute-start(bf16[256,2048]{1,0:T(8,128)(2,1)} %constant_dynamic-update-slice_fusion.73), channel_id=1, source_target_pairs={{0,1},{1,0},{2,3},{3,2},{4,5},{5,4},{6,7},{7,6},{8,9},{9,8},{10,11... | collective-permute-start | bytes 3145736 | tf_op jit(solution)/shard_map/ppermute | solution.py:73
  517.4 36.1 %collective-permute-start.54 = (bf16[256,2048]{1,0:T(8,128)(2,1)S(1)}, bf16[256,2048]{1,0:T(8,128)(2,1)S(1)}, u32[]{:S(2)}, u32[]{:S(2)}) collective-permute-start(bf16[256,2048]{1,0:T(8,128)(2,1)S(1)} %collective-permute-done.53), channel_id=1, source_target_pairs={{0,1},{1,0},{2,3},{3,2},{4,5},{5,4},{6,7},{7,6},{8,9},{9,8},{10,11... | collective-permute-start | bytes 3145736 | tf_op jit(solution)/shard_map/ppermute | solution.py:73
  600.2 41.6 %collective-permute-start.84 = (bf16[864,1024]{1,0:T(8,128)(2,1)S(1)}, bf16[864,1024]{1,0:T(8,128)(2,1)S(1)}, u32[]{:S(2)}, u32[]{:S(2)}) collective-permute-start(bf16[864,1024]{1,0:T(8,128)(2,1)S(1)} %fusion.63), channel_id=1, source_target_pairs={{0,4},{4,0},{8,12},{12,8},{16,20},{20,16},{24,28},{28,24},{1,5},{5... | collective-permute-start | bytes 5308424 | tf_op jit(solution)/shard_map/ppermute | solution.py:61
  618.4 97.7 %collective-permute-start.80 = (bf16[1024,1728]{0,1:T(8,128)(2,1)}, bf16[1024,1728]{0,1:T(8,128)(2,1)}, u32[]{:S(2)}, u32[]{:S(2)}) collective-permute-start(bf16[1024,1728]{0,1:T(8,128)(2,1)} %convolution_convert_fusion), channel_id=1, source_target_pairs={{0,4},{4,0},{8,12},{12,8},{16,20},{20,16},{24,28},{28,24},{1,5},{5... | collective-permute-start | bytes 10616840 | tf_op jit(solution)/shard_map/ppermute | solution.py:61
  622.0 33.7 %collective-permute-start.50 = (bf16[512,2048]{1,0:T(8,128)(2,1)S(1)}, bf16[512,2048]{1,0:T(8,128)(2,1)S(1)}, u32[]{:S(2)}, u32[]{:S(2)}) collective-permute-start(bf16[512,2048]{1,0:T(8,128)(2,1)S(1)} %pad_maximum_fusion.8), channel_id=1, source_target_pairs={{0,1},{1,0},{2,3},{3,2},{4,5},{5,4},{6,7},{7,6},{8,9},{9,8},{10,11... | collective-permute-start | bytes 6291464 | tf_op jit(solution)/shard_map/ppermute | solution.py:73
  650.4 42.0 %collective-permute-start.58 = (bf16[256,2048]{1,0:T(8,128)(2,1)S(1)}, bf16[256,2048]{1,0:T(8,128)(2,1)S(1)}, u32[]{:S(2)}, u32[]{:S(2)}) collective-permute-start(bf16[256,2048]{1,0:T(8,128)(2,1)S(1)} %fusion.93), channel_id=1, source_target_pairs={{0,2},{1,3},{2,0},{3,1},{4,6},{5,7},{6,4},{7,5},{8,10},{9,11},{10,... | collective-permute-start | bytes 3145736 | tf_op jit(solution)/shard_map/ppermute | solution.py:73
  651.7 32.1 %collective-permute-start.85 = (bf16[864,256]{1,0:T(8,128)(2,1)S(1)}, bf16[864,256]{1,0:T(8,128)(2,1)S(1)}, u32[]{:S(2)}, u32[]{:S(2)}) collective-permute-start(bf16[864,256]{1,0:T(8,128)(2,1)S(1)} %get-tuple-element.54), channel_id=1, source_target_pairs={{0,24},{4,28},{8,0},{12,4},{16,8},{20,12},{24,16},{28,20},{1,25},{... | collective-permute-start | bytes 1327112 | tf_op jit(solution)/shard_map/ppermute | solution.py:68
  655.7 34.4 %collective-permute-start.87 = (bf16[864,256]{1,0:T(8,128)(2,1)S(1)}, bf16[864,256]{1,0:T(8,128)(2,1)S(1)}, u32[]{:S(2)}, u32[]{:S(2)}) collective-permute-start(bf16[864,256]{1,0:T(8,128)(2,1)S(1)} %get-tuple-element.55), channel_id=1, source_target_pairs={{0,8},{4,12},{8,16},{12,20},{16,24},{20,28},{24,0},{28,4},{1,9},{5... | collective-permute-start | bytes 1327112 | tf_op jit(solution)/shard_map/ppermute | solution.py:68
  692.4 41.1 %collective-permute-start.57 = (bf16[256,2048]{1,0:T(8,128)(2,1)S(1)}, bf16[256,2048]{1,0:T(8,128)(2,1)S(1)}, u32[]{:S(2)}, u32[]{:S(2)}) collective-permute-start(bf16[256,2048]{1,0:T(8,128)(2,1)S(1)} %fusion.93), channel_id=1, source_target_pairs={{0,1},{1,0},{2,3},{3,2},{4,5},{5,4},{6,7},{7,6},{8,9},{9,8},{10,11... | collective-permute-start | bytes 3145736 | tf_op jit(solution)/shard_map/ppermute | solution.py:73
  692.4 41.1 %collective-permute-start.59 = (bf16[256,2048]{1,0:T(8,128)(2,1)S(1)}, bf16[256,2048]{1,0:T(8,128)(2,1)S(1)}, u32[]{:S(2)}, u32[]{:S(2)}) collective-permute-start(bf16[256,2048]{1,0:T(8,128)(2,1)S(1)} %collective-permute-done.58), channel_id=1, source_target_pairs={{0,1},{1,0},{2,3},{3,2},{4,5},{5,4},{6,7},{7,6},{8,9},{9,8},{10,11... | collective-permute-start | bytes 3145736 | tf_op jit(solution)/shard_map/ppermute | solution.py:73
  727.2 70.4 %collective-permute-start.81 = (bf16[256,1728]{0,1:T(8,128)(2,1)}, bf16[256,1728]{0,1:T(8,128)(2,1)}, u32[]{:S(2)}, u32[]{:S(2)}) collective-permute-start(bf16[256,1728]{0,1:T(8,128)(2,1)} %get-tuple-element.39), channel_id=1, source_target_pairs={{0,24},{4,28},{8,0},{12,4},{16,8},{20,12},{24,16},{28,20},{1,25},{... | collective-permute-start | bytes 2654216 | tf_op jit(solution)/shard_map/ppermute | solution.py:68
  731.7 65.9 %collective-permute-start.82 = (bf16[256,1728]{0,1:T(8,128)(2,1)}, bf16[256,1728]{0,1:T(8,128)(2,1)}, u32[]{:S(2)}, u32[]{:S(2)}) collective-permute-start(bf16[256,1728]{0,1:T(8,128)(2,1)} %get-tuple-element.41), channel_id=1, source_target_pairs={{0,16},{4,20},{8,24},{12,28},{16,0},{20,4},{24,8},{28,12},{1,17},{... | collective-permute-start | bytes 2654216 | tf_op jit(solution)/shard_map/ppermute | solution.py:68
  731.7 74.5 %collective-permute-start.83 = (bf16[256,1728]{0,1:T(8,128)(2,1)}, bf16[256,1728]{0,1:T(8,128)(2,1)}, u32[]{:S(2)}, u32[]{:S(2)}) collective-permute-start(bf16[256,1728]{0,1:T(8,128)(2,1)} %get-tuple-element.40), channel_id=1, source_target_pairs={{0,8},{4,12},{8,16},{12,20},{16,24},{20,28},{24,0},{28,4},{1,9},{5... | collective-permute-start | bytes 2654216 | tf_op jit(solution)/shard_map/ppermute | solution.py:68
  765.3 45.0 %collective-permute-start.76 = (bf16[864,1024]{1,0:T(8,128)(2,1)}, bf16[864,1024]{1,0:T(8,128)(2,1)}, u32[]{:S(2)}, u32[]{:S(2)}) collective-permute-start(bf16[864,1024]{1,0:T(8,128)(2,1)} %fusion.60), channel_id=1, source_target_pairs={{0,4},{4,0},{8,12},{12,8},{16,20},{20,16},{24,28},{28,24},{1,5},{5... | collective-permute-start | bytes 5308424 | tf_op jit(solution)/shard_map/ppermute | solution.py:61
  783.3 65.4 %collective-permute-start.68 = (bf16[1024,1024]{1,0:T(8,128)(2,1)}, bf16[1024,1024]{1,0:T(8,128)(2,1)}, u32[]{:S(2)}, u32[]{:S(2)}) collective-permute-start(bf16[1024,1024]{1,0:T(8,128)(2,1)} %convolution_convert_fusion.2), channel_id=1, source_target_pairs={{0,4},{4,0},{8,12},{12,8},{16,20},{20,16},{24,28},{28,24},{1,5},{5... | collective-permute-start | bytes 6291464 | tf_op jit(solution)/shard_map/ppermute | solution.py:61
  797.6 58.0 %collective-permute-start.60 = (bf16[512,2048]{1,0:T(8,128)(2,1)S(1)}, bf16[512,2048]{1,0:T(8,128)(2,1)S(1)}, u32[]{:S(2)}, u32[]{:S(2)}) collective-permute-start(bf16[512,2048]{1,0:T(8,128)(2,1)S(1)} %pad_maximum_fusion.11), channel_id=1, source_target_pairs={{0,1},{1,0},{2,3},{3,2},{4,5},{5,4},{6,7},{7,6},{8,9},{9,8},{10,11... | collective-permute-start | bytes 6291464 | tf_op jit(solution)/shard_map/ppermute | solution.py:73
  816.4 42.8 %collective-permute-start.77 = (bf16[864,256]{1,0:T(8,128)(2,1)S(1)}, bf16[864,256]{1,0:T(8,128)(2,1)S(1)}, u32[]{:S(2)}, u32[]{:S(2)}) collective-permute-start(bf16[864,256]{1,0:T(8,128)(2,1)S(1)} %get-tuple-element.59), channel_id=1, source_target_pairs={{0,24},{4,28},{8,0},{12,4},{16,8},{20,12},{24,16},{28,20},{1,25},{... | collective-permute-start | bytes 1327112 | tf_op jit(solution)/shard_map/ppermute | solution.py:68
  816.4 43.9 %collective-permute-start.78 = (bf16[864,256]{1,0:T(8,128)(2,1)S(1)}, bf16[864,256]{1,0:T(8,128)(2,1)S(1)}, u32[]{:S(2)}, u32[]{:S(2)}) collective-permute-start(bf16[864,256]{1,0:T(8,128)(2,1)S(1)} %get-tuple-element.61), channel_id=1, source_target_pairs={{0,16},{4,20},{8,24},{12,28},{16,0},{20,4},{24,8},{28,12},{1,17},{... | collective-permute-start | bytes 1327112 | tf_op jit(solution)/shard_map/ppermute | solution.py:68
  820.4 47.3 %collective-permute-start.79 = (bf16[864,256]{1,0:T(8,128)(2,1)S(1)}, bf16[864,256]{1,0:T(8,128)(2,1)S(1)}, u32[]{:S(2)}, u32[]{:S(2)}) collective-permute-start(bf16[864,256]{1,0:T(8,128)(2,1)S(1)} %get-tuple-element.60), channel_id=1, source_target_pairs={{0,8},{4,12},{8,16},{12,20},{16,24},{20,28},{24,0},{28,4},{1,9},{5... | collective-permute-start | bytes 1327112 | tf_op jit(solution)/shard_map/ppermute | solution.py:68
  855.0 37.4 %collective-permute-start.69 = (bf16[256,1024]{1,0:T(8,128)(2,1)S(1)}, bf16[256,1024]{1,0:T(8,128)(2,1)S(1)}, u32[]{:S(2)}, u32[]{:S(2)}) collective-permute-start(bf16[256,1024]{1,0:T(8,128)(2,1)S(1)} %get-tuple-element.49), channel_id=1, source_target_pairs={{0,24},{4,28},{8,0},{12,4},{16,8},{20,12},{24,16},{28,20},{1,25},{... | collective-permute-start | bytes 1572872 | tf_op jit(solution)/shard_map/ppermute | solution.py:68
  855.6 37.3 %collective-permute-start.70 = (bf16[256,1024]{1,0:T(8,128)(2,1)S(1)}, bf16[256,1024]{1,0:T(8,128)(2,1)S(1)}, u32[]{:S(2)}, u32[]{:S(2)}) collective-permute-start(bf16[256,1024]{1,0:T(8,128)(2,1)S(1)} %get-tuple-element.51), channel_id=1, source_target_pairs={{0,16},{4,20},{8,24},{12,28},{16,0},{20,4},{24,8},{28,12},{1,17},{... | collective-permute-start | bytes 1572872 | tf_op jit(solution)/shard_map/ppermute | solution.py:68
  859.1 40.4 %collective-permute-start.71 = (bf16[256,1024]{1,0:T(8,128)(2,1)S(1)}, bf16[256,1024]{1,0:T(8,128)(2,1)S(1)}, u32[]{:S(2)}, u32[]{:S(2)}) collective-permute-start(bf16[256,1024]{1,0:T(8,128)(2,1)S(1)} %get-tuple-element.50), channel_id=1, source_target_pairs={{0,8},{4,12},{8,16},{12,20},{16,24},{20,28},{24,0},{28,4},{1,9},{5... | collective-permute-start | bytes 1572872 | tf_op jit(solution)/shard_map/ppermute | solution.py:68
  860.4 41.8 %collective-permute-start.61 = (bf16[256,2048]{1,0:T(8,128)(2,1)S(1)}, bf16[256,2048]{1,0:T(8,128)(2,1)S(1)}, u32[]{:S(2)}, u32[]{:S(2)}) collective-permute-start(bf16[256,2048]{1,0:T(8,128)(2,1)S(1)} %fusion.36), channel_id=1, source_target_pairs={{0,2},{1,3},{2,0},{3,1},{4,6},{5,7},{6,4},{7,5},{8,10},{9,11},{10,... | collective-permute-start | bytes 3145736 | tf_op jit(solution)/shard_map/ppermute | solution.py:73
  867.7 36.4 %collective-permute-start.51 = (bf16[256,2048]{1,0:T(8,128)(2,1)S(1)}, bf16[256,2048]{1,0:T(8,128)(2,1)S(1)}, u32[]{:S(2)}, u32[]{:S(2)}) collective-permute-start(bf16[256,2048]{1,0:T(8,128)(2,1)S(1)} %copy-done.37), channel_id=1, source_target_pairs={{0,2},{1,3},{2,0},{3,1},{4,6},{5,7},{6,4},{7,5},{8,10},{9,11},{10,... | collective-permute-start | bytes 3145736 | tf_op jit(solution)/shard_map/ppermute | solution.py:73
  892.4 77.1 %collective-permute-start.72 = (bf16[1024,1728]{0,1:T(8,128)(2,1)}, bf16[1024,1728]{0,1:T(8,128)(2,1)}, u32[]{:S(2)}, u32[]{:S(2)}) collective-permute-start(bf16[1024,1728]{0,1:T(8,128)(2,1)} %convolution_convert_fusion.1), channel_id=1, source_target_pairs={{0,4},{4,0},{8,12},{12,8},{16,20},{20,16},{24,28},{28,24},{1,5},{5... | collective-permute-start | bytes 10616840 | tf_op jit(solution)/shard_map/ppermute | solution.py:61
  913.2 56.3 %collective-permute-start.64 = (f32[2,1024]{1,0:T(2,128)S(1)}, f32[2,1024]{1,0:T(2,128)S(1)}, u32[]{:S(2)}, u32[]{:S(2)}) collective-permute-start(f32[2,1024]{1,0:T(2,128)S(1)} %slice.386), channel_id=1, source_target_pairs={{0,4},{4,0},{8,12},{12,8},{16,20},{20,16},{24,28},{28,24},{1,5},{5... | collective-permute-start | bytes 24584 | tf_op jit(solution)/shard_map/ppermute | solution.py:61
  975.7 80.3 %collective-permute-start.73 = (bf16[256,1728]{0,1:T(8,128)(2,1)S(1)}, bf16[256,1728]{0,1:T(8,128)(2,1)S(1)}, u32[]{:S(2)}, u32[]{:S(2)}) collective-permute-start(bf16[256,1728]{0,1:T(8,128)(2,1)S(1)} %get-tuple-element.42), channel_id=1, source_target_pairs={{0,24},{4,28},{8,0},{12,4},{16,8},{20,12},{24,16},{28,20},{1,25},{... | collective-permute-start | bytes 2654216 | tf_op jit(solution)/shard_map/ppermute | solution.py:68
  975.8 80.2 %collective-permute-start.74 = (bf16[256,1728]{0,1:T(8,128)(2,1)S(1)}, bf16[256,1728]{0,1:T(8,128)(2,1)S(1)}, u32[]{:S(2)}, u32[]{:S(2)}) collective-permute-start(bf16[256,1728]{0,1:T(8,128)(2,1)S(1)} %get-tuple-element.44), channel_id=1, source_target_pairs={{0,16},{4,20},{8,24},{12,28},{16,0},{20,4},{24,8},{28,12},{1,17},{... | collective-permute-start | bytes 2654216 | tf_op jit(solution)/shard_map/ppermute | solution.py:68
  976.7 79.2 %collective-permute-start.75 = (bf16[256,1728]{0,1:T(8,128)(2,1)S(1)}, bf16[256,1728]{0,1:T(8,128)(2,1)S(1)}, u32[]{:S(2)}, u32[]{:S(2)}) collective-permute-start(bf16[256,1728]{0,1:T(8,128)(2,1)S(1)} %get-tuple-element.43), channel_id=1, source_target_pairs={{0,8},{4,12},{8,16},{12,20},{16,24},{20,28},{24,0},{28,4},{1,9},{5... | collective-permute-start | bytes 2654216 | tf_op jit(solution)/shard_map/ppermute | solution.py:68
  977.8 74.0 %collective-permute-start.65 = (f32[2,256]{1,0:T(2,128)S(1)}, f32[2,256]{1,0:T(2,128)S(1)}, u32[]{:S(2)}, u32[]{:S(2)}) collective-permute-start(f32[2,256]{1,0:T(2,128)S(1)} %get-tuple-element.80), channel_id=1, source_target_pairs={{0,24},{4,28},{8,0},{12,4},{16,8},{20,12},{24,16},{28,20},{1,25},{... | collective-permute-start | bytes 6152 | tf_op jit(solution)/shard_map/ppermute | solution.py:68
  979.3 72.6 %collective-permute-start.66 = (f32[2,256]{1,0:T(2,128)S(1)}, f32[2,256]{1,0:T(2,128)S(1)}, u32[]{:S(2)}, u32[]{:S(2)}) collective-permute-start(f32[2,256]{1,0:T(2,128)S(1)} %get-tuple-element.82), channel_id=1, source_target_pairs={{0,16},{4,20},{8,24},{12,28},{16,0},{20,4},{24,8},{28,12},{1,17},{... | collective-permute-start | bytes 6152 | tf_op jit(solution)/shard_map/ppermute | solution.py:68
  (121 other events, 2673.4 us)

commit v2 on v1

v2 whole, which is shorter than its diff:
```python
import functools

import jax
import jax.numpy as jnp
from jax import lax
from jax.experimental import pallas as pl
from jax.experimental.pallas import tpu as pltpu
from jax.sharding import PartitionSpec as P

KEY = 256
VAL = 432
LOW = jnp.bfloat16
WIDE = jnp.float32


def multiply(left, right):
    return jnp.dot(left, right, preferred_element_type=WIDE)


def multiply_left(left, right):
    return lax.dot_general(left, right, (((0,), (0,)), ((), ())), preferred_element_type=WIDE)


def multiply_right(left, right):
    return lax.dot_general(left, right, (((1,), (1,)), ((), ())), preferred_element_type=WIDE)


def rms_scale(values, gain):
    return values * lax.rsqrt(jnp.mean(values * values, axis=-1, keepdims=True) + 1e-06) * gain


def group_norm(values):
    centred = values - jnp.mean(values, axis=-1, keepdims=True)
    return centred * lax.rsqrt(jnp.mean(centred * centred, axis=-1, keepdims=True) + 1.0)


def rotary_tables(position, width):
    half = width // 2
    frequency = 10000.0 ** (-2.0 * jnp.arange(half, dtype=jnp.int32).astype(WIDE) / width)
    angle = position.astype(WIDE)[:, None] * frequency[None, :]
    return (jnp.cos(angle), jnp.sin(angle))


def rotate(values, cosine, sine):
    half = values.shape[-1] // 2
    first = values[..., :half]
    second = values[..., half:]
    return jnp.concatenate(
        [first * cosine - second * sine, second * cosine + first * sine], axis=-1
    )


def decay_mask(position, segments, first_head, count):
    distance = position[:, None] - position[None, :]
    same = (distance >= 0) & (segments[:, None] == segments[None, :])
    heads = (jnp.arange(count, dtype=jnp.int32) + first_head).astype(WIDE)
    rates = jnp.log1p(-jnp.exp2(-5.0 - heads))
    steps_back = jnp.maximum(distance, 0).astype(WIDE)
    decay = jnp.exp(rates[:, None, None] * steps_back[None, :, :])
    return jnp.where(same[None, :, :], decay, jnp.zeros((), WIDE))


def by_place():
    count = lax.axis_size("dp")
    return [list(range(0, count, 2)) + list(range(1, count, 2))]


def gather_dp(shard, axis):
    return lax.all_gather(shard, "dp", axis=axis, tiled=True, axis_index_groups=by_place())


def scatter_dp(value, axis):
    return lax.psum_scatter(
        value, "dp", scatter_dimension=axis, tiled=True, axis_index_groups=by_place()
    )


def swap_tensor(value, bit):
    count = lax.axis_size("tensor")
    return lax.ppermute(value, "tensor", [(i, i ^ bit) for i in range(count)])


def after(value, earlier):
    return value if earlier is None else lax.optimization_barrier((value, earlier))[0]


def gather_tensor(block):
    beside = swap_tensor(block, 1)
    across = swap_tensor(block, 2)
    beyond = swap_tensor(across, 1)
    return jnp.concatenate([block, beside, across, beyond], axis=0)


def scatter_tensor(partial):
    rows = partial.shape[0] // 4
    one, two, three, four = [partial[k * rows : (k + 1) * rows] for k in range(4)]
    got = swap_tensor(jnp.concatenate([two, four], axis=0).astype(LOW), 1).astype(WIDE)
    across = swap_tensor((three + got[rows:]).astype(LOW), 2).astype(WIDE)
    return (one + got[:rows]) + across


MESH = pl.DeviceIdType.MESH
ANY = pl.BlockSpec(memory_space=pl.ANY)
INSIDE = pl.BlockSpec(memory_space=pltpu.VMEM)
ROOM = 60 * 1024 * 1024


def greet(peers):
    barrier = pltpu.get_barrier_semaphore()
    for peer in peers:
        pl.semaphore_signal(barrier, inc=1, device_id=peer, device_id_type=MESH)
    pl.semaphore_wait(barrier, len(peers))


def gather_kernel(lines, members, count, *refs):
    hidden_ref, grad_ref, gain_ref = refs[:3]
    shards = refs[3 : 3 + count]
    normed_all, grad_all, gain_all = refs[3 + count : 6 + count]
    wholes = refs[6 + count : 6 + 2 * count]
    normed_own, line_send, line_recv, side_send, side_recv = refs[6 + 2 * count : 11 + 2 * count]
    near_send, near_recv, gain_send, gain_recv, home = refs[11 + 2 * count :]
    parts = 2 * lines
    me = lax.axis_index("dp")
    line, side = me // 2, lax.rem(me, 2)
    own = lax.axis_index("tensor")
    rest = lax.rem(own, 2)
    half = own // 2
    partners = [
        {"tensor": 2 * lax.rem(half + k // 2, 2) + lax.rem(rest + k % 2, 2)}
        for k in range(1, members)
    ]
    others = [{"dp": lax.rem(me + k, parts)} for k in range(1, parts)]
    greet(others + partners)
    opposite = {"dp": 2 * line + (1 - side)}
    here = side * lines + line

    def remote(source, target, send, recv, device):
        return pltpu.make_async_remote_copy(
            src_ref=source,
            dst_ref=target,
            send_sem=send,
            recv_sem=recv,
            device_id=device,
            device_id_type=MESH,
        )

    gains = []
    for k in range(1, parts):
        gains.append(
            remote(
                gain_ref,
                gain_all.at[here],
                gain_send.at[k],
                gain_recv.at[k],
                others[k - 1],
            )
        )
    for copy in gains:
        copy.start()
    gain_all[here] = gain_ref[...]

    copies = []
    for k in range(1, members):
        copy = remote(
            grad_ref, grad_all.at[k], near_send.at[0, k], near_recv.at[0, k], partners[k - 1]
        )
        copies.append(copy)
    local = [pltpu.make_async_copy(grad_ref, grad_all.at[0], home.at[0])]
    local[0].start()

    steps = {}
    across = {}

    def start_lines(w):
        for step in range(1, lines):
            copy = remote(
                shards[w],
                wholes[w].at[here],
                line_send.at[w, step],
                line_recv.at[w, step],
                {"dp": 2 * lax.rem(line + step, lines) + side},
            )
            copy.start()
            steps[w, step] = copy
        copy = remote(
            shards[w], wholes[w].at[here], side_send.at[w, 0], side_recv.at[w, 0], opposite
        )
        copy.start()
        across[w, 0] = copy
        copy = pltpu.make_async_copy(shards[w], wholes[w].at[here], home.at[2 + w])
        copy.start()
        local.append(copy)

    start_lines(0)
    start_lines(1)

    values = hidden_ref[...].astype(WIDE)
    scaled = values * lax.rsqrt(jnp.mean(values * values, axis=-1, keepdims=True) + 1e-06)
    for copy in gains:
        copy.wait()
    width = gain_ref.shape[1]
    for p in range(parts):
        columns = slice(p * width, (p + 1) * width)
        normed_own[:, columns] = (scaled[:, columns] * gain_all[p][:1]).astype(LOW)
    for k in range(1, members):
        copy = remote(
            normed_own, normed_all.at[k], near_send.at[1, k], near_recv.at[1, k], partners[k - 1]
        )
        copy.start()
        copies.insert(0, copy)
    copy = pltpu.make_async_copy(normed_own, normed_all.at[0], home.at[1])
    copy.start()
    local.append(copy)
    for copy in copies[members - 1 :]:
        copy.start()

    for w in range(count):
        if w + 2 < count:
            start_lines(w + 2)
        for step in range(1, lines):
            steps[w, step].wait_recv()
            place = side * lines + lax.rem(line + lines - step, lines)
            copy = remote(
                wholes[w].at[place],
                wholes[w].at[place],
                side_send.at[w, step],
                side_recv.at[w, step],
                opposite,
            )
            copy.start()
            across[w, step] = copy
    for w in range(count):
        for step in range(1, lines):
            steps[w, step].wait_send()
        for step in range(lines):
            across[w, step].wait()
    for copy in copies:
        copy.wait()
    for copy in local:
        copy.wait()


def gather_all(hidden, grad, gains, shards, lines, members):
    count = len(shards)
    parts = 2 * lines
    rows, width = hidden.shape
    sent = sum(shard.size for shard in shards) * parts * 2
    return pl.pallas_call(
        functools.partial(gather_kernel, lines, members, count),
        out_shape=[
            jax.ShapeDtypeStruct((members, rows, width), LOW),
            jax.ShapeDtypeStruct((members, rows, width), LOW),
            jax.ShapeDtypeStruct((parts,) + gains.shape, WIDE),
        ]
        + [jax.ShapeDtypeStruct((parts,) + shard.shape, LOW) for shard in shards],
        in_specs=[INSIDE, ANY, INSIDE] + [ANY] * count,
        out_specs=[ANY, ANY, INSIDE] + [ANY] * count,
        scratch_shapes=[
            pltpu.VMEM((rows, width), LOW),
            pltpu.SemaphoreType.DMA((count, lines)),
            pltpu.SemaphoreType.DMA((count, lines)),
            pltpu.SemaphoreType.DMA((count, lines)),
            pltpu.SemaphoreType.DMA((count, lines)),
            pltpu.SemaphoreType.DMA((2, members)),
            pltpu.SemaphoreType.DMA((2, members)),
            pltpu.SemaphoreType.DMA((parts,)),
            pltpu.SemaphoreType.DMA((parts,)),
            pltpu.SemaphoreType.DMA((2 + count,)),
        ],
        compiler_params=pltpu.CompilerParams(
            collective_id=0, has_side_effects=True, vmem_limit_bytes=32 * 1024 * 1024
        ),
        cost_estimate=pl.CostEstimate(flops=0, bytes_accessed=20 * sent, transcendentals=0),
        name="gather_all",
    )(hidden, grad, gains, *shards)


def scatter_kernel(lines, count, *refs):
    left_ref = refs[0]
    rights = refs[1 : 1 + count]
    outs = refs[1 + count : 1 + 2 * count]
    buffers = refs[1 + 2 * count :]
    far_held, far_got, near_held, near_got = [
        buffers[k * count : (k + 1) * count] for k in range(4)
    ]
    side_send, side_recv, line_send, line_recv = buffers[4 * count :]
    me = lax.axis_index("dp")
    line, side = me // 2, lax.rem(me, 2)
    opposite = {"dp": 2 * line + (1 - side)}
    greet(
        [{"dp": 2 * lax.rem(line + step, lines) + side} for step in range(1, lines)] + [opposite]
    )
    rows = outs[0].shape[0]

    def product(w, place):
        block = left_ref[pl.ds(pl.multiple_of(place * rows, rows), rows), :]
        return jnp.dot(block, rights[w][...], preferred_element_type=WIDE)

    def far_copy(w, place):
        return pltpu.make_async_remote_copy(
            src_ref=far_held[w].at[place],
            dst_ref=far_got[w].at[place],
            send_sem=side_send.at[w, place],
            recv_sem=side_recv.at[w, place],
            device_id=opposite,
            device_id_type=MESH,
        )

    def near_copy(w, step):
        return pltpu.make_async_remote_copy(
            src_ref=near_held[w].at[step],
            dst_ref=near_got[w].at[step],
            send_sem=line_send.at[w, step],
            recv_sem=line_recv.at[w, step],
            device_id={"dp": 2 * lax.rem(line + step, lines) + side},
            device_id_type=MESH,
        )

    def send_far(w):
        def body(step, carry):
            place = lax.rem(line + step + 1, lines)
            far_held[w][place] = product(w, (1 - side) * lines + place).astype(LOW)
            far_copy(w, place).start()
            return carry

        lax.fori_loop(0, lines, body, 0)

    def send_near(w):
        def body(step, carry):
            place = lax.rem(line + step, lines)
            part = product(w, side * lines + place)
            far_copy(w, place).wait_recv()
            near_held[w][step] = (part + far_got[w][place].astype(WIDE)).astype(LOW)
            near_copy(w, step).start()
            return carry

        lax.fori_loop(1, lines, body, 0)
        part = product(w, side * lines + line)
        far_copy(w, line).wait_recv()
        outs[w][...] = part + far_got[w][line].astype(WIDE)

    def finish(w):
        def body(step, carry):
            near_copy(w, step).wait_recv()
            outs[w][...] += near_got[w][step].astype(WIDE)
            near_copy(w, step).wait_send()
            return carry

        lax.fori_loop(1, lines, body, 0)

        def sent(place, carry):
            far_copy(w, place).wait_send()
            return carry

        lax.fori_loop(0, lines, sent, 0)

    send_far(0)
    for w in range(count):
        if w + 1 < count:
            send_far(w + 1)
        send_near(w)
    for w in range(count):
        finish(w)


def scatter_rows(left, rights, lines, tag):
    count = len(rights)
    rows = left.shape[0] // (2 * lines)
    blocks = [(lines, rows, right.shape[1]) for right in rights]
    columns = sum(right.shape[1] for right in rights)
    return pl.pallas_call(
        functools.partial(scatter_kernel, lines, count),
        out_shape=[jax.ShapeDtypeStruct(block[1:], WIDE) for block in blocks],
        in_specs=[INSIDE] * (1 + count),
        out_specs=[INSIDE] * count,
        scratch_shapes=[pltpu.VMEM(block, LOW) for _ in range(4) for block in blocks]
        + [pltpu.SemaphoreType.DMA((count, lines))] * 4,
        compiler_params=pltpu.CompilerParams(
            collective_id=tag, has_side_effects=True, vmem_limit_bytes=ROOM
        ),
        cost_estimate=pl.CostEstimate(
            flops=2 * left.size * columns,
            bytes_accessed=40 * left.shape[0] * columns,
            transcendentals=0,
        ),
        name="scatter_rows",
    )(left, *rights)


def on_device(
    hidden_in,
    out_grad,
    segment_ids,
    norm1_gain,
    w_query,
    w_key,
    w_value,
    w_gate,
    w_out,
    norm2_gain,
    w_mlp_gate,
    w_mlp_up,
    w_mlp_down,
):
    _, rows, width = hidden_in.shape
    parts = lax.axis_size("dp")
    lines = parts // 2
    slice_width = width // parts
    own = lax.axis_index("tensor")
    members = lax.axis_size("tensor")
    length = rows * members

    def to_places(value):
        blocks = [value[:, k * slice_width : (k + 1) * slice_width] for k in by_place()[0]]
        return jnp.concatenate(blocks, axis=1)

    def from_places(value):
        blocks = [value[:, k * slice_width : (k + 1) * slice_width] for k in range(parts)]
        return jnp.concatenate([blocks[k // 2 + k % 2 * lines] for k in range(parts)], axis=1)

    heads_here = w_query.shape[1] // KEY
    first_head = own * heads_here
    key_columns = w_query.shape[1]
    value_columns = w_value.shape[1]

    resid_low = to_places(hidden_in.reshape(rows, width))
    grad_local = to_places(out_grad.reshape(rows, width))
    gain_rows = jnp.concatenate(
        [norm1_gain[None], norm2_gain[None], jnp.zeros((6, slice_width), LOW)]
    ).astype(WIDE)
    normed, grad_full, gains, *gathered = gather_all(
        resid_low,
        grad_local,
        gain_rows,
        [w_query, w_key, w_value, w_gate, w_out],
        lines,
        members,
    )
    normed = normed.reshape(length, width)
    grad_full = grad_full.reshape(length, width)
    gain_first = gains[:, 0].reshape(width)
    gain_second = gains[:, 1].reshape(width)
    query_weight, key_weight, value_weight, gate_weight = [
        whole.reshape(width, whole.shape[2]) for whole in gathered[:4]
    ]
    out_weight = jnp.concatenate([gathered[4][k] for k in range(parts)], axis=1)
    resid_in = resid_low.astype(WIDE)
    w_mlp_gate = after(w_mlp_gate, gains)
    w_mlp_up = after(w_mlp_up, gains)
    w_mlp_down = after(w_mlp_down, gains)
    mlp_gate_weight = gather_dp(w_mlp_gate, 0)
    mlp_up_weight = gather_dp(w_mlp_up, 0)
    down_weight = gather_dp(w_mlp_down, 1)

    position = jnp.concatenate(
        [(own ^ k) * rows + jnp.arange(rows, dtype=jnp.int32) for k in range(members)]
    )
    segments = jnp.concatenate(
        [
            lax.dynamic_slice_in_dim(segment_ids.reshape(length), (own ^ k) * rows, rows)
            for k in range(members)
        ]
    )
    cosine, sine = rotary_tables(position, KEY)
    cosine = cosine[:, None, :]
    sine = sine[:, None, :]

    key_shape = (length, heads_here, KEY)
    query_pre = multiply(normed, query_weight).reshape(key_shape)
    key_pre = multiply(normed, key_weight).reshape(key_shape)
    query = (rotate(query_pre, cosine, sine) * KEY ** (-0.5)).astype(LOW)
    keys = rotate(key_pre, cosine, sine).astype(LOW)
    values = multiply(normed, value_weight).astype(LOW).reshape(length, heads_here, VAL)
    gate_pre = multiply(normed, gate_weight)

    def retention_scores():
        mask = decay_mask(position, segments, first_head, heads_here)
        raw = jnp.einsum("nhk,mhk->hnm", query, keys, preferred_element_type=WIDE)
        return (raw * mask, mask)

    weighted, mask = retention_scores()
    scores_low = weighted.astype(LOW)
    retained = jnp.einsum(
        "hnm,mhv->nhv", scores_low, values, preferred_element_type=WIDE
    ).reshape(length, value_columns)

    def gate_mix(retained_in, gate_in):
        grouped = group_norm(retained_in.reshape(length, heads_here, VAL)).reshape(
            retained_in.shape
        )
        return grouped * jax.nn.silu(gate_in)

    mixed = gate_mix(retained, gate_pre).astype(LOW)
    resid_mid = resid_in + scatter_tensor(multiply(mixed, out_weight))
    normed_mid = gather_tensor(rms_scale(resid_mid, gain_second).astype(LOW))
    gate_hidden = multiply(normed_mid, mlp_gate_weight)
    up_hidden = multiply(normed_mid, mlp_up_weight)

    def gelu_mix(gate_in, up_in):
        return jax.nn.gelu(gate_in, approximate=True) * up_in

    hidden = gelu_mix(gate_hidden, up_hidden).astype(LOW)
    def grad_of_columns(left, right):
        return scatter_dp(multiply_left(left, right).astype(LOW), 1).astype(WIDE)

    def grad_of_rows(left, right):
        return scatter_dp(multiply_left(left, right).astype(LOW), 0).astype(WIDE)

    down_grad = grad_of_columns(hidden, grad_full)
    resid_out = resid_mid + scatter_tensor(multiply(hidden, down_weight))
    hidden_out = from_places(resid_out.astype(LOW)).reshape(hidden_in.shape)

    hidden_grad = multiply_right(grad_full, down_weight)
    _, pull_mix = jax.vjp(gelu_mix, gate_hidden, up_hidden)
    gate_hidden_grad, up_hidden_grad = pull_mix(hidden_grad)
    gate_hidden_low = gate_hidden_grad.astype(LOW)
    up_hidden_low = up_hidden_grad.astype(LOW)
    mlp_gate_grad = grad_of_rows(normed_mid, gate_hidden_low)
    mlp_up_grad = grad_of_rows(normed_mid, up_hidden_low)
    normed_mid_grad = scatter_tensor(
        multiply_right(gate_hidden_low, mlp_gate_weight)
        + multiply_right(up_hidden_low, mlp_up_weight)
    )
    _, pull_second = jax.vjp(rms_scale, resid_mid, gain_second)
    mid_from_norm, gain_second_part = pull_second(normed_mid_grad)
    resid_mid_grad = grad_local.astype(WIDE) + mid_from_norm
    mid_full = gather_tensor(resid_mid_grad.astype(LOW))
    out_weight_grad = grad_of_columns(mixed, mid_full)
    mixed_grad = multiply_right(mid_full, out_weight)
    _, pull_gate = jax.vjp(gate_mix, retained, gate_pre)
    retained_grad, gate_pre_grad = pull_gate(mixed_grad)
    retained_low = retained_grad.astype(LOW).reshape(length, heads_here, VAL)
    gate_pre_low = gate_pre_grad.astype(LOW)
    score_grad = jnp.einsum("nhv,mhv->hnm", retained_low, values, preferred_element_type=WIDE)
    raw_grad = (score_grad * mask).astype(LOW)
    query_grad = jnp.einsum("hnm,mhk->nhk", raw_grad, keys, preferred_element_type=WIDE)
    key_grad = jnp.einsum("hnm,nhk->mhk", raw_grad, query, preferred_element_type=WIDE)
    value_grad = (
        jnp.einsum("hnm,nhv->mhv", scores_low, retained_low, preferred_element_type=WIDE)
        .astype(LOW)
        .reshape(length, value_columns)
    )
    query_pre_grad = (
        (rotate(query_grad, cosine, -sine) * KEY ** (-0.5)).astype(LOW).reshape(length, key_columns)
    )
    key_pre_grad = rotate(key_grad, cosine, -sine).astype(LOW).reshape(length, key_columns)
    total = multiply_right(query_pre_grad, query_weight)
    total = total + multiply_right(key_pre_grad, key_weight)
    total = total + multiply_right(value_grad, value_weight)
    normed_grad = scatter_tensor(total + multiply_right(gate_pre_low, gate_weight))
    gate_weight_grad, value_weight_grad, query_weight_grad, key_weight_grad = scatter_rows(
        normed.T, [gate_pre_low, value_grad, query_pre_grad, key_pre_grad], lines, 1
    )
    _, pull_first = jax.vjp(rms_scale, resid_in, gain_first)
    in_from_norm, gain_first_part = pull_first(normed_grad)
    in_grad = from_places(resid_mid_grad + in_from_norm).reshape(hidden_in.shape)

    gain_part = jnp.stack([gain_first_part, gain_second_part])
    gain_part = gain_part + swap_tensor(gain_part, 1)
    gain_part = gain_part + swap_tensor(gain_part, 2)
    gain_total = scatter_dp(gain_part, 1)
    return (
        hidden_out,
        in_grad,
        gain_total[0],
        query_weight_grad,
        key_weight_grad,
        value_weight_grad,
        gate_weight_grad,
        out_weight_grad,
        gain_total[1],
        mlp_gate_grad,
        mlp_up_grad,
        down_grad,
    )


def solution(mesh):
    return jax.shard_map(
        on_device,
        mesh=mesh,
        in_specs=(
            P("dp", "tensor", None),
            P("dp", "tensor", None),
            P("dp", None),
            P("dp"),
            P("dp", "tensor"),
            P("dp", "tensor"),
            P("dp", "tensor"),
            P("dp", "tensor"),
            P("tensor", "dp"),
            P("dp"),
            P("dp", "tensor"),
            P("dp", "tensor"),
            P("tensor", "dp"),
        ),
        out_specs=(
            P("dp", "tensor", None),
            P("dp", "tensor", None),
            P("dp"),
            P("dp", "tensor"),
            P("dp", "tensor"),
            P("dp", "tensor"),
            P("dp", "tensor"),
            P("tensor", "dp"),
            P("dp"),
            P("dp", "tensor"),
            P("dp", "tensor"),
            P("tensor", "dp"),
        ),
        check_vma=False,
    )
```

time: 1060 us -> 930 us (0.88)
  waiting for transfers between devices: 652 us -> 172 us
  Pallas kernels: 0 us -> 388 us
  starting transfers between devices: 84.5 us -> 11.2 us
  local copies, waits for them, and re-layouts: 94.6 us -> 108 us
  between operations: 2.57 us -> 15.7 us
    ppermute x66 -> x0, waiting for transfers between devices: 638 us -> none  [the longest x36 321 us: shift_line(): return lax.ppermute(value, 'dp', pairs)]
    pallas_call x0 -> x2, Pallas kernels: none -> 388 us  [the longest x1 199 us: gather_all(): pl.pallas_call(functools.partial(gather_kernel, lines, members, count), o...]
    ppermute x22 -> x16, waiting for transfers between devices: 13.7 us -> 121 us  [swap_tensor(): return lax.ppermute(value, 'tensor', [(i, i ^ bit) for i in range(count)])]
    ppermute x66 -> x0, starting transfers between devices: 73.4 us -> none  [the longest x36 51.7 us: shift_line(): return lax.ppermute(value, 'dp', pairs)]
    all_gather x0 -> x3, waiting for transfers between devices: none -> 32.5 us  [gather_dp(): lax.all_gather(shard, 'dp', axis=axis, tiled=True, axis_index_groups=by_p...]
    dot_general x10 -> x4, matrix products: 55.9 us -> 27.8 us  [multiply_left(): lax.dot_general(left, right, (((0,), (0,)), ((), ())), preferred_element_...]
    dot_general x5 -> x8, matrix products: 43 us -> 65.3 us  [multiply(): return jnp.dot(left, right, preferred_element_type=WIDE)]
    reduce_scatter x0 -> x4, waiting for transfers between devices: none -> 17.9 us  [scatter_dp(): lax.psum_scatter(value, 'dp', scatter_dimension=axis, tiled=True, axis_in...]
  transfers between devices with their start and end apart: 88 -> 24, of which waited for: 41 -> 12; matrix products, arithmetic and copies ran while one was open for 20% -> 29% of each run, Pallas kernels for 0% -> 20%
where the time goes in v2:
time: 930 us; the launch traced here: 924 us
  Pallas kernels  388 us (42%)
  matrix products  176 us (19%)
  waiting for transfers between devices  172 us (18%)
  local copies, waits for them, and re-layouts  108 us (12%)
  other arithmetic  53.8 us (6%)
  between operations  15.7 us (2%)
  starting transfers between devices  11.2 us (1%)
    pallas_call x1, Pallas kernels, gather_all(): pl.pallas_call(functools.partial(gather_kernel, lines, members, count), o...  199 us
    pallas_call x1, Pallas kernels, scatter_rows(): pl.pallas_call(functools.partial(scatter_kernel, lines, count), out_shape...  189 us
    ppermute x16, waiting for transfers between devices, swap_tensor(): return lax.ppermute(value, 'tensor', [(i, i ^ bit) for i in range(count)])  121 us
    unnamed x202, local copies, waits for them, and re-layouts  70 us
    dot_general x8, matrix products, multiply_right(): lax.dot_general(left, right, (((1,), (1,)), ((), ())), preferred_element_...  69.3 us
    dot_general x8, matrix products, multiply(): return jnp.dot(left, right, preferred_element_type=WIDE)  65.3 us
    all_gather x3, waiting for transfers between devices, gather_dp(): lax.all_gather(shard, 'dp', axis=axis, tiled=True, axis_index_groups=by_p...  32.5 us
    dot_general x4, matrix products, multiply_left(): lax.dot_general(left, right, (((0,), (0,)), ((), ())), preferred_element_...  27.8 us
  transfers between devices with their start and end apart: 24, of which 12 were waited for; matrix products, arithmetic and copies ran while one was open for 29% of the time, Pallas kernels for 20%

profile of v2, /device:TPU:8, one launch (start us, length us, event | category | flops | bytes accessed | tf_op | source)
XLA Modules:
  0.0 924.1 jit_solution(3433894574313756094)
XLA Ops:
  25.1 199.3 %gather_all.1 = (bf16[4,256,2048]{2,1,0:T(8,128)(2,1)}, bf16[4,256,2048]{2,1,0:T(8,128)(2,1)}, f32[8,8,256]{2,1,0:T(8,128)S(1)}, bf16[8,256,512]{2,1,0:T(8,128)(...) custom-call(bf16[256,2048]{1,0:T(8,128)(2,1)S(1)} %get-tuple-element, ...), custom_call_target="tpu_custom_call" | custom-call | bytes 296222720 | tf_op jit(solution)/shard_map/gather_all/pallas_call | solution.py:248
  233.4 1.9 bitcast_dynamic-update-slice_fusion.7
  239.0 1.9 bitcast_dynamic-update-slice_fusion.4
  242.7 4.0 copy.94
  246.7 4.0 copy.92
  250.6 6.8 fusion.67
  257.4 3.7 fusion.66
  261.1 2.6 fusion
  265.0 3.0 fusion.35
  268.0 7.5 convolution_convert_fusion.5
  276.3 3.2 copy-done.28
  279.5 2.9 multiply_convert_fusion.1
  282.5 2.1 bitcast_reduce_fusion
  285.1 2.4 fusion.13
  289.4 5.0 copy.100
  298.1 10.9 %multiply_convert_fusion.4 = (bf16[1024,864]{1,0:T(8,128)(2,1)S(1)}, f32[1024,864]{1,0:T(8,128)}) fusion(f32[1024,864]{1,0:T(8,128)} %copy.100, bf16[1024,2048]{1,0:T(8,128)(2,1)} %bitcast.135, bf16[2048,864]{1,0:T(8,128)(2,1)} %bitcast.121), kind=kOutput, calls=%fused_computation.32 | convolution fusion | flops 3629187072 | bytes 16580608 | tf_op jit(solution)/shard_map/dot_general | solution.py:17
  309.0 7.2 fusion.62
  316.6 4.1 collective-permute-done
  321.3 2.0 copy-done.21
  326.5 23.4 %collective-permute-done.1 = bf16[256,2048]{1,0:T(8,128)(2,1)S(1)} collective-permute-done((bf16[256,2048]{1,0:T(8,128)(2,1)}, bf16[256,2048]{1,0:T(8,128)(2,1)S(1)}, u32[]{:S(2)}, u32[]{:S(2)}) %collective-permute-start.1) | collective-permute-done | bytes 1048608 | tf_op jit(solution)/shard_map/ppermute | solution.py:80
  349.9 3.5 multiply_reduce_fusion.4
  356.0 23.6 %collective-permute-done.3 = bf16[256,2048]{1,0:T(8,128)(2,1)S(1)} collective-permute-done((bf16[256,2048]{1,0:T(8,128)(2,1)S(1)}, bf16[256,2048]{1,0:T(8,128)(2,1)S(1)}, u32[]{:S(2)}, u32[]{:S(2)}) %collective-permute-start.3) | collective-permute-done | bytes 1048608 | tf_op jit(solution)/shard_map/ppermute | solution.py:80
  382.4 9.0 fusion.52
  391.5 9.6 %fusion.68 = f32[1024,864]{1,0:T(8,128)} fusion(bf16[1024,2048]{1,0:T(8,128)(2,1)} %bitcast.181, bf16[864,2048]{1,0:T(8,128)(2,1)} %all-gather.8.cloned.1.call-done), kind=kOutput, calls=%fused_computation.194 | convolution fusion | flops 3623878656 | bytes 11272192 | tf_op jit(solution)/shard_map/dot_general | solution.py:25
  401.1 32.5 %all-gather.4.cloned.1.call-done = bf16[2048,864]{0,1:T(8,128)(2,1)} async-done(((bf16[256,864]{0,1:T(8,128)(2,1)}), bf16[2048,864]{0,1:T(8,128)(2,1)}) %all-gather.4.cloned.1.call-update) | async-done | bytes 3538960 | tf_op jit(solution)/shard_map/all_gather | solution.py:69
  433.6 13.7 %multiply_convert_fusion.2 = (bf16[1024,864]{1,0:T(8,128)(2,1)S(1)}, bf16[1024,864]{1,0:T(8,128)(2,1)}, bf16[1024,864]{1,0:T(8,128)(2,1)}) fusion(f32[1024,864]{1,0:T(8,128)} %fusion.68, f32[1024,864]{1,0:T(8,128)} %fusion.52, bf16[2048,864]{0,1:T(8,128)(2,1)} %all-gather.4.cloned.1.call-done, bf16[256,2048]{1,0:T(8,128)(2,1)} %collective-permute-done.4, ...), kind=kOutput, calls=%fused_computation.30 | convolution fusion | flops 3663659008 | bytes 20119552 | tf_op jit(solution)/shard_map/dot_general | solution.py:17
  448.6 7.0 convolution_convert_fusion.1
  457.1 6.6 fusion.69
  463.7 6.9 fusion.63
  473.9 7.1 convolution_convert_fusion.2
  481.6 2.1 fusion.22
  485.2 23.0 %collective-permute-done.8 = bf16[256,2048]{1,0:T(8,128)(2,1)S(1)} collective-permute-done((bf16[256,2048]{1,0:T(8,128)(2,1)S(1)}, bf16[256,2048]{1,0:T(8,128)(2,1)S(1)}, u32[]{:S(2)}, u32[]{:S(2)}) %collective-permute-start.8) | collective-permute-done | bytes 1048608 | tf_op jit(solution)/shard_map/ppermute | solution.py:80
  508.2 2.5 multiply_reduce_fusion.2
  513.4 22.2 %collective-permute-done.10 = bf16[256,2048]{1,0:T(8,128)(2,1)S(1)} collective-permute-done((bf16[256,2048]{1,0:T(8,128)(2,1)S(1)}, bf16[256,2048]{1,0:T(8,128)(2,1)S(1)}, u32[]{:S(2)}, u32[]{:S(2)}) %collective-permute-start.10) | collective-permute-done | bytes 1048608 | tf_op jit(solution)/shard_map/ppermute | solution.py:80
  535.6 5.4 convolution_convert_fusion
  541.1 12.4 %fusion.34 = (f32[1024,864]{1,0:T(8,128)}, bf16[1024,864]{1,0:T(8,128)(2,1)}) fusion(f32[1024,864]{1,0:T(8,128)} %get-tuple-element.128, f32[1024,864]{1,0:T(8,128)} %copy.100, bf16[864,2048]{1,0:T(8,128)(2,1)} %bitcast_dynamic-update-slice_fusion, bf16[256,2048]{1,0:T(8,128)(2,1)} %collective-permute-done.11, ...), kind=kOutput, calls=%fused_computation.102 | convolution fusion | flops 3652157440 | bytes 20119552 | tf_op jit(solution)/shard_map/dot_general | solution.py:25
  553.5 5.0 copy.112
  558.6 4.3 multiply_reduce_fusion
  568.1 3.9 multiply_convert_fusion
  575.6 2.0 convolution_convert_fusion.4
  580.2 6.8 fusion.71
  587.0 6.9 fusion.72
  595.9 5.8 fusion.70
  601.7 14.3 %fusion.64 = (bf16[1024,2048]{1,0:T(8,128)(2,1)S(1)}, f32[1024,2048]{1,0:T(8,128)}) fusion(f32[1024,2048]{1,0:T(8,128)} %fusion.72, f32[1024,2048]{1,0:T(8,128)} %fusion.71, f32[1024,2048]{1,0:T(8,128)} %fusion.70, bf16[1024,512]{0,1:T(8,128)(2,1)S(1)} %bitcast.129, bf16[2048,512]{1,0:T(8,128)(2,1)S(1)} %bitcast.118), kind=kOutput, calls=%fused_computation.190 | convolution fusion | flops 2155872256 | bytes 40894464 | tf_op jit(solution)/shard_map/dot_general | solution.py:25
  617.0 3.8 collective-permute-done.12
  623.5 6.6 fusion.65
  630.1 17.1 %collective-permute-done.13 = bf16[256,2048]{1,0:T(8,128)(2,1)S(1)} collective-permute-done((bf16[256,2048]{1,0:T(8,128)(2,1)S(1)}, bf16[256,2048]{1,0:T(8,128)(2,1)S(1)}, u32[]{:S(2)}, u32[]{:S(2)}) %collective-permute-start.13) | collective-permute-done | bytes 1048608 | tf_op jit(solution)/shard_map/ppermute | solution.py:80
  647.2 2.1 fusion.19
  655.9 8.5 convolution_convert_fusion.3
  664.4 6.7 copy.130
  671.1 2.1 convert_element_type.191
  673.2 2.0 copy-done.22
  675.2 2.9 fusion.24
  680.9 2.3 copy.131.refs_3_
  683.2 3.8 copy.118.refs_2_
  687.0 188.7 %scatter_rows.1 = (f32[256,864]{1,0:T(8,128)}, f32[256,864]{1,0:T(8,128)}, f32[256,512]{1,0:T(8,128)}, f32[256,512]{1,0:T(8,128)}) custom-call(bf16[2048,1024]{1,0:T(8,128)(2,1)} %bitcast.138, bf16[1024,864]{1,0:T(8,128)(2,1)} %get-tuple-element.87.refs_1_, bf16[1024,864]{1,0:T(8,128)(2,1)} %copy.118.refs_2_, bf16[1024,512]{1,0:T(8,128)(2,1)} %copy.131.refs_3_, ...), custom_call_target="tpu_custom_call" | custom-call | flops 11542724608 | bytes 225443840 | tf_op jit(solution)/shard_map/scatter_rows/pallas_call | solution.py:371
  875.7 2.4 copy.119
  878.0 2.4 copy.120
  880.4 2.0 convert_element_type.219
  882.4 2.0 convert_element_type.217
  884.4 2.0 convert_element_type.221
  886.4 5.2 fusion.15
  895.6 17.9 %reduce-scatter.8.cloned.1.call-done = bf16[864,256]{1,0:T(8,128)(2,1)} async-done(((bf16[864,2048]{1,0:T(8,128)(2,1)}), bf16[864,256]{1,0:T(8,128)(2,1)}) %reduce-scatter.8.cloned.1.call-update) | async-done | bytes 442384 | tf_op jit(solution)/shard_map/reduce_scatter | solution.py:73
  913.4 2.0 convert_element_type.215
  (298 shorter events, 92.6 us)
Async XLA Ops:
  7.2 13.0 %copy-start.50 = (bf16[256,864]{0,1:T(8,128)(2,1)S(1)}, bf16[256,864]{0,1:T(8,128)(2,1)}, u32[]{:S(2)}) copy-start(bf16[256,864]{0,1:T(8,128)(2,1)} %param.19) | copy-start | bytes 1327108
  7.2 14.6 %copy-start.65 = (bf16[256]{0:T(256)(128)(2,1)S(1)}, bf16[256]{0:T(256)(128)(2,1)}, u32[]{:S(2)}) copy-start(bf16[256]{0:T(256)(128)(2,1)} %param.16) | copy-start | bytes 1540
  7.2 14.6 %copy-start.66 = (bf16[256]{0:T(256)(128)(2,1)S(1)}, bf16[256]{0:T(256)(128)(2,1)}, u32[]{:S(2)}) copy-start(bf16[256]{0:T(256)(128)(2,1)} %param.22) | copy-start | bytes 1540
  7.2 15.8 %copy-start.7 = (bf16[864,256]{1,0:T(8,128)(2,1)S(1)}, bf16[864,256]{1,0:T(8,128)(2,1)}, u32[]{:S(2)}) copy-start(bf16[864,256]{1,0:T(8,128)(2,1)} %refs_7_.1) | copy-start | bytes 1327108
  7.2 375.2 %all-gather.6.cloned.1.call-start = ((), (), s32[]{:S(2)}) async-start(), calls=%async_computation.6 | async-start | bytes 3981312 | tf_op jit(solution)/shard_map/all_gather | solution.py:69
  22.8 327.2 %copy-start = (bf16[256,2048]{1,0:T(8,128)(2,1)}, bf16[256,2048]{1,0:T(8,128)(2,1)S(1)}, u32[]{:S(2)}) copy-start(bf16[256,2048]{1,0:T(8,128)(2,1)S(1)} %get-tuple-element.138.refs_0_) | copy-start | bytes 3145732
  232.3 159.1 %all-gather.8.cloned.1.call-start = ((), (), s32[]{:S(2)}) async-start(), calls=%async_computation.7 | async-start | bytes 3981312 | tf_op jit(solution)/shard_map/all_gather | solution.py:69
  233.1 200.5 %all-gather.4.cloned.1.call-start = ((), (), s32[]{:S(2)}) async-start(), calls=%async_computation.5 | async-start | bytes 3981312 | tf_op jit(solution)/shard_map/all_gather | solution.py:69
  250.6 6.8 copy-start.27
  250.6 6.8 copy-start.39
  265.0 11.3 %copy-start.43 = (pred[1024,1024]{1,0:T(8,128)(4,1)}, pred[1024,1024]{1,0:T(8,128)(4,1)S(1)}, u32[]{:S(2)}) copy-start(pred[1024,1024]{1,0:T(8,128)(4,1)S(1)} %fusion.1) | copy-start | bytes 3145732
  268.0 7.5 copy-start.23
  268.0 7.5 copy-start.40
  268.0 7.6 copy-start.41
  275.5 7.0 copy-start.67
  276.3 6.2 copy-start.30
  276.3 6.2 copy-start.32
  276.3 6.2 copy-start.34
  276.3 6.2 copy-start.36
  309.0 7.2 copy-start.75
  316.2 5.1 copy-start.38
  316.5 4.2 collective-permute-start
  324.5 25.4 %collective-permute-start.1 = (bf16[256,2048]{1,0:T(8,128)(2,1)}, bf16[256,2048]{1,0:T(8,128)(2,1)S(1)}, u32[]{:S(2)}, u32[]{:S(2)}) collective-permute-start(bf16[256,2048]{1,0:T(8,128)(2,1)} %fusion.28), channel_id=1, source_target_pairs={{0,2},{1,3},{2,0},{3,1},{4,6},{5,7},{6,4},{7,5},{8,10},{9,11},{10,... | collective-permute-start | bytes 3145736 | tf_op jit(solution)/shard_map/ppermute | solution.py:80
  325.4 555.0 %reduce-scatter.12.cloned.1.call-start = ((), (), s32[]{:S(2)}) async-start(), calls=%async_computation.10 | async-start | bytes 3981312 | tf_op jit(solution)/shard_map/reduce_scatter | solution.py:73
  355.1 92.2 %copy-start.45 = (bf16[256,2048]{1,0:T(8,128)(2,1)}, bf16[256,2048]{1,0:T(8,128)(2,1)S(1)}, u32[]{:S(2)}) copy-start(bf16[256,2048]{1,0:T(8,128)(2,1)S(1)} %multiply_convert_fusion.5) | copy-start | bytes 3145732
  355.1 24.5 %collective-permute-start.3 = (bf16[256,2048]{1,0:T(8,128)(2,1)S(1)}, bf16[256,2048]{1,0:T(8,128)(2,1)S(1)}, u32[]{:S(2)}, u32[]{:S(2)}) collective-permute-start(bf16[256,2048]{1,0:T(8,128)(2,1)S(1)} %multiply_convert_fusion.5), channel_id=1, source_target_pairs={{0,2},{1,3},{2,0},{3,1},{4,6},{5,7},{6,4},{7,5},{8,10},{9,11},{10,... | collective-permute-start | bytes 3145736 | tf_op jit(solution)/shard_map/ppermute | solution.py:80
  356.0 23.6 %collective-permute-start.2 = (bf16[256,2048]{1,0:T(8,128)(2,1)S(1)}, bf16[256,2048]{1,0:T(8,128)(2,1)S(1)}, u32[]{:S(2)}, u32[]{:S(2)}) collective-permute-start(bf16[256,2048]{1,0:T(8,128)(2,1)S(1)} %multiply_convert_fusion.5), channel_id=1, source_target_pairs={{0,1},{1,0},{2,3},{3,2},{4,5},{5,4},{6,7},{7,6},{8,9},{9,8},{10,11... | collective-permute-start | bytes 3145736 | tf_op jit(solution)/shard_map/ppermute | solution.py:80
  379.6 67.7 %copy-start.60 = (bf16[256,2048]{1,0:T(8,128)(2,1)}, bf16[256,2048]{1,0:T(8,128)(2,1)S(1)}, u32[]{:S(2)}) copy-start(bf16[256,2048]{1,0:T(8,128)(2,1)S(1)} %collective-permute-done.3) | copy-start | bytes 3145732
  379.6 2.8 collective-permute-start.4
  433.6 15.0 %copy-start.63 = (bf16[256,2048]{1,0:T(8,128)(2,1)S(1)}, bf16[256,2048]{1,0:T(8,128)(2,1)}, u32[]{:S(2)}) copy-start(bf16[256,2048]{1,0:T(8,128)(2,1)} %copy-done.62) | copy-start | bytes 3145732
  455.6 426.9 %reduce-scatter.10.cloned.1.call-start = ((), (), s32[]{:S(2)}) async-start(), calls=%async_computation.9 | async-start | bytes 3981312 | tf_op jit(solution)/shard_map/reduce_scatter | solution.py:73
  457.1 6.7 copy-start.58
  457.1 6.7 copy-start.72
  472.4 8.6 collective-permute-start.7
  481.0 403.5 %reduce-scatter.14.cloned.1.call-start = ((), (), s32[]{:S(2)}) async-start(), calls=%async_computation.11 | async-start | bytes 3981312 | tf_op jit(solution)/shard_map/reduce_scatter | solution.py:73
  481.6 26.6 %copy-start.18 = (f32[256,2048]{1,0:T(8,128)S(1)}, f32[256,2048]{1,0:T(8,128)}, u32[]{:S(2)}) copy-start(f32[256,2048]{1,0:T(8,128)} %copy-done.17) | copy-start | bytes 6291460
  483.6 24.6 %collective-permute-start.8 = (bf16[256,2048]{1,0:T(8,128)(2,1)S(1)}, bf16[256,2048]{1,0:T(8,128)(2,1)S(1)}, u32[]{:S(2)}, u32[]{:S(2)}) collective-permute-start(bf16[256,2048]{1,0:T(8,128)(2,1)S(1)} %fusion.22), channel_id=1, source_target_pairs={{0,2},{1,3},{2,0},{3,1},{4,6},{5,7},{6,4},{7,5},{8,10},{9,11},{10,... | collective-permute-start | bytes 3145736 | tf_op jit(solution)/shard_map/ppermute | solution.py:80
  510.7 25.0 %copy-start.56 = (bf16[4,256,2048]{2,1,0:T(8,128)(2,1)S(1)}, bf16[4,256,2048]{2,1,0:T(8,128)(2,1)}, u32[]{:S(2)}) copy-start(bf16[4,256,2048]{2,1,0:T(8,128)(2,1)} %get-tuple-element.37) | copy-start | bytes 12582916
  510.7 25.0 %copy-start.73 = (bf16[1024,864]{1,0:T(8,128)(2,1)S(1)}, bf16[1024,864]{1,0:T(8,128)(2,1)}, u32[]{:S(2)}) copy-start(bf16[1024,864]{1,0:T(8,128)(2,1)} %get-tuple-element.90) | copy-start | bytes 5308420
  512.0 29.1 %copy-start.47 = (bf16[256,2048]{1,0:T(8,128)(2,1)}, bf16[256,2048]{1,0:T(8,128)(2,1)S(1)}, u32[]{:S(2)}) copy-start(bf16[256,2048]{1,0:T(8,128)(2,1)S(1)} %fusion.51) | copy-start | bytes 3145732
  512.0 23.7 %collective-permute-start.10 = (bf16[256,2048]{1,0:T(8,128)(2,1)S(1)}, bf16[256,2048]{1,0:T(8,128)(2,1)S(1)}, u32[]{:S(2)}, u32[]{:S(2)}) collective-permute-start(bf16[256,2048]{1,0:T(8,128)(2,1)S(1)} %fusion.51), channel_id=1, source_target_pairs={{0,2},{1,3},{2,0},{3,1},{4,6},{5,7},{6,4},{7,5},{8,10},{9,11},{10,... | collective-permute-start | bytes 3145736 | tf_op jit(solution)/shard_map/ppermute | solution.py:80
  513.4 27.6 %collective-permute-start.9 = (bf16[256,2048]{1,0:T(8,128)(2,1)S(1)}, bf16[256,2048]{1,0:T(8,128)(2,1)}, u32[]{:S(2)}, u32[]{:S(2)}) collective-permute-start(bf16[256,2048]{1,0:T(8,128)(2,1)S(1)} %fusion.51), channel_id=1, source_target_pairs={{0,1},{1,0},{2,3},{3,2},{4,5},{5,4},{6,7},{7,6},{8,9},{9,8},{10,11... | collective-permute-start | bytes 3145736 | tf_op jit(solution)/shard_map/ppermute | solution.py:80
  535.6 5.5 copy-start.59
  535.6 5.5 collective-permute-start.11
  541.0 351.9 %reduce-scatter.16.cloned.1.call-start = ((), (), s32[]{:S(2)}) async-start(), calls=%async_computation.12 | async-start | bytes 1179648
  558.6 4.3 copy-start.15
  558.6 5.5 copy-start.16
  580.2 6.8 copy-start.11
  580.2 6.8 copy-start.76
  594.2 7.4 copy-start.26
  595.9 5.8 copy-start.3
  616.2 5.1 copy-start.19
  616.4 4.4 collective-permute-start.12
  621.7 25.5 %collective-permute-start.13 = (bf16[256,2048]{1,0:T(8,128)(2,1)S(1)}, bf16[256,2048]{1,0:T(8,128)(2,1)S(1)}, u32[]{:S(2)}, u32[]{:S(2)}) collective-permute-start(bf16[256,2048]{1,0:T(8,128)(2,1)S(1)} %fusion.20), channel_id=1, source_target_pairs={{0,2},{1,3},{2,0},{3,1},{4,6},{5,7},{6,4},{7,5},{8,10},{9,11},{10,... | collective-permute-start | bytes 3145736 | tf_op jit(solution)/shard_map/ppermute | solution.py:80
  623.5 23.7 %copy-start.1 = (bf16[256,2048]{1,0:T(8,128)(2,1)S(1)}, bf16[256,2048]{1,0:T(8,128)(2,1)}, u32[]{:S(2)}) copy-start(bf16[256,2048]{1,0:T(8,128)(2,1)} %copy-done) | copy-start | bytes 3145732
  623.5 23.7 %copy-start.51 = (f32[8,1,256]{2,1,0:T(1,128)S(1)}, f32[8,1,256]{2,1,0:T(1,128)}, u32[]{:S(2)}) copy-start(f32[8,1,256]{2,1,0:T(1,128)} %get-tuple-element.114) | copy-start | bytes 24580
  649.3 1.2 collective-permute-start.14
  650.6 3.8 collective-permute-start.15
  653.8 17.4 %collective-permute-start.5 = (bf16[512,2048]{1,0:T(8,128)(2,1)}, bf16[512,2048]{1,0:T(8,128)(2,1)}, u32[]{:S(2)}, u32[]{:S(2)}) collective-permute-start(bf16[512,2048]{1,0:T(8,128)(2,1)} %pad_maximum_fusion.3), channel_id=1, source_target_pairs={{0,1},{1,0},{2,3},{3,2},{4,5},{5,4},{6,7},{7,6},{8,9},{9,8},{10,11... | collective-permute-start | bytes 6291464 | tf_op jit(solution)/shard_map/ppermute | solution.py:80
  655.9 257.6 %reduce-scatter.8.cloned.1.call-start = ((), (), s32[]{:S(2)}) async-start(), calls=%async_computation.8 | async-start | bytes 3981312 | tf_op jit(solution)/shard_map/reduce_scatter | solution.py:73
  678.1 208.4 %collective-permute-start.6 = (bf16[256,2048]{1,0:T(8,128)(2,1)}, bf16[256,2048]{1,0:T(8,128)(2,1)}, u32[]{:S(2)}, u32[]{:S(2)}) collective-permute-start(bf16[256,2048]{1,0:T(8,128)(2,1)} %fusion.24), channel_id=1, source_target_pairs={{0,2},{1,3},{2,0},{3,1},{4,6},{5,7},{6,4},{7,5},{8,10},{9,11},{10,... | collective-permute-start | bytes 3145736 | tf_op jit(solution)/shard_map/ppermute | solution.py:80
  891.8 23.7 %copy-start.49 = (f32[256,512]{1,0:T(8,128)S(1)}, f32[256,512]{1,0:T(8,128)}, u32[]{:S(2)}) copy-start(f32[256,512]{1,0:T(8,128)} %get-tuple-element.158) | copy-start | bytes 1572868
  891.9 24.3 %copy-start.48 = (f32[256,512]{1,0:T(8,128)S(1)}, f32[256,512]{1,0:T(8,128)}, u32[]{:S(2)}) copy-start(f32[256,512]{1,0:T(8,128)} %get-tuple-element.159) | copy-start | bytes 1572868
  892.9 24.2 %copy-start.52 = (f32[256,2048]{1,0:T(8,128)}, f32[256,2048]{1,0:T(8,128)S(1)}, u32[]{:S(2)}) copy-start(f32[256,2048]{1,0:T(8,128)S(1)} %slice_dynamic-update-slice_fusion) | copy-start | bytes 6291460
  (39 other events, 79.4 us)
Sparse Core Ops, SparseCore 0:
  232.5 65.5 all-gather.5
  300.1 65.7 all-gather.7
  367.8 65.7 all-gather.3
  455.7 79.7 reduce-scatter.11
  539.0 79.0 reduce-scatter.9
  621.6 79.0 reduce-scatter.13
  704.1 110.0 reduce-scatter.15
  818.3 95.1 reduce-scatter.7

commit v3 on v0

v3 whole, which is shorter than its diff:
```python
import functools
import math

import jax
import jax.numpy as jnp
from jax import lax
from jax.experimental import pallas as pl
from jax.experimental.pallas import tpu as pltpu
from jax.sharding import PartitionSpec as P

KEY = 256
VAL = 432
LOW = jnp.bfloat16
WIDE = jnp.float32
WEIGHTS = 8
MESH = pl.DeviceIdType.MESH
ANY = pl.BlockSpec(memory_space=pl.ANY)
INSIDE = pl.BlockSpec(memory_space=pltpu.VMEM)
ROOM = 60 * 1024 * 1024

def rotary_tables(position, width):
    half = width // 2
    frequency = 10000.0 ** (-2.0 * jnp.arange(half, dtype=jnp.int32).astype(WIDE) / width)
    angle = position.astype(WIDE)[:, None] * frequency[None, :]
    return (jnp.cos(angle), jnp.sin(angle))


def greet(peers):
    barrier = pltpu.get_barrier_semaphore()
    for peer in peers:
        pl.semaphore_signal(barrier, inc=1, device_id=peer, device_id_type=MESH)
    pl.semaphore_wait(barrier, len(peers))


def remote(source, target, send, recv, device):
    return pltpu.make_async_remote_copy(
        src_ref=source,
        dst_ref=target,
        send_sem=send,
        recv_sem=recv,
        device_id=device,
        device_id_type=MESH,
    )


def forward_kernel(lines, members, *refs):
    hidden_ref, grad_ref, gain_ref, cos_ref, sin_ref, down_seg, along_seg, rate_ref = refs[:8]
    shards = refs[8:16]
    normed_turned, grad_all, gain_all = refs[16:19]
    wholes = refs[19:27]
    query_out, keys_out, values_out, gate_out, grad_turned = refs[27:32]
    retained_out, mixed_out, resid_out, mid_turned, gate_hidden_out, up_hidden_out = refs[32:38]
    hidden_out = refs[38]
    normed, mid, short, wide_one, wide_two, turned = refs[39:45]
    query, keys, scores, values, retained, gate, mixed, hidden = refs[45:53]
    held, got, base = refs[53:56]
    line_send, line_recv, side_send, side_recv = refs[56:60]
    near_send, near_recv, gain_send, gain_recv, home = refs[60:]

    parts = 2 * lines
    rows, width = hidden_ref.shape
    slice_width = gain_ref.shape[1]
    heads = rate_ref.shape[0]
    value_columns = values.shape[2]
    me = lax.axis_index("dp")
    line, side = me // 2, lax.rem(me, 2)
    here = side * lines + line
    own = lax.axis_index("tensor")
    half, rest = own // 2, lax.rem(own, 2)

    def member(k):
        return 2 * lax.rem(half + k // 2, 2) + lax.rem(rest + lax.rem(k, 2), 2)

    partners = [None] + [{"tensor": member(k)} for k in range(1, members)]
    others = [{"dp": lax.rem(me + k, parts)} for k in range(1, parts)]
    opposite = {"dp": 2 * line + (1 - side)}
    greet(others + partners[1:])

    local = {}
    slots = iter(range(32))

    def keep(source, target):
        slot = next(slots)
        local[slot] = pltpu.make_async_copy(source, target, home.at[slot])
        local[slot].start()
        return slot

    def finish(slot):
        local.pop(slot).wait()

    near = {}

    def near_start(tag, source, target, k):
        copy = remote(source, target, near_send.at[tag], near_recv.at[tag], partners[k])
        copy.start()
        near[tag] = copy

    steps = {}
    across = {}
    ours = {}

    def start_lines(w):
        for step in range(1, lines):
            steps[w, step] = remote(
                shards[w],
                wholes[w].at[here],
                line_send.at[w, step],
                line_recv.at[w, step],
                {"dp": 2 * lax.rem(line + step, lines) + side},
            )
            steps[w, step].start()
        across[w, 0] = remote(
            shards[w], wholes[w].at[here], side_send.at[w, 0], side_recv.at[w, 0], opposite
        )
        across[w, 0].start()
        ours[w] = keep(shards[w], wholes[w].at[here])

    def pass_on(w, third):
        for step in range(1 + third * (lines - 1) // 3, 1 + (third + 1) * (lines - 1) // 3):
            steps[w, step].wait_recv()
            place = side * lines + lax.rem(line + lines - step, lines)
            across[w, step] = remote(
                wholes[w].at[place],
                wholes[w].at[place],
                side_send.at[w, step],
                side_recv.at[w, step],
                opposite,
            )
            across[w, step].start()

    def complete(w):
        for step in range(lines):
            across[w, step].wait_recv()
        finish(ours[w])

    def load(w, target, sem):
        copy = pltpu.make_async_copy(wholes[w], target, sem)
        copy.start()
        copy.wait()

    def stage(w, target, body):
        if w + 1 < WEIGHTS:
            pass_on(w + 1, 0)
        complete(w)
        load(w, target, home.at[home.shape[0] - 1 - w])
        lax.fori_loop(0, members // 2, body, 0)
        if w + 1 < WEIGHTS:
            pass_on(w + 1, 1)
        lax.fori_loop(members // 2, members, body, 0)
        if w + 1 < WEIGHTS:
            pass_on(w + 1, 2)
        if w + 3 < WEIGHTS:
            start_lines(w + 3)

    gains = []
    for k in range(1, parts):
        copy = remote(
            gain_ref, gain_all.at[here], gain_send.at[k], gain_recv.at[k], others[k - 1]
        )
        copy.start()
        gains.append(copy)
    gain_all[here] = gain_ref[...]
    for w in range(3):
        start_lines(w)

    def scale_into(target, scaled, which):
        for p in range(parts):
            columns = slice(p * slice_width, (p + 1) * slice_width)
            target[0, :, columns] = (
                scaled[:, columns] * gain_all[p][which : which + 1]
            ).astype(LOW)

    resid = hidden_ref[...].astype(WIDE)
    scaled = resid * lax.rsqrt(jnp.mean(resid * resid, axis=-1, keepdims=True) + 1e-06)
    for copy in gains:
        copy.wait_recv()
    scale_into(normed, scaled, 0)
    for k in range(1, members):
        near_start(k - 1, normed.at[0], normed.at[k], k)
    for k in range(1, members):
        near_start(2 + k, grad_ref, mid.at[k], k)
    grad_kept = keep(grad_ref, mid.at[0])
    for third in range(3):
        pass_on(0, third)
    for k in range(1, members):
        near[k - 1].wait_recv()

    def turn_over(source):
        tile = 256

        def body(k, carry):
            at = pl.ds(pl.multiple_of(k * rows, rows), rows)
            for c in range(width // tile):
                columns = slice(c * tile, (c + 1) * tile)
                turned[columns, at] = source[k, :, columns].T
            return carry

        lax.fori_loop(0, members, body, 0)

    turn_over(normed)
    turned_kept = keep(turned, normed_turned)

    def flat(ref):
        return ref[...].reshape(width, ref.shape[2])

    def turn(source, target, scale):
        def body(k, carry):
            pre = jnp.dot(normed[k], flat(source), preferred_element_type=WIDE)
            at = pl.ds(pl.multiple_of(k * rows, rows), rows)
            cosine, sine = cos_ref[at, :], sin_ref[at, :]
            wing = KEY // 2
            for h in range(heads):
                first = pre[:, h * KEY : h * KEY + wing]
                second = pre[:, h * KEY + wing : (h + 1) * KEY]
                target[k, :, h * KEY : h * KEY + wing] = (
                    (first * cosine - second * sine) * scale
                ).astype(LOW)
                target[k, :, h * KEY + wing : (h + 1) * KEY] = (
                    (second * cosine + first * sine) * scale
                ).astype(LOW)
            return carry

        return body

    stage(0, short, turn(short, query, KEY ** (-0.5)))
    keep(query, query_out)
    stage(1, short, turn(short, keys, 1.0))
    keep(keys, keys_out)

    def score(k, carry):
        place = member(k)
        at = pl.multiple_of(place * rows, rows)
        segment = down_seg[pl.ds(at, rows), :]
        for h in range(heads):
            head = slice(h * KEY, (h + 1) * KEY)
            for m in range(members):
                start = pl.multiple_of(member(m) * rows, rows)
                raw = lax.dot_general(
                    query[k, :, head],
                    keys[m, :, head],
                    (((1,), (1,)), ((), ())),
                    preferred_element_type=WIDE,
                )
                distance = (
                    lax.broadcasted_iota(jnp.int32, (rows, rows), 0)
                    - lax.broadcasted_iota(jnp.int32, (rows, rows), 1)
                    + (at - start)
                )
                same = (distance >= 0) & (segment == along_seg[:, pl.ds(start, rows)])
                decay = jnp.exp(
                    rate_ref[h : h + 1, :1] * jnp.maximum(distance, 0).astype(WIDE)
                )
                scores[h, k, :, m * rows : (m + 1) * rows] = (
                    raw * jnp.where(same, decay, 0.0)
                ).astype(LOW)
        return carry

    lax.fori_loop(0, members, score, 0)
    finish(grad_kept)
    for k in range(1, members):
        near[2 + k].wait_recv()
    finish(turned_kept)
    turn_over(mid)
    turned_kept = keep(turned, grad_turned)
    grad_kept = keep(mid, grad_all)

    column = lax.broadcasted_iota(jnp.int32, (rows, value_columns), 1)

    def by_head(parts_of):
        result = parts_of[0]
        for h in range(1, heads):
            result = jnp.where(column < h * VAL, result, parts_of[h])
        return result

    def head_mean(value):
        means = []
        for h in range(heads):
            inside = (column >= h * VAL) & (column < (h + 1) * VAL)
            total = jnp.sum(jnp.where(inside, value, 0.0), axis=-1, keepdims=True)
            means.append(total * (1.0 / VAL))
        return by_head(means)

    def make_values(k, carry):
        values[k] = jnp.dot(normed[k], flat(wide_one), preferred_element_type=WIDE).astype(LOW)
        return carry

    stage(2, wide_one, make_values)
    keep(values, values_out)

    def retain(k, carry):
        every = values[...].reshape(members * rows, value_columns)
        retained[k] = by_head(
            [
                jnp.dot(scores[h, k], every, preferred_element_type=WIDE)
                for h in range(heads)
            ]
        )
        return carry

    lax.fori_loop(0, members, retain, 0)
    retained_kept = keep(retained, retained_out)

    def make_mixed(k, carry):
        pre = jnp.dot(normed[k], flat(wide_two), preferred_element_type=WIDE)
        gate[k] = pre
        value = retained[k]
        centred = value - head_mean(value)
        grouped = centred * lax.rsqrt(head_mean(centred * centred) + 1.0)
        mixed[k] = (grouped * (pre / (1.0 + jnp.exp(-pre)))).astype(LOW)
        return carry

    stage(3, wide_two, make_mixed)
    gate_kept = keep(gate, gate_out)
    keep(mixed, mixed_out)

    def project(k, put):
        for p in range(parts):
            columns = slice(p * slice_width, (p + 1) * slice_width)
            put(
                columns,
                lax.dot_general(
                    mixed[k],
                    wide_one[p],
                    (((1,), (1,)), ((), ())),
                    preferred_element_type=WIDE,
                ),
            )

    def put_low(slot):
        def put(columns, value):
            held[slot, :, columns] = value.astype(LOW)

        return put

    def put_sum(columns, value):
        base[:, columns] = value

    pass_on(5, 0)
    complete(4)
    load(4, wide_one, home.at[home.shape[0] - 5])
    finish(grad_kept)
    project(3, put_low(0))
    near_start(6, held.at[0], got.at[0], 1)
    project(2, put_sum)
    pass_on(5, 1)
    near[6].wait_recv()
    held[1] = (base[...] + got[0].astype(WIDE)).astype(LOW)
    near_start(8, held.at[1], got.at[1], 2)
    project(1, put_low(2))
    near_start(7, held.at[2], got.at[2], 1)
    project(0, put_sum)
    pass_on(5, 2)
    start_lines(7)
    near[7].wait_recv()
    base[...] = base[...] + got[2].astype(WIDE) + hidden_ref[...].astype(WIDE)
    pass_on(6, 0)
    near[8].wait_recv()
    resid = base[...] + got[1].astype(WIDE)
    resid_out[...] = resid
    scaled = resid * lax.rsqrt(jnp.mean(resid * resid, axis=-1, keepdims=True) + 1e-06)
    scale_into(mid, scaled, 1)
    near_start(10, mid.at[0], mid.at[2], 2)
    near_start(9, mid.at[0], mid.at[1], 1)
    pass_on(6, 1)
    pass_on(6, 2)
    near[10].wait_recv()
    near_start(11, mid.at[2], mid.at[3], 1)
    complete(5)
    load(5, wide_two, home.at[home.shape[0] - 6])
    near[9].wait_recv()
    near[11].wait_recv()
    finish(retained_kept)
    finish(gate_kept)

    def make_gate(k, carry):
        gate[k] = jnp.dot(mid[k], flat(wide_two), preferred_element_type=WIDE)
        return carry

    lax.fori_loop(0, members, make_gate, 0)
    keep(gate, gate_hidden_out)
    finish(turned_kept)
    turn_over(mid)
    keep(turned, mid_turned)
    pass_on(7, 0)
    pass_on(7, 1)
    pass_on(7, 2)
    complete(6)
    load(6, wide_one, home.at[home.shape[0] - 7])

    def make_hidden(k, carry):
        up = jnp.dot(mid[k], flat(wide_one), preferred_element_type=WIDE)
        retained[k] = up
        pre = gate[k]
        inner = (2.0 / math.pi) ** 0.5 * (pre + 0.044715 * (pre * pre * pre))
        hidden[k] = (0.5 * pre * (1.0 + jnp.tanh(inner)) * up).astype(LOW)
        return carry

    lax.fori_loop(0, members, make_hidden, 0)
    keep(retained, up_hidden_out)
    keep(hidden, hidden_out)
    complete(7)
    for w in range(WEIGHTS):
        for step in range(1, lines):
            steps[w, step].wait_send()
        for step in range(lines):
            across[w, step].wait_send()
    for copy in gains:
        copy.wait_send()
    for copy in near.values():
        copy.wait_send()
    for slot in list(local):
        finish(slot)


def forward(hidden, grad, gains, cosine, sine, segments, rates, shards, lines, members):
    parts = 2 * lines
    rows, width = hidden.shape
    heads = rates.shape[0]
    key_columns, value_columns = shards[0].shape[1], shards[2].shape[1]
    length = rows * members
    blocks = (members, rows)
    turned = (width, length)
    outs = [
        (turned, LOW),
        (blocks + (width,), LOW),
        ((parts,) + gains.shape, WIDE),
    ]
    outs += [((parts,) + shard.shape, LOW) for shard in shards]
    outs += [
        (blocks + (key_columns,), LOW),
        (blocks + (key_columns,), LOW),
        (blocks + (value_columns,), LOW),
        (blocks + (value_columns,), WIDE),
        (turned, LOW),
        (blocks + (value_columns,), WIDE),
        (blocks + (value_columns,), LOW),
        ((rows, width), WIDE),
        (turned, LOW),
        (blocks + (value_columns,), WIDE),
        (blocks + (value_columns,), WIDE),
        (blocks + (value_columns,), LOW),
    ]
    places = [ANY] * len(outs)
    places[2] = INSIDE
    places[18] = INSIDE
    tags = 12
    return pl.pallas_call(
        functools.partial(forward_kernel, lines, members),
        out_shape=[jax.ShapeDtypeStruct(shape, dtype) for shape, dtype in outs],
        in_specs=[INSIDE, ANY] + [INSIDE] * 6 + [ANY] * WEIGHTS,
        out_specs=places,
        scratch_shapes=[
            pltpu.VMEM(blocks + (width,), LOW),
            pltpu.VMEM(blocks + (width,), LOW),
            pltpu.VMEM((parts,) + shards[0].shape, LOW),
            pltpu.VMEM((parts,) + shards[2].shape, LOW),
            pltpu.VMEM((parts,) + shards[2].shape, LOW),
            pltpu.VMEM(turned, LOW),
            pltpu.VMEM(blocks + (key_columns,), LOW),
            pltpu.VMEM(blocks + (key_columns,), LOW),
            pltpu.VMEM((heads, members, rows, length), LOW),
            pltpu.VMEM(blocks + (value_columns,), LOW),
            pltpu.VMEM(blocks + (value_columns,), WIDE),
            pltpu.VMEM(blocks + (value_columns,), WIDE),
            pltpu.VMEM(blocks + (value_columns,), LOW),
            pltpu.VMEM(blocks + (value_columns,), LOW),
            pltpu.VMEM((3, rows, width), LOW),
            pltpu.VMEM((3, rows, width), LOW),
            pltpu.VMEM((rows, width), WIDE),
            pltpu.SemaphoreType.DMA((WEIGHTS, lines)),
            pltpu.SemaphoreType.DMA((WEIGHTS, lines)),
            pltpu.SemaphoreType.DMA((WEIGHTS, lines)),
            pltpu.SemaphoreType.DMA((WEIGHTS, lines)),
            pltpu.SemaphoreType.DMA((tags,)),
            pltpu.SemaphoreType.DMA((tags,)),
            pltpu.SemaphoreType.DMA((parts,)),
            pltpu.SemaphoreType.DMA((parts,)),
            pltpu.SemaphoreType.DMA((40,)),
        ],
        compiler_params=pltpu.CompilerParams(
            collective_id=0, has_side_effects=True, vmem_limit_bytes=ROOM
        ),
        cost_estimate=pl.CostEstimate(
            flops=10**11, bytes_accessed=10**9, transcendentals=0
        ),
        name="forward",
    )(hidden, grad, gains, cosine, sine, segments.T, segments, rates, *shards)


class Scatter:
    def __init__(self, lines, held, far_got, near_got, spare, sems):
        self.lines = lines
        self.held, self.far_got, self.near_got, self.spare = held, far_got, near_got, spare
        self.side_send, self.side_recv, self.line_send, self.line_recv, self.home = sems
        me = lax.axis_index("dp")
        self.line, self.side = me // 2, lax.rem(me, 2)
        self.opposite = {"dp": 2 * self.line + (1 - self.side)}

    def peer(self, step):
        return {"dp": 2 * lax.rem(self.line + step, self.lines) + self.side}

    def peers(self):
        return [self.opposite] + [self.peer(step) for step in range(1, self.lines)]

    def far_copy(self, w, place):
        return remote(
            self.held[w].at[place],
            self.far_got[w].at[place],
            self.side_send.at[w, place],
            self.side_recv.at[w, place],
            self.opposite,
        )

    def near_copy(self, w, step):
        place = lax.rem(self.line + step, self.lines)
        return remote(
            self.held[w].at[place],
            self.near_got[w].at[step],
            self.line_send.at[w, step],
            self.line_recv.at[w, step],
            self.peer(step),
        )

    def fetch(self, source):
        spare = self.spare[source.shape[-1]]
        copy = pltpu.make_async_copy(source, spare, self.home)
        copy.start()
        copy.wait()
        return spare[...].astype(WIDE)

    def product(self, left, right, place):
        rows = self.held[0].shape[1]
        block = left[pl.ds(pl.multiple_of(place * rows, rows), rows), :]
        every = right[...]
        return jnp.dot(
            block,
            every.reshape(every.shape[0] * every.shape[1], every.shape[2]),
            preferred_element_type=WIDE,
        )

    def far(self, w, left, right):
        def body(step, carry):
            place = lax.rem(self.line + step + 1, self.lines)
            other = (1 - self.side) * self.lines + place
            self.held[w][place] = self.product(left, right, other).astype(LOW)
            self.far_copy(w, place).start()
            return carry

        lax.fori_loop(0, self.lines, body, 0)

    def near(self, w, left, right):
        def body(step, carry):
            place = lax.rem(self.line + step, self.lines)
            part = self.product(left, right, self.side * self.lines + place)
            self.far_copy(w, place).wait_recv()
            total = part + self.fetch(self.far_got[w].at[place])
            self.far_copy(w, place).wait_send()
            self.held[w][place] = total.astype(LOW)
            self.near_copy(w, step).start()
            return carry

        lax.fori_loop(1, self.lines, body, 0)
        part = self.product(left, right, self.side * self.lines + self.line)
        self.far_copy(w, self.line).wait_recv()
        total = part + self.fetch(self.far_got[w].at[self.line])
        self.far_copy(w, self.line).wait_send()
        self.held[w][self.line] = total.astype(LOW)
        self.own_copy(w).start()

    def own_copy(self, w):
        return pltpu.make_async_copy(
            self.held[w].at[self.line], self.near_got[w].at[0], self.line_send.at[w, 0]
        )

    def finish(self, w):
        def body(step, carry):
            self.near_copy(w, step).wait()
            return carry

        lax.fori_loop(1, self.lines, body, 0)
        self.own_copy(w).wait()


class Near:
    def __init__(self, send, recv):
        self.send, self.recv = send, recv
        self.flight = {}
        own = lax.axis_index("tensor")
        half, rest = own // 2, lax.rem(own, 2)
        self.member = lambda k: 2 * lax.rem(half + k // 2, 2) + lax.rem(rest + lax.rem(k, 2), 2)

    def partners(self, members):
        return [{"tensor": self.member(k)} for k in range(1, members)]

    def start(self, tag, source, target, k):
        copy = remote(source, target, self.send.at[tag], self.recv.at[tag], self.partners(4)[k - 1])
        copy.start()
        self.flight[tag] = copy

    def wait(self, tag):
        self.flight[tag].wait_recv()

    def sent(self, tag):
        self.flight[tag].wait_send()


def dot_across(left, right):
    return lax.dot_general(
        left, right, (((1,), (1,)), ((), ())), preferred_element_type=WIDE
    )


def feed_kernel(lines, members, *refs):
    grad_ref, grad_turned, mid_turned, hidden, resid_ref, gain_all = refs[:6]
    gate_weight, up_weight, down_weight, gate_hidden, up_hidden = refs[6:11]
    near_got, mid_all, mid_grad_out, hidden_out, gain_out = refs[11:14], *refs[14:18]
    far_got = refs[18:21]
    gate_low, up_low, pre, up = refs[21:25]
    scatter_held = refs[25:28]
    spare, held, got, last, base, mid = refs[28:34]
    sems = refs[34:38]
    near_send, near_recv, home = refs[38:]
    parts = 2 * lines
    rows, width = resid_ref.shape
    slice_width = width // parts
    scatter = Scatter(
        lines,
        scatter_held,
        far_got,
        near_got,
        {spare.shape[1]: spare},
        sems + (home.at[0],),
    )
    near = Near(near_send, near_recv)
    greet(scatter.peers() + near.partners(members))
    scatter.far(0, grad_turned, hidden)

    def flat(ref):
        return ref[...].reshape(width, ref.shape[2])

    def pull(k, carry):
        first = pltpu.make_async_copy(gate_hidden.at[k], pre, home.at[1])
        second = pltpu.make_async_copy(up_hidden.at[k], up, home.at[2])
        first.start()
        second.start()
        grad = jnp.dot(grad_ref[k], flat(down_weight), preferred_element_type=WIDE)
        first.wait()
        second.wait()
        value = pre[...]
        root = (2.0 / math.pi) ** 0.5
        square = value * value
        lift = jnp.tanh(root * (value + 0.044715 * (value * square)))
        ramp = 0.5 * (1.0 + lift)
        slope = ramp + 0.5 * value * (1.0 - lift * lift) * root * (1.0 + 0.134145 * square)
        gate_low[k] = (grad * up[...] * slope).astype(LOW)
        up_low[k] = (grad * (value * ramp)).astype(LOW)
        return carry

    lax.fori_loop(0, members, pull, 0)
    scatter.far(1, mid_turned, gate_low)

    def back(k, put):
        for p in range(parts):
            columns = slice(p * slice_width, (p + 1) * slice_width)
            put(
                columns,
                dot_across(gate_low[k], gate_weight[p]) + dot_across(up_low[k], up_weight[p]),
            )

    def put_low(slot):
        def put(columns, value):
            held[slot, :, columns] = value.astype(LOW)

        return put

    def put_sum(columns, value):
        base[:, columns] = value

    back(3, put_low(0))
    near.start(0, held.at[0], got.at[0], 1)
    back(2, put_sum)
    near.wait(0)
    near.sent(0)
    held[0] = (base[...] + got[0].astype(WIDE)).astype(LOW)
    near.start(1, held.at[0], got.at[1], 2)
    back(1, put_low(1))
    near.start(2, held.at[1], got.at[2], 1)
    back(0, put_sum)
    scatter.far(2, mid_turned, up_low)
    near.wait(2)
    base[...] += got[2].astype(WIDE)
    near.wait(1)
    normed_grad = base[...] + got[1].astype(WIDE)
    resid = resid_ref[...]
    scale = lax.rsqrt(jnp.mean(resid * resid, axis=-1, keepdims=True) + 1e-06)
    unit = resid * scale
    base[...] = normed_grad * unit
    gain_out[...] = jnp.broadcast_to(
        jnp.sum(base[...], axis=0, keepdims=True), gain_out.shape
    )
    dot = jnp.zeros((rows, 1), WIDE)
    for p in range(parts):
        columns = slice(p * slice_width, (p + 1) * slice_width)
        dot += jnp.sum(base[:, columns] * gain_all[p][1:2], axis=-1, keepdims=True)
    dot = dot * (1.0 / width)
    base[...] = normed_grad
    for p in range(parts):
        columns = slice(p * slice_width, (p + 1) * slice_width)
        block = resid_ref[:, columns] * scale
        mid_grad = grad_ref[0, :, columns].astype(WIDE) + scale * (
            base[:, columns] * gain_all[p][1:2] - block * dot
        )
        base[:, columns] = mid_grad
        mid[:, columns] = mid_grad.astype(LOW)
    mid_grad_copy = pltpu.make_async_copy(base, mid_grad_out, home.at[1])
    mid_grad_copy.start()
    near.start(3, mid, mid_all.at[2], 2)
    near.start(4, mid, mid_all.at[1], 1)
    own = pltpu.make_async_copy(mid, mid_all.at[0], home.at[3])
    own.start()
    scatter.near(0, grad_turned, hidden)
    near.wait(3)
    near.start(5, mid_all.at[2], mid_all.at[3], 1)
    scatter.near(1, mid_turned, gate_low)

    def down(k, put):
        for p in range(parts):
            columns = slice(p * slice_width, (p + 1) * slice_width)
            put(columns, dot_across(hidden[k], down_weight[p]))

    near.sent(1)
    near.sent(2)
    down(3, put_low(0))
    mid_grad_copy.wait()
    near.start(6, held.at[0], last.at[0], 1)
    down(2, put_sum)
    near.wait(6)
    near.sent(6)
    held[0] = (base[...] + last[0].astype(WIDE)).astype(LOW)
    near.start(7, held.at[0], last.at[1], 2)
    down(1, put_low(1))
    near.start(8, held.at[1], last.at[2], 1)
    down(0, put_sum)
    scatter.near(2, mid_turned, up_low)
    near.wait(8)
    near.wait(7)
    own.wait()
    near.sent(3)
    near.sent(4)
    mid[...] = (
        base[...] + last[2].astype(WIDE) + last[1].astype(WIDE) + resid_ref[...]
    ).astype(LOW)
    own = pltpu.make_async_copy(mid, hidden_out, home.at[3])
    own.start()
    for w in range(3):
        scatter.finish(w)
    near.wait(4)
    near.wait(5)
    own.wait()
    for tag in (5, 7, 8):
        near.sent(tag)


def feed_backward(
    grad, grad_turned, mid_turned, hidden, resid, gains, weights, pres, lines, members
):
    parts = 2 * lines
    rows, width = resid.shape
    columns = hidden.shape[2]
    slice_width = width // parts
    blocks = (members, rows)
    piece = (lines, slice_width, columns)
    outs = [(piece, LOW)] * 3
    outs += [
        (blocks + (width,), LOW),
        ((rows, width), WIDE),
        ((rows, width), LOW),
        ((8, width), WIDE),
    ]
    outs += [(piece, LOW)] * 3
    return pl.pallas_call(
        functools.partial(feed_kernel, lines, members),
        out_shape=[jax.ShapeDtypeStruct(shape, dtype) for shape, dtype in outs],
        in_specs=[INSIDE] * 9 + [ANY] * 2,
        out_specs=[ANY] * 6 + [INSIDE] + [ANY] * 3,
        scratch_shapes=[
            pltpu.VMEM(blocks + (columns,), LOW),
            pltpu.VMEM(blocks + (columns,), LOW),
            pltpu.VMEM((rows, columns), WIDE),
            pltpu.VMEM((rows, columns), WIDE),
            pltpu.VMEM(piece, LOW),
            pltpu.VMEM(piece, LOW),
            pltpu.VMEM(piece, LOW),
            pltpu.VMEM(piece[1:], LOW),
            pltpu.VMEM((2, rows, width), LOW),
            pltpu.VMEM((3, rows, width), LOW),
            pltpu.VMEM((3, rows, width), LOW),
            pltpu.VMEM((rows, width), WIDE),
            pltpu.VMEM((rows, width), LOW),
            pltpu.SemaphoreType.DMA((3, lines)),
            pltpu.SemaphoreType.DMA((3, lines)),
            pltpu.SemaphoreType.DMA((3, lines)),
            pltpu.SemaphoreType.DMA((3, lines)),
            pltpu.SemaphoreType.DMA((9,)),
            pltpu.SemaphoreType.DMA((9,)),
            pltpu.SemaphoreType.DMA((4,)),
        ],
        compiler_params=pltpu.CompilerParams(
            collective_id=1, has_side_effects=True, vmem_limit_bytes=ROOM
        ),
        cost_estimate=pl.CostEstimate(flops=10**11, bytes_accessed=10**9, transcendentals=0),
        name="feed_backward",
    )(grad, grad_turned, mid_turned, hidden, resid, gains, *weights, *pres)[:7]


def retention_kernel(lines, members, *refs):
    mixed, normed_turned, query, keys, values = refs[:5]
    cos_ref, sin_ref, down_seg, along_seg, rate_ref = refs[5:10]
    hidden_ref, gain_all, gain_part = refs[10:13]
    mid_grad_ref, mid_all, retained_all, gate_all = refs[13:17]
    weights = refs[17:22]
    near_got, in_grad_out, gain_out = refs[22:27], refs[27], refs[28]
    far_got = refs[29:34]
    turned, wide_one, wide_two, short_one, short_two = refs[34:39]
    gate_low, retained_low, value_low, query_low, key_low = refs[39:44]
    scatter_held = refs[44:49]
    spare_wide, spare_short, held, got, base, retained, gate = refs[49:56]
    pieces, piece_got, total, total_got = refs[56:60]
    sems = refs[60:64]
    near_send, near_recv, gain_send, gain_recv, home = refs[64:]
    parts = 2 * lines
    rows, width = hidden_ref.shape
    slice_width = width // parts
    heads = rate_ref.shape[0]
    value_columns = values.shape[2]
    length = rows * members
    scatter = Scatter(
        lines,
        scatter_held,
        far_got,
        near_got,
        {spare_wide.shape[1]: spare_wide, spare_short.shape[1]: spare_short},
        sems + (home.at[0],),
    )
    near = Near(near_send, near_recv)
    me = lax.axis_index("dp")
    here = scatter.side * lines + scatter.line
    others = [{"dp": lax.rem(me + k, parts)} for k in range(1, parts)]
    greet(others + near.partners(members))

    def fetch(source, target, sem):
        copy = pltpu.make_async_copy(source, target, home.at[sem])
        copy.start()
        return copy

    out_copy = fetch(weights[0], wide_one, 1)
    value_copy = fetch(weights[2], wide_two, 2)
    query_copy = fetch(weights[3], short_one, 3)
    key_copy = fetch(weights[4], short_two, 4)
    grad_copy = fetch(mid_grad_ref, in_grad_out, 7)

    def turn_over(k, carry):
        fetch(mid_all.at[k], held.at[0], 8).wait()
        at = pl.ds(pl.multiple_of(k * rows, rows), rows)
        for c in range(width // 256):
            columns = slice(c * 256, (c + 1) * 256)
            turned[columns, at] = held[0, :, columns].T
        return carry

    lax.fori_loop(0, members, turn_over, 0)
    scatter.far(0, turned, mixed)
    out_copy.wait()

    column = lax.broadcasted_iota(jnp.int32, (rows, value_columns), 1)

    def by_head(parts_of):
        result = parts_of[0]
        for h in range(1, heads):
            result = jnp.where(column < h * VAL, result, parts_of[h])
        return result

    def inside(h):
        return (column >= h * VAL) & (column < (h + 1) * VAL)

    def head_mean(value):
        return by_head(
            [
                jnp.sum(jnp.where(inside(h), value, 0.0), axis=-1, keepdims=True) * (1.0 / VAL)
                for h in range(heads)
            ]
        )

    def unmix(k, carry):
        first = fetch(retained_all.at[k], retained, 5)
        second = fetch(gate_all.at[k], gate, 6)
        fetch(mid_all.at[k], held.at[0], 8).wait()
        grad = jnp.dot(
            held[0],
            wide_one[...].reshape(width, value_columns),
            preferred_element_type=WIDE,
        )
        first.wait()
        second.wait()
        value = retained[...]
        centred = value - head_mean(value)
        rate = lax.rsqrt(head_mean(centred * centred) + 1.0)
        pre = gate[...]
        sigma = 1.0 / (1.0 + jnp.exp(-pre))
        gate_low[k] = (
            grad * (centred * rate) * (sigma * (1.0 + pre * (1.0 - sigma)))
        ).astype(LOW)
        grouped_grad = grad * (pre * sigma)
        retained_low[k] = (
            rate * (grouped_grad - head_mean(grouped_grad))
            - (rate * rate * rate) * centred * head_mean(grouped_grad * centred)
        ).astype(LOW)
        return carry

    lax.fori_loop(0, members, unmix, 0)
    scatter.far(1, normed_turned, gate_low)
    gate_copy = fetch(weights[1], wide_one, 1)

    def decay(h, late, early, late_segment, early_segment, turn):
        sign = -1 if turn else 1
        distance = (
            sign
            * (
                lax.broadcasted_iota(jnp.int32, (rows, rows), 0)
                - lax.broadcasted_iota(jnp.int32, (rows, rows), 1)
            )
            + (late - early)
        )
        same = (distance >= 0) & (late_segment == early_segment)
        return jnp.where(
            same,
            jnp.exp(rate_ref[h : h + 1, :1] * jnp.maximum(distance, 0).astype(WIDE)),
            0.0,
        )

    def start_of(k):
        return pl.multiple_of(near.member(k) * rows, rows)

    wing = KEY // 2
    along = [along_seg[:, pl.ds(start_of(k), rows)] for k in range(members)]

    def turn_back(target, k, h, grad, scale):
        at = pl.ds(pl.multiple_of(k * rows, rows), rows)
        cosine, sine = cos_ref[at, :], sin_ref[at, :]
        first, second = grad[:, :wing], grad[:, wing:]
        target[k, :, h * KEY : h * KEY + wing] = (
            (first * cosine + second * sine) * scale
        ).astype(LOW)
        target[k, :, h * KEY + wing : (h + 1) * KEY] = (
            (second * cosine - first * sine) * scale
        ).astype(LOW)

    def early_side(m, carry):
        early = start_of(m)
        early_segment = down_seg[pl.ds(early, rows), :]
        value_grads = []
        for h in range(heads):
            head = slice(h * KEY, (h + 1) * KEY)
            masked = jnp.where(inside(h), values[m].astype(WIDE), 0.0).astype(LOW)
            value_grad = jnp.zeros((rows, value_columns), WIDE)
            key_grad = jnp.zeros((rows, KEY), WIDE)
            for n in range(members):
                late = start_of(n)
                late_segment = along[n]
                mask = decay(h, late, early, late_segment, early_segment, True)
                score = (dot_across(keys[m, :, head], query[n, :, head]) * mask).astype(LOW)
                raw = (dot_across(masked, retained_low[n]) * mask).astype(LOW)
                value_grad += jnp.dot(score, retained_low[n], preferred_element_type=WIDE)
                key_grad += jnp.dot(raw, query[n, :, head], preferred_element_type=WIDE)
            value_grads.append(value_grad)
            turn_back(key_low, m, h, key_grad, 1.0)
        value_low[m] = by_head(value_grads).astype(LOW)
        return carry

    lax.fori_loop(0, members, early_side, 0)
    scatter.far(2, normed_turned, value_low)
    scatter.far(4, normed_turned, key_low)
    scatter.near(0, turned, mixed)

    def late_side(n, carry):
        late = start_of(n)
        late_segment = down_seg[pl.ds(late, rows), :]
        for h in range(heads):
            head = slice(h * KEY, (h + 1) * KEY)
            masked = jnp.where(inside(h), retained_low[n].astype(WIDE), 0.0).astype(LOW)
            query_grad = jnp.zeros((rows, KEY), WIDE)
            for m in range(members):
                early = start_of(m)
                early_segment = along[m]
                mask = decay(h, late, early, late_segment, early_segment, False)
                raw = (dot_across(masked, values[m]) * mask).astype(LOW)
                query_grad += jnp.dot(raw, keys[m, :, head], preferred_element_type=WIDE)
            turn_back(query_low, n, h, query_grad, KEY ** (-0.5))
        return carry

    lax.fori_loop(0, members, late_side, 0)
    scatter.far(3, normed_turned, query_low)
    scatter.near(1, normed_turned, gate_low)
    for copy in (gate_copy, value_copy, query_copy, key_copy, grad_copy):
        copy.wait()

    def back(k, put):
        for p in range(parts):
            columns = slice(p * slice_width, (p + 1) * slice_width)
            put(
                columns,
                dot_across(gate_low[k], wide_one[p])
                + dot_across(value_low[k], wide_two[p])
                + dot_across(query_low[k], short_one[p])
                + dot_across(key_low[k], short_two[p]),
            )

    def put_low(slot):
        def put(columns, value):
            held[slot, :, columns] = value.astype(LOW)

        return put

    def put_sum(columns, value):
        base[:, columns] = value

    back(3, put_low(0))
    near.start(0, held.at[0], got.at[0], 1)
    back(2, put_sum)
    near.wait(0)
    near.sent(0)
    held[0] = (base[...] + got[0].astype(WIDE)).astype(LOW)
    near.start(1, held.at[0], got.at[1], 2)
    back(1, put_low(1))
    near.start(2, held.at[1], got.at[2], 1)
    back(0, put_sum)
    scatter.near(2, normed_turned, value_low)
    near.wait(2)
    base[...] += got[2].astype(WIDE)
    near.wait(1)
    normed_grad = base[...] + got[1].astype(WIDE)
    base[...] = normed_grad
    resid = hidden_ref[...].astype(WIDE)
    scale = lax.rsqrt(jnp.mean(resid * resid, axis=-1, keepdims=True) + 1e-06)
    dot = jnp.zeros((rows, 1), WIDE)
    for p in range(parts):
        columns = slice(p * slice_width, (p + 1) * slice_width)
        product = base[:, columns] * (hidden_ref[:, columns].astype(WIDE) * scale)
        row = lax.broadcasted_iota(jnp.int32, (8, slice_width), 0)
        pieces[p] = jnp.where(
            row == 0, jnp.sum(product, axis=0, keepdims=True), gain_part[:, columns]
        )
        dot += jnp.sum(product * gain_all[p][0:1], axis=-1, keepdims=True)
    dot = dot * (1.0 / width)
    gains = []
    for k in range(1, parts):
        other = lax.rem(me + k, parts)
        place = lax.rem(other, 2) * lines + other // 2
        copy = remote(
            pieces.at[place], piece_got.at[k], gain_send.at[k], gain_recv.at[k], others[k - 1]
        )
        copy.start()
        gains.append(copy)
    for p in range(parts):
        columns = slice(p * slice_width, (p + 1) * slice_width)
        block = hidden_ref[:, columns].astype(WIDE) * scale
        in_grad_out[:, columns] += scale * (
            base[:, columns] * gain_all[p][0:1] - block * dot
        )
    value = pieces[here]
    for k in range(1, parts):
        gains[k - 1].wait_recv()
        value = value + piece_got[k]
    total[...] = value
    for k in range(1, members):
        near.start(2 + k, total, total_got.at[k], k)
    scatter.near(4, normed_turned, key_low)
    scatter.near(3, normed_turned, query_low)
    for w in (0, 1, 2, 4, 3):
        scatter.finish(w)
    for k in range(1, members):
        near.wait(2 + k)
        value = value + total_got[k]
    gain_out[...] = value
    for tag in range(1, 2 + members):
        near.sent(tag)
    for copy in gains:
        copy.wait_send()


def retention_backward(inside, streamed, weights, lines, members, slice_width):
    parts = 2 * lines
    rows, width = inside[10].shape
    blocks = (members, rows)
    wide, short = weights[0].shape[2], weights[3].shape[2]
    widths = [wide, wide, wide, short, short]
    pieces = [(lines, slice_width, columns) for columns in widths]
    outs = [(piece, LOW) for piece in pieces]
    outs += [((rows, width), WIDE), ((8, slice_width), WIDE)]
    outs += [(piece, LOW) for piece in pieces]
    return pl.pallas_call(
        functools.partial(retention_kernel, lines, members),
        out_shape=[jax.ShapeDtypeStruct(shape, dtype) for shape, dtype in outs],
        in_specs=[INSIDE] * 13 + [ANY] * 9,
        out_specs=[ANY] * 5 + [INSIDE] * 2 + [ANY] * 5,
        scratch_shapes=[
            pltpu.VMEM((width, rows * members), LOW),
            pltpu.VMEM(weights[0].shape, LOW),
            pltpu.VMEM(weights[0].shape, LOW),
            pltpu.VMEM(weights[3].shape, LOW),
            pltpu.VMEM(weights[3].shape, LOW),
            pltpu.VMEM(blocks + (wide,), LOW),
            pltpu.VMEM(blocks + (wide,), LOW),
            pltpu.VMEM(blocks + (wide,), LOW),
            pltpu.VMEM(blocks + (short,), LOW),
            pltpu.VMEM(blocks + (short,), LOW),
        ]
        + [pltpu.VMEM(piece, LOW) for piece in pieces]
        + [
            pltpu.VMEM((slice_width, wide), LOW),
            pltpu.VMEM((slice_width, short), LOW),
            pltpu.VMEM((2, rows, width), LOW),
            pltpu.VMEM((3, rows, width), LOW),
            pltpu.VMEM((rows, width), WIDE),
            pltpu.VMEM((rows, wide), WIDE),
            pltpu.VMEM((rows, wide), WIDE),
            pltpu.VMEM((parts, 8, slice_width), WIDE),
            pltpu.VMEM((parts, 8, slice_width), WIDE),
            pltpu.VMEM((8, slice_width), WIDE),
            pltpu.VMEM((members, 8, slice_width), WIDE),
            pltpu.SemaphoreType.DMA((5, lines)),
            pltpu.SemaphoreType.DMA((5, lines)),
            pltpu.SemaphoreType.DMA((5, lines)),
            pltpu.SemaphoreType.DMA((5, lines)),
            pltpu.SemaphoreType.DMA((6,)),
            pltpu.SemaphoreType.DMA((6,)),
            pltpu.SemaphoreType.DMA((parts,)),
            pltpu.SemaphoreType.DMA((parts,)),
            pltpu.SemaphoreType.DMA((9,)),
        ],
        compiler_params=pltpu.CompilerParams(
            collective_id=2, has_side_effects=True, vmem_limit_bytes=ROOM
        ),
        cost_estimate=pl.CostEstimate(flops=10**11, bytes_accessed=10**9, transcendentals=0),
        name="retention_backward",
    )(*inside, *streamed, *weights)[:7]


def on_device(
    hidden_in,
    out_grad,
    segment_ids,
    norm1_gain,
    w_query,
    w_key,
    w_value,
    w_gate,
    w_out,
    norm2_gain,
    w_mlp_gate,
    w_mlp_up,
    w_mlp_down,
):
    _, rows, width = hidden_in.shape
    parts = lax.axis_size("dp")
    lines = parts // 2
    slice_width = width // parts
    own = lax.axis_index("tensor")
    members = lax.axis_size("tensor")
    order = list(range(0, parts, 2)) + list(range(1, parts, 2))

    def to_places(value):
        blocks = [value[:, k * slice_width : (k + 1) * slice_width] for k in order]
        return jnp.concatenate(blocks, axis=1)

    def from_places(value):
        blocks = [value[:, k * slice_width : (k + 1) * slice_width] for k in range(parts)]
        return jnp.concatenate([blocks[k // 2 + k % 2 * lines] for k in range(parts)], axis=1)

    heads_here = w_query.shape[1] // KEY
    resid_low = to_places(hidden_in.reshape(rows, width))
    grad_local = to_places(out_grad.reshape(rows, width))
    gain_rows = jnp.concatenate(
        [norm1_gain[None], norm2_gain[None], jnp.zeros((6, slice_width), LOW)]
    ).astype(WIDE)
    position = jnp.concatenate(
        [(own ^ k) * rows + jnp.arange(rows, dtype=jnp.int32) for k in range(members)]
    )
    cosine, sine = rotary_tables(position, KEY)
    head_numbers = (jnp.arange(heads_here, dtype=jnp.int32) + own * heads_here).astype(WIDE)
    rates = jnp.log1p(-jnp.exp2(-5.0 - head_numbers))
    rates = jnp.broadcast_to(rates[:, None], (heads_here, 128))
    outs = forward(
        resid_low,
        grad_local,
        gain_rows,
        cosine,
        sine,
        segment_ids,
        rates,
        [w_query, w_key, w_value, w_gate, w_out.T, w_mlp_gate, w_mlp_up, w_mlp_down.T],
        lines,
        members,
    )
    normed_turned, grad_full, gains = outs[:3]
    query_weight, key_weight, value_weight, gate_weight, out_weight = outs[3:8]
    query, keys, values, gate_pre, grad_turned = outs[11:16]
    retained, mixed, resid_mid, mid_turned, gate_hidden, up_hidden, hidden = outs[16:]
    down_grad, mlp_gate_grad, mlp_up_grad, mid_all, mid_grad, hidden_out, gain_part = feed_backward(
        grad_full,
        grad_turned,
        mid_turned,
        hidden,
        resid_mid,
        gains,
        outs[8:11],
        (gate_hidden, up_hidden),
        lines,
        members,
    )
    out_weight_grad, gate_grad, value_grad, query_grad, key_grad, in_grad, gain_total = (
        retention_backward(
            [
                mixed,
                normed_turned,
                query,
                keys,
                values,
                cosine,
                sine,
                segment_ids.T,
                segment_ids,
                rates,
                resid_low,
                gains,
                gain_part,
            ],
            [mid_grad, mid_all, retained, gate_pre],
            [out_weight, gate_weight, value_weight, query_weight, key_weight],
            lines,
            members,
            slice_width,
        )
    )
    def add_up(pieces):
        return jnp.sum(pieces.astype(WIDE), axis=0)

    return (
        from_places(hidden_out).reshape(hidden_in.shape),
        from_places(in_grad).reshape(hidden_in.shape),
        gain_total[0],
        add_up(query_grad),
        add_up(key_grad),
        add_up(value_grad),
        add_up(gate_grad),
        add_up(out_weight_grad).T,
        gain_total[1],
        add_up(mlp_gate_grad),
        add_up(mlp_up_grad),
        add_up(down_grad).T,
    )


def solution(mesh):
    return jax.shard_map(
        on_device,
        mesh=mesh,
        in_specs=(
            P("dp", "tensor", None),
            P("dp", "tensor", None),
            P("dp", None),
            P("dp"),
            P("dp", "tensor"),
            P("dp", "tensor"),
            P("dp", "tensor"),
            P("dp", "tensor"),
            P("tensor", "dp"),
            P("dp"),
            P("dp", "tensor"),
            P("dp", "tensor"),
            P("tensor", "dp"),
        ),
        out_specs=(
            P("dp", "tensor", None),
            P("dp", "tensor", None),
            P("dp"),
            P("dp", "tensor"),
            P("dp", "tensor"),
            P("dp", "tensor"),
            P("dp", "tensor"),
            P("tensor", "dp"),
            P("dp"),
            P("dp", "tensor"),
            P("dp", "tensor"),
            P("tensor", "dp"),
        ),
        check_vma=False,
    )
```

time: 2050 us -> 798 us (0.39)
  waiting for transfers between devices: 1670 us -> 0 us
  Pallas kernels: 0 us -> 741 us
  matrix products: 220 us -> 0 us
  blocking collectives: 75.9 us -> 0 us
  other arithmetic: 38.7 us -> 13.2 us
    reduce_scatter x12 -> x0, waiting for transfers between devices: 1120 us -> none  [the longest x1 133 us: on_device(): lax.psum_scatter(value_weight_grad, 'dp', scatter_dimension=0, tiled=True)]
    pallas_call x0 -> x3, Pallas kernels: none -> 741 us  [the longest x1 322 us: forward(): pl.pallas_call(functools.partial(forward_kernel, lines, members), out_sha...]
    all_gather x12 -> x0, waiting for transfers between devices: 550 us -> none  [the longest x1 61.3 us: on_device(): lax.all_gather(w_mlp_up, 'dp', axis=0, tiled=True)]
    dot_general x30 -> x0, matrix products: 220 us -> none  [the longest x8 68.4 us: multiply(): return jnp.dot(left, right, preferred_element_type=jnp.float32)]
    all_gather x2 -> x0, blocking collectives: 34.8 us -> none  [the longest x1 18 us: on_device(): lax.all_gather(norm1_gain, 'dp', axis=0, tiled=True)]
    unnamed x1 -> x0, blocking collectives: 34.3 us -> none
  transfers between devices with their start and end apart: 24 -> 0, of which waited for: 23 -> 0; matrix products, arithmetic and copies ran while one was open for 8% -> 0% of each run, Pallas kernels for 0% -> 0%
where the time goes in v3:
time: 798 us; the launch traced here: 787 us
  Pallas kernels  741 us (93%)
  local copies, waits for them, and re-layouts  31.5 us (4%)
  other arithmetic  13.2 us (2%)
    pallas_call x1, Pallas kernels, forward(): pl.pallas_call(functools.partial(forward_kernel, lines, members), out_sha...  322 us
    pallas_call x1, Pallas kernels, retention_backward(): pl.pallas_call(functools.partial(retention_kernel, lines, members), out_s...  234 us
    pallas_call x1, Pallas kernels, feed_backward(): pl.pallas_call(functools.partial(feed_kernel, lines, members), out_shape=...  185 us
    unnamed x72, local copies, waits for them, and re-layouts  26 us

profile of v3, /device:TPU:8, one launch (start us, length us, event | category | flops | bytes accessed | tf_op | source)
XLA Modules:
  0.0 787.1 jit_solution(4753072608608085704)
XLA Ops:
  0.6 0.0 copy-start.9
  0.7 0.0 copy-start.8
  0.7 0.0 copy-start.7
  0.7 0.6 broadcast_in_dim.20.refs_7_.refs_9_
  1.3 0.1 pad.6.clone
  1.4 0.7 broadcast_in_dim.8
  2.1 0.7 broadcast_in_dim.18
  2.8 0.7 maximum_convert_fusion.refs_2_
  3.4 0.0 copy-start.10
  3.4 2.0 copy.42.refs_10_
  5.5 0.0 copy-start.15
  5.5 2.0 copy.43.refs_11_
  7.5 0.0 copy-done.7
  7.5 1.0 copy.39
  8.5 0.0 copy-done.8
  8.5 1.0 copy.44.refs_13_
  9.4 0.0 copy-done.9
  9.4 1.0 copy.45.refs_14_
  10.4 0.0 copy-done.10
  10.4 1.0 copy.40
  11.4 0.0 copy-done.15
  11.4 1.0 copy.41.refs_5_.refs_7_
  12.4 3.0 multiply_sine_fusion
  15.5 0.0 copy-done.6
  15.7 0.0 copy-done.5
  15.9 0.0 copy-start.13
  15.9 1.0 copy-done.13
  16.9 1.0 copy-done.12
  17.8 321.9 %forward.1 = (bf16[2048,1024]{1,0:T(8,128)(2,1)}, bf16[4,256,2048]{2,1,0:T(8,128)(2,1)}, f32[8,8,256]{2,1,0:T(8,128)}, bf16[8,256,512]{2,1,0:T(8,128)(2,1)}, bf1...) custom-call(bf16[256,2048]{1,0:T(8,128)(2,1)} %copy-done.12, ...), custom_call_target="tpu_custom_call" | custom-call | flops 99999997952 | bytes 1000000000 | tf_op jit(solution)/shard_map/forward/pallas_call | solution.py:447
  339.7 185.0 %feed_backward.1 = (bf16[4,256,864]{2,1,0:T(8,128)(2,1)}, bf16[4,256,864]{2,1,0:T(8,128)(2,1)}, bf16[4,256,864]{2,1,0:T(8,128)(2,1)}, bf16[4,256,2048]{2,1,0:T(8...) custom-call(bf16[4,256,2048]{2,1,0:T(8,128)(2,1)} %get-tuple-element, ...), custom_call_target="tpu_custom_call" | custom-call | flops 99999997952 | bytes 1000000000 | tf_op jit(solution)/shard_map/feed_backward/pallas_call | solution.py:781
  524.7 234.1 %retention_backward.1 = (bf16[4,256,864]{2,1,0:T(8,128)(2,1)}, bf16[4,256,864]{2,1,0:T(8,128)(2,1)}, bf16[4,256,864]{2,1,0:T(8,128)(2,1)}, bf16[4,256,512]{2,1,0...) custom-call(bf16[4,256,864]{2,1,0:T(8,128)(2,1)} %get-tuple-element., ...), custom_call_target="tpu_custom_call" | custom-call | flops 99999997952 | bytes 1000000000 | tf_op jit(solution)/shard_map/retention_backward/pallas_call | solution.py:1100
  758.8 0.0 copy-start.4
  758.8 1.4 fusion
  760.2 2.2 convert_reduce_fusion.7
  762.4 2.2 convert_reduce_fusion.6
  764.7 0.0 copy-done.4
  764.7 0.3 convert_reduce_fusion.5
  764.9 1.2 copy.47
  766.1 0.0 copy-done.3
  766.2 0.3 convert_reduce_fusion.4
  766.4 1.2 copy.48
  767.6 2.0 convert_reduce_fusion.3
  769.6 1.2 copy.49
  770.8 0.0 copy-done.2
  770.8 0.3 convert_reduce_fusion.2
  771.1 1.2 copy.50
  772.3 2.0 convert_reduce_fusion.1
  774.3 1.2 copy.51
  775.5 0.0 copy-done.1
  775.5 0.3 convert_reduce_fusion
  775.8 0.0 copy-start
  775.8 1.2 copy.52
  777.0 0.9 slice_dynamic-update-slice_fusion.31
  777.9 0.9 slice_dynamic-update-slice_fusion.30
  778.8 0.9 slice_dynamic-update-slice_fusion.29
  779.8 0.9 slice_dynamic-update-slice_fusion.28
  780.7 0.9 slice_dynamic-update-slice_fusion.27
  781.6 0.9 slice_dynamic-update-slice_fusion.26
  782.5 0.9 slice_dynamic-update-slice_fusion.25
  783.4 0.9 slice_dynamic-update-slice_fusion.24
  784.4 0.0 copy-start.14
  784.4 0.0 copy-done
  784.6 0.7 copy-done.14
  785.3 1.3 copy-done.11
  (36 shorter events, 0.5 us)
Async XLA Ops:
  0.6 8.8 %copy-start.9 = (bf16[256,864]{0,1:T(8,128)(2,1)S(1)}, bf16[256,864]{0,1:T(8,128)(2,1)}, u32[]{:S(2)}) copy-start(bf16[256,864]{0,1:T(8,128)(2,1)} %param.24) | copy-start | bytes 1327108
  0.7 7.8 copy-start.8
  0.7 6.8 copy-start.7
  3.4 7.0 copy-start.10
  5.5 5.9 copy-start.15
  8.5 7.0 copy-start.6
  10.4 5.2 copy-start.5
  15.9 1.0 copy-start.13
  16.9 1.0 copy-start.12
  758.8 5.9 copy-start.4
  764.7 1.5 copy-start.3
  767.6 3.2 copy-start.2
  772.3 3.2 copy-start.1
  775.8 8.6 %copy-start = (f32[256,2048]{1,0:T(8,128)S(1)}, f32[256,2048]{1,0:T(8,128)}, u32[]{:S(2)}) copy-start(f32[256,2048]{1,0:T(8,128)} %get-tuple-element.76) | copy-start | bytes 6291460
  784.4 1.0 copy-start.14
  785.3 1.3 copy-start.11

commit v4 on v3

--- a/solution.py
+++ b/solution.py
@@ -95,20 +95,54 @@
         copy.start()
         near[tag] = copy
 
-    steps = {}
     across = {}
     ours = {}
 
+    inner = lines == 4
+
+    def line_copy(w, step):
+        return remote(
+            shards[w],
+            wholes[w].at[here],
+            line_send.at[w, step],
+            line_recv.at[w, step],
+            {"dp": 2 * lax.rem(line + step, lines) + side},
+        )
+
+    def relay_copy(w):
+        place = side * lines + 3 * (2 - line)
+        return remote(
+            wholes[w].at[place],
+            wholes[w].at[place],
+            line_send.at[w, 0],
+            line_recv.at[w, 2 * line - 1],
+            {"dp": 6 * (line - 1) + side},
+        )
+
+    def side_copy(w, step):
+        place = side * lines + lax.rem(line + lines - step, lines)
+        return remote(
+            wholes[w].at[place],
+            wholes[w].at[place],
+            side_send.at[w, step],
+            side_recv.at[w, step],
+            opposite,
+        )
+
+    def on_line(w, step, act):
+        if inner and step != 2:
+
+            @pl.when(line != (3 if step == 1 else 0))
+            def _():
+                act(line_copy(w, step))
+        else:
+            act(line_copy(w, step))
+
+    sends = [2, 1, 3] if inner else list(range(1, lines))
+
     def start_lines(w):
-        for step in range(1, lines):
-            steps[w, step] = remote(
-                shards[w],
-                wholes[w].at[here],
-                line_send.at[w, step],
-                line_recv.at[w, step],
-                {"dp": 2 * lax.rem(line + step, lines) + side},
-            )
-            steps[w, step].start()
+        for step in sends:
+            on_line(w, step, lambda copy: copy.start())
         across[w, 0] = remote(
             shards[w], wholes[w].at[here], side_send.at[w, 0], side_recv.at[w, 0], opposite
         )
@@ -116,21 +150,24 @@
         ours[w] = keep(shards[w], wholes[w].at[here])
 
     def pass_on(w, third):
-        for step in range(1 + third * (lines - 1) // 3, 1 + (third + 1) * (lines - 1) // 3):
-            steps[w, step].wait_recv()
-            place = side * lines + lax.rem(line + lines - step, lines)
-            across[w, step] = remote(
-                wholes[w].at[place],
-                wholes[w].at[place],
-                side_send.at[w, step],
-                side_recv.at[w, step],
-                opposite,
-            )
-            across[w, step].start()
+        for at in range(third * (lines - 1) // 3, (third + 1) * (lines - 1) // 3):
+            step = at + 1
+            if inner:
+                late = 3 - 2 * ((3 - line) // 3)
+                step = [2, 4 - late, late][at]
+            line_copy(w, step).wait_recv()
+            if inner and at == 0:
+
+                @pl.when((line == 1) | (line == 2))
+                def _():
+                    relay_copy(w).start()
+
+            side_copy(w, step).start()
 
     def complete(w):
-        for step in range(lines):
-            across[w, step].wait_recv()
+        across[w, 0].wait_recv()
+        for step in range(1, lines):
+            side_copy(w, step).wait_recv()
         finish(ours[w])
 
     def load(w, target, sem):
@@ -400,10 +437,16 @@
     keep(hidden, hidden_out)
     complete(7)
     for w in range(WEIGHTS):
-        for step in range(1, lines):
-            steps[w, step].wait_send()
-        for step in range(lines):
-            across[w, step].wait_send()
+        for step in sends:
+            on_line(w, step, lambda copy: copy.wait_send())
+            side_copy(w, step).wait_send()
+        across[w, 0].wait_send()
+        if inner:
+
+            @pl.when((line == 1) | (line == 2))
+            def _():
+                relay_copy(w).wait_send()
+
     for copy in gains:
         copy.wait_send()
     for copy in near.values():
@@ -538,9 +581,23 @@
             preferred_element_type=WIDE,
         )
 
+
+    def extra_copy(self, w, step):
+        place = lax.rem(self.line + step, self.lines)
+        return remote(
+            self.held[w].at[place],
+            self.far_got[w].at[self.lines],
+            self.line_send.at[w, step],
+            self.line_recv.at[w, 0],
+            {"dp": 2 * (2 if step == 1 else 1) + self.side},
+        )
+
     def far(self, w, left, right):
-        def body(step, carry):
-            place = lax.rem(self.line + step + 1, self.lines)
+        def body(at, carry):
+            step = 1 + at
+            if self.lines == 4:
+                step = 1 + 2 * at - 3 * (at // 2)
+            place = lax.rem(self.line + step, self.lines)
             other = (1 - self.side) * self.lines + place
             self.held[w][place] = self.product(left, right, other).astype(LOW)
             self.far_copy(w, place).start()
@@ -548,24 +605,64 @@
 
         lax.fori_loop(0, self.lines, body, 0)
 
-    def near(self, w, left, right):
-        def body(step, carry):
-            place = lax.rem(self.line + step, self.lines)
+    def near(self, w, left, right, quarter):
+        def add(place):
             part = self.product(left, right, self.side * self.lines + place)
             self.far_copy(w, place).wait_recv()
             total = part + self.fetch(self.far_got[w].at[place])
             self.far_copy(w, place).wait_send()
-            self.held[w][place] = total.astype(LOW)
+            return total
+
+        def body(step, carry):
+            place = lax.rem(self.line + step, self.lines)
+            self.held[w][place] = add(place).astype(LOW)
             self.near_copy(w, step).start()
             return carry
 
-        lax.fori_loop(1, self.lines, body, 0)
-        part = self.product(left, right, self.side * self.lines + self.line)
-        self.far_copy(w, self.line).wait_recv()
-        total = part + self.fetch(self.far_got[w].at[self.line])
-        self.far_copy(w, self.line).wait_send()
-        self.held[w][self.line] = total.astype(LOW)
+        if self.lines != 4:
+            first, last = [1 + (quarter + k) * self.lines // 4 for k in range(2)]
+            lax.fori_loop(first, min(last, self.lines), body, 0)
+        elif quarter < 2:
+            step = 1 + 2 * quarter
+            end = 3 - 3 * quarter
+            place = lax.rem(self.line + step, self.lines)
+            self.held[w][place] = add(place).astype(LOW)
+
+            @pl.when(self.line == end)
+            def _():
+                self.extra_copy(w, step).start()
+
+            @pl.when(self.line != end)
+            def _():
+                self.near_copy(w, step).start()
+        elif quarter == 2:
+            place = lax.rem(self.line + 2, self.lines)
+            total = add(place)
+            self.held[w][place] = total.astype(LOW)
+
+            @pl.when((self.line == 1) | (self.line == 2))
+            def _():
+                self.extra_copy(w, 1).wait_recv()
+                self.held[w][place] = (
+                    self.held[w][place].astype(WIDE)
+                    + self.fetch(self.far_got[w].at[self.lines])
+                ).astype(LOW)
+
+            self.near_copy(w, 2).start()
+        if quarter < 3:
+            return
+        self.held[w][self.line] = add(self.line).astype(LOW)
         self.own_copy(w).start()
+        if self.lines == 4:
+
+            @pl.when((self.line == 0) | (self.line == 3))
+            def _():
+                spare = self.spare[self.held[w].shape[2]]
+                spare[...] = jnp.zeros(spare.shape, LOW)
+                slot = 1 + 2 * (self.line // 3)
+                copy = pltpu.make_async_copy(spare, self.near_got[w].at[slot], self.home)
+                copy.start()
+                copy.wait()
 
     def own_copy(self, w):
         return pltpu.make_async_copy(
@@ -573,11 +670,25 @@
         )
 
     def finish(self, w):
-        def body(step, carry):
-            self.near_copy(w, step).wait()
-            return carry
-
-        lax.fori_loop(1, self.lines, body, 0)
+        if self.lines != 4:
+
+            def body(step, carry):
+                self.near_copy(w, step).wait()
+                return carry
+
+            lax.fori_loop(1, self.lines, body, 0)
+        else:
+            for step in range(1, 4):
+                copy = self.near_copy(w, step)
+                copy.wait_send()
+                if step == 2:
+                    copy.wait_recv()
+                else:
+
+                    @pl.when(self.line != (0 if step == 1 else 3))
+                    def _():
+                        copy.wait_recv()
+
         self.own_copy(w).wait()
 
 
@@ -611,17 +722,24 @@
 
 
 def feed_kernel(lines, members, *refs):
-    grad_ref, grad_turned, mid_turned, hidden, resid_ref, gain_all = refs[:6]
-    gate_weight, up_weight, down_weight, gate_hidden, up_hidden = refs[6:11]
+    grad_turned, hidden, gain_all = refs[:3]
+    later = refs[3:9]
+    gate_hidden, up_hidden = refs[9:11]
     near_got, mid_all, mid_grad_out, hidden_out, gain_out = refs[11:14], *refs[14:18]
     far_got = refs[18:21]
     gate_low, up_low, pre, up = refs[21:25]
     scatter_held = refs[25:28]
     spare, held, got, last, base, mid = refs[28:34]
     sems = refs[34:38]
-    near_send, near_recv, home = refs[38:]
+    near_send, near_recv, home = refs[38:41]
+    loaded = refs[41:]
+    grad_ref, mid_turned, resid_ref, gate_weight, up_weight, down_weight = loaded
     parts = 2 * lines
     rows, width = resid_ref.shape
+    loads = []
+    for k, order in enumerate((5, 0, 1, 3, 4, 2)):
+        loads.append(pltpu.make_async_copy(later[order], loaded[order], home.at[4 + k]))
+        loads[k].start()
     slice_width = width // parts
     scatter = Scatter(
         lines,
@@ -656,7 +774,12 @@
         up_low[k] = (grad * (value * ramp)).astype(LOW)
         return carry
 
-    lax.fori_loop(0, members, pull, 0)
+    for load in loads:
+        load.wait()
+    lax.fori_loop(0, members // 2, pull, 0)
+    scatter.near(0, grad_turned, hidden, 0)
+    lax.fori_loop(members // 2, members, pull, 0)
+    scatter.near(0, grad_turned, hidden, 1)
     scatter.far(1, mid_turned, gate_low)
 
     def back(k, put):
@@ -678,6 +801,7 @@
 
     back(3, put_low(0))
     near.start(0, held.at[0], got.at[0], 1)
+    scatter.near(0, grad_turned, hidden, 2)
     back(2, put_sum)
     near.wait(0)
     near.sent(0)
@@ -685,10 +809,13 @@
     near.start(1, held.at[0], got.at[1], 2)
     back(1, put_low(1))
     near.start(2, held.at[1], got.at[2], 1)
+    scatter.near(0, grad_turned, hidden, 3)
     back(0, put_sum)
     scatter.far(2, mid_turned, up_low)
+    scatter.near(1, mid_turned, gate_low, 0)
     near.wait(2)
     base[...] += got[2].astype(WIDE)
+    scatter.near(1, mid_turned, gate_low, 1)
     near.wait(1)
     normed_grad = base[...] + got[1].astype(WIDE)
     resid = resid_ref[...]
@@ -718,10 +845,8 @@
     near.start(4, mid, mid_all.at[1], 1)
     own = pltpu.make_async_copy(mid, mid_all.at[0], home.at[3])
     own.start()
-    scatter.near(0, grad_turned, hidden)
-    near.wait(3)
-    near.start(5, mid_all.at[2], mid_all.at[3], 1)
-    scatter.near(1, mid_turned, gate_low)
+    scatter.near(1, mid_turned, gate_low, 2)
+    scatter.near(1, mid_turned, gate_low, 3)
 
     def down(k, put):
         for p in range(parts):
@@ -734,14 +859,19 @@
     mid_grad_copy.wait()
     near.start(6, held.at[0], last.at[0], 1)
     down(2, put_sum)
+    scatter.near(2, mid_turned, up_low, 0)
+    near.wait(3)
+    near.start(5, mid_all.at[2], mid_all.at[3], 1)
     near.wait(6)
     near.sent(6)
     held[0] = (base[...] + last[0].astype(WIDE)).astype(LOW)
     near.start(7, held.at[0], last.at[1], 2)
     down(1, put_low(1))
     near.start(8, held.at[1], last.at[2], 1)
+    scatter.near(2, mid_turned, up_low, 1)
     down(0, put_sum)
-    scatter.near(2, mid_turned, up_low)
+    scatter.near(2, mid_turned, up_low, 2)
+    scatter.near(2, mid_turned, up_low, 3)
     near.wait(8)
     near.wait(7)
     own.wait()
@@ -770,6 +900,7 @@
     slice_width = width // parts
     blocks = (members, rows)
     piece = (lines, slice_width, columns)
+    later = [grad, mid_turned, resid, *weights]
     outs = [(piece, LOW)] * 3
     outs += [
         (blocks + (width,), LOW),
@@ -777,11 +908,11 @@
         ((rows, width), LOW),
         ((8, width), WIDE),
     ]
-    outs += [(piece, LOW)] * 3
+    outs += [((lines + 1,) + piece[1:], LOW)] * 3
     return pl.pallas_call(
         functools.partial(feed_kernel, lines, members),
         out_shape=[jax.ShapeDtypeStruct(shape, dtype) for shape, dtype in outs],
-        in_specs=[INSIDE] * 9 + [ANY] * 2,
+        in_specs=[INSIDE] * 3 + [ANY] * 8,
         out_specs=[ANY] * 6 + [INSIDE] + [ANY] * 3,
         scratch_shapes=[
             pltpu.VMEM(blocks + (columns,), LOW),
@@ -803,18 +934,19 @@
             pltpu.SemaphoreType.DMA((3, lines)),
             pltpu.SemaphoreType.DMA((9,)),
             pltpu.SemaphoreType.DMA((9,)),
-            pltpu.SemaphoreType.DMA((4,)),
-        ],
+            pltpu.SemaphoreType.DMA((10,)),
+        ]
+        + [pltpu.VMEM(value.shape, value.dtype) for value in later],
         compiler_params=pltpu.CompilerParams(
             collective_id=1, has_side_effects=True, vmem_limit_bytes=ROOM
         ),
         cost_estimate=pl.CostEstimate(flops=10**11, bytes_accessed=10**9, transcendentals=0),
         name="feed_backward",
-    )(grad, grad_turned, mid_turned, hidden, resid, gains, *weights, *pres)[:7]
+    )(grad_turned, hidden, gains, *later, *pres)[:7]
 
 
 def retention_kernel(lines, members, *refs):
-    mixed, normed_turned, query, keys, values = refs[:5]
+    later = refs[:5]
     cos_ref, sin_ref, down_seg, along_seg, rate_ref = refs[5:10]
     hidden_ref, gain_all, gain_part = refs[10:13]
     mid_grad_ref, mid_all, retained_all, gate_all = refs[13:17]
@@ -822,12 +954,15 @@
     near_got, in_grad_out, gain_out = refs[22:27], refs[27], refs[28]
     far_got = refs[29:34]
     turned, wide_one, wide_two, short_one, short_two = refs[34:39]
-    gate_low, retained_low, value_low, query_low, key_low = refs[39:44]
-    scatter_held = refs[44:49]
-    spare_wide, spare_short, held, got, base, retained, gate = refs[49:56]
-    pieces, piece_got, total, total_got = refs[56:60]
-    sems = refs[60:64]
-    near_send, near_recv, gain_send, gain_recv, home = refs[64:]
+    gate_low, retained_low, query_low, key_low = refs[39:43]
+    scatter_held = refs[43:48]
+    spare_wide, spare_short, held, got, base, retained, gate = refs[48:55]
+    pieces, piece_got, total, total_got = refs[55:59]
+    sems = refs[59:63]
+    near_send, near_recv, gain_send, gain_recv, home = refs[63:68]
+    loaded = refs[68:]
+    mixed, normed_turned, query, keys, values = loaded
+    value_low = mixed
     parts = 2 * lines
     rows, width = hidden_ref.shape
     slice_width = width // parts
@@ -858,6 +993,7 @@
     query_copy = fetch(weights[3], short_one, 3)
     key_copy = fetch(weights[4], short_two, 4)
     grad_copy = fetch(mid_grad_ref, in_grad_out, 7)
+    loads = [fetch(later[k], loaded[k], 9 + k) for k in range(5)]
 
     def turn_over(k, carry):
         fetch(mid_all.at[k], held.at[0], 8).wait()
@@ -868,8 +1004,11 @@
         return carry
 
     lax.fori_loop(0, members, turn_over, 0)
+    loads[0].wait()
     scatter.far(0, turned, mixed)
     out_copy.wait()
+    for load in loads[1:]:
+        load.wait()
 
     column = lax.broadcasted_iota(jnp.int32, (rows, value_columns), 1)
 
@@ -916,7 +1055,10 @@
         ).astype(LOW)
         return carry
 
-    lax.fori_loop(0, members, unmix, 0)
+    lax.fori_loop(0, members // 2, unmix, 0)
+    scatter.near(0, turned, mixed, 0)
+    lax.fori_loop(members // 2, members, unmix, 0)
+    scatter.near(0, turned, mixed, 1)
     scatter.far(1, normed_turned, gate_low)
     gate_copy = fetch(weights[1], wide_one, 1)
 
@@ -976,10 +1118,15 @@
         value_low[m] = by_head(value_grads).astype(LOW)
         return carry
 
-    lax.fori_loop(0, members, early_side, 0)
+    scatter.near(0, turned, mixed, 2)
+    scatter.near(0, turned, mixed, 3)
+    early_side(0, 0)
+    for m in range(1, members):
+        early_side(m, 0)
+        scatter.near(1, normed_turned, gate_low, m - 1)
     scatter.far(2, normed_turned, value_low)
     scatter.far(4, normed_turned, key_low)
-    scatter.near(0, turned, mixed)
+    scatter.near(1, normed_turned, gate_low, 3)
 
     def late_side(n, carry):
         late = start_of(n)
@@ -997,9 +1144,11 @@
             turn_back(query_low, n, h, query_grad, KEY ** (-0.5))
         return carry
 
-    lax.fori_loop(0, members, late_side, 0)
+    lax.fori_loop(0, members // 2, late_side, 0)
+    scatter.near(2, normed_turned, value_low, 0)
+    lax.fori_loop(members // 2, members, late_side, 0)
+    scatter.near(2, normed_turned, value_low, 1)
     scatter.far(3, normed_turned, query_low)
-    scatter.near(1, normed_turned, gate_low)
     for copy in (gate_copy, value_copy, query_copy, key_copy, grad_copy):
         copy.wait()
 
@@ -1026,14 +1175,17 @@
     back(3, put_low(0))
     near.start(0, held.at[0], got.at[0], 1)
     back(2, put_sum)
+    scatter.near(2, normed_turned, value_low, 2)
     near.wait(0)
     near.sent(0)
     held[0] = (base[...] + got[0].astype(WIDE)).astype(LOW)
     near.start(1, held.at[0], got.at[1], 2)
     back(1, put_low(1))
     near.start(2, held.at[1], got.at[2], 1)
+    scatter.near(2, normed_turned, value_low, 3)
     back(0, put_sum)
-    scatter.near(2, normed_turned, value_low)
+    for quarter in range(4):
+        scatter.near(4, normed_turned, key_low, quarter)
     near.wait(2)
     base[...] += got[2].astype(WIDE)
     near.wait(1)
@@ -1073,8 +1225,8 @@
     total[...] = value
     for k in range(1, members):
         near.start(2 + k, total, total_got.at[k], k)
-    scatter.near(4, normed_turned, key_low)
-    scatter.near(3, normed_turned, query_low)
+    for quarter in range(4):
+        scatter.near(3, normed_turned, query_low, quarter)
     for w in (0, 1, 2, 4, 3):
         scatter.finish(w)
     for k in range(1, members):
@@ -1096,11 +1248,11 @@
     pieces = [(lines, slice_width, columns) for columns in widths]
     outs = [(piece, LOW) for piece in pieces]
     outs += [((rows, width), WIDE), ((8, slice_width), WIDE)]
-    outs += [(piece, LOW) for piece in pieces]
+    outs += [((lines + 1,) + piece[1:], LOW) for piece in pieces]
     return pl.pallas_call(
         functools.partial(retention_kernel, lines, members),
         out_shape=[jax.ShapeDtypeStruct(shape, dtype) for shape, dtype in outs],
-        in_specs=[INSIDE] * 13 + [ANY] * 9,
+        in_specs=[ANY] * 5 + [INSIDE] * 8 + [ANY] * 9,
         out_specs=[ANY] * 5 + [INSIDE] * 2 + [ANY] * 5,
         scratch_shapes=[
             pltpu.VMEM((width, rows * members), LOW),
@@ -1108,7 +1260,6 @@
             pltpu.VMEM(weights[0].shape, LOW),
             pltpu.VMEM(weights[3].shape, LOW),
             pltpu.VMEM(weights[3].shape, LOW),
-            pltpu.VMEM(blocks + (wide,), LOW),
             pltpu.VMEM(blocks + (wide,), LOW),
             pltpu.VMEM(blocks + (wide,), LOW),
             pltpu.VMEM(blocks + (short,), LOW),
@@ -1135,8 +1286,9 @@
             pltpu.SemaphoreType.DMA((6,)),
             pltpu.SemaphoreType.DMA((parts,)),
             pltpu.SemaphoreType.DMA((parts,)),
-            pltpu.SemaphoreType.DMA((9,)),
-        ],
+            pltpu.SemaphoreType.DMA((14,)),
+        ]
+        + [pltpu.VMEM(value.shape, value.dtype) for value in inside[:5]],
         compiler_params=pltpu.CompilerParams(
             collective_id=2, has_side_effects=True, vmem_limit_bytes=ROOM
         ),

time: 798 us -> 716 us (0.90)
  Pallas kernels: 741 us -> 658 us
    pallas_call x1, Pallas kernels: 185 us -> 137 us  [feed_backward(): pl.pallas_call(functools.partial(feed_kernel, lines, members), out_shape=...]
    pallas_call x1, Pallas kernels: 234 us -> 213 us  [retention_backward(): pl.pallas_call(functools.partial(retention_kernel, lines, members), out_s...]
    pallas_call x1, Pallas kernels: 322 us -> 307 us  [forward(): pl.pallas_call(functools.partial(forward_kernel, lines, members), out_sha...]
where the time goes in v4:
time: 716 us; the launch traced here: 704 us
  Pallas kernels  658 us (92%)
  local copies, waits for them, and re-layouts  31.5 us (4%)
  other arithmetic  13.2 us (2%)
    pallas_call x1, Pallas kernels, forward(): pl.pallas_call(functools.partial(forward_kernel, lines, members), out_sha...  307 us
    pallas_call x1, Pallas kernels, retention_backward(): pl.pallas_call(functools.partial(retention_kernel, lines, members), out_s...  213 us
    pallas_call x1, Pallas kernels, feed_backward(): pl.pallas_call(functools.partial(feed_kernel, lines, members), out_shape=...  137 us
    unnamed x72, local copies, waits for them, and re-layouts  26 us

profile of v4, /device:TPU:8, one launch (start us, length us, event | category | flops | bytes accessed | tf_op | source)
XLA Modules:
  0.0 704.0 jit_solution(4053096130369929503)
XLA Ops:
  0.6 0.0 copy-start.9
  0.7 0.0 copy-start.8
  0.7 0.0 copy-start.7
  0.7 0.6 broadcast_in_dim.20.refs_7_.refs_9_
  1.3 0.1 pad.6.clone
  1.4 0.7 broadcast_in_dim.8
  2.1 0.7 broadcast_in_dim.18
  2.8 0.7 maximum_convert_fusion.refs_2_
  3.4 0.0 copy-start.10
  3.4 2.0 copy.42.refs_10_
  5.5 0.0 copy-start.15
  5.5 2.0 copy.43.refs_11_
  7.5 0.0 copy-done.7
  7.5 1.0 copy.39
  8.5 0.0 copy-done.8
  8.5 1.0 copy.44.refs_13_
  9.4 0.0 copy-done.9
  9.4 1.0 copy.45.refs_14_
  10.4 0.0 copy-done.10
  10.4 1.0 copy.40
  11.4 0.0 copy-done.15
  11.4 1.0 copy.41.refs_5_.refs_7_
  12.4 3.0 multiply_sine_fusion
  15.5 0.0 copy-done.6
  15.6 0.0 copy-done.5
  15.9 0.0 copy-start.13
  15.9 1.0 copy-done.13
  16.9 1.0 copy-done.12
  17.8 307.3 %forward.1 = (bf16[2048,1024]{1,0:T(8,128)(2,1)}, bf16[4,256,2048]{2,1,0:T(8,128)(2,1)}, f32[8,8,256]{2,1,0:T(8,128)}, bf16[8,256,512]{2,1,0:T(8,128)(2,1)}, bf1...) custom-call(bf16[256,2048]{1,0:T(8,128)(2,1)} %copy-done.12, ...), custom_call_target="tpu_custom_call" | custom-call | flops 99999997952 | bytes 1000000000 | tf_op jit(solution)/shard_map/forward/pallas_call | solution.py:490
  325.1 137.1 %feed_backward.1 = (bf16[4,256,864]{2,1,0:T(8,128)(2,1)}, bf16[4,256,864]{2,1,0:T(8,128)(2,1)}, bf16[4,256,864]{2,1,0:T(8,128)(2,1)}, bf16[4,256,2048]{2,1,0:T(8...) custom-call(bf16[2048,1024]{1,0:T(8,128)(2,1)} %get-tuple-element.49, ...), custom_call_target="tpu_custom_call" | custom-call | flops 99999997952 | bytes 1000000000 | tf_op jit(solution)/shard_map/feed_backward/pallas_call | solution.py:912
  462.2 213.4 %retention_backward.1 = (bf16[4,256,864]{2,1,0:T(8,128)(2,1)}, bf16[4,256,864]{2,1,0:T(8,128)(2,1)}, bf16[4,256,864]{2,1,0:T(8,128)(2,1)}, bf16[4,256,512]{2,1,0...) custom-call(bf16[4,256,864]{2,1,0:T(8,128)(2,1)} %get-tuple-element., ...), custom_call_target="tpu_custom_call" | custom-call | flops 99999997952 | bytes 1000000000 | tf_op jit(solution)/shard_map/retention_backward/pallas_call | solution.py:1252
  675.7 0.0 copy-start.4
  675.7 1.4 fusion
  677.1 2.2 convert_reduce_fusion.7
  679.3 2.2 convert_reduce_fusion.6
  681.5 0.0 copy-done.4
  681.5 0.3 convert_reduce_fusion.5
  681.8 1.2 copy.47
  683.0 0.0 copy-done.3
  683.0 0.3 convert_reduce_fusion.4
  683.3 1.2 copy.48
  684.5 2.0 convert_reduce_fusion.3
  686.5 1.2 copy.49
  687.7 0.0 copy-done.2
  687.7 0.3 convert_reduce_fusion.2
  688.0 1.2 copy.50
  689.2 2.0 convert_reduce_fusion.1
  691.2 1.2 copy.51
  692.4 0.0 copy-done.1
  692.4 0.3 convert_reduce_fusion
  692.7 0.0 copy-start
  692.7 1.2 copy.52
  693.9 0.9 slice_dynamic-update-slice_fusion.31
  694.8 0.9 slice_dynamic-update-slice_fusion.30
  695.7 0.9 slice_dynamic-update-slice_fusion.29
  696.7 0.9 slice_dynamic-update-slice_fusion.28
  697.6 0.9 slice_dynamic-update-slice_fusion.27
  698.5 0.9 slice_dynamic-update-slice_fusion.26
  699.4 0.9 slice_dynamic-update-slice_fusion.25
  700.3 0.9 slice_dynamic-update-slice_fusion.24
  701.3 0.0 copy-start.14
  701.3 0.0 copy-done
  701.5 0.7 copy-done.14
  702.2 1.3 copy-done.11
  (36 shorter events, 0.5 us)
Async XLA Ops:
  0.6 8.8 %copy-start.9 = (bf16[256,864]{0,1:T(8,128)(2,1)S(1)}, bf16[256,864]{0,1:T(8,128)(2,1)}, u32[]{:S(2)}) copy-start(bf16[256,864]{0,1:T(8,128)(2,1)} %param.24) | copy-start | bytes 1327108
  0.7 7.8 %copy-start.8 = (bf16[256,864]{0,1:T(8,128)(2,1)S(1)}, bf16[256,864]{0,1:T(8,128)(2,1)}, u32[]{:S(2)}) copy-start(bf16[256,864]{0,1:T(8,128)(2,1)} %param.23) | copy-start | bytes 1327108
  0.7 6.8 copy-start.7
  3.4 7.0 copy-start.10
  5.5 5.9 copy-start.15
  8.5 7.0 copy-start.6
  10.4 5.2 copy-start.5
  15.9 1.0 copy-start.13
  16.9 1.0 copy-start.12
  675.7 5.9 copy-start.4
  681.5 1.5 copy-start.3
  684.5 3.2 copy-start.2
  689.2 3.2 copy-start.1
  692.7 8.6 %copy-start = (f32[256,2048]{1,0:T(8,128)S(1)}, f32[256,2048]{1,0:T(8,128)}, u32[]{:S(2)}) copy-start(f32[256,2048]{1,0:T(8,128)} %get-tuple-element.76) | copy-start | bytes 6291460
  701.3 1.0 copy-start.14
  702.2 1.3 copy-start.11

commit v5 on v4

--- a/solution.py
+++ b/solution.py
@@ -55,11 +55,11 @@
     query, keys, scores, values, retained, gate, mixed, hidden = refs[45:53]
     held, got, base = refs[53:56]
     line_send, line_recv, side_send, side_recv = refs[56:60]
-    near_send, near_recv, gain_send, gain_recv, home = refs[60:]
+    near_send, near_recv, gain_send, gain_recv, home, tail_send, tail_recv, gain_rows = refs[60:]
 
     parts = 2 * lines
     rows, width = hidden_ref.shape
-    slice_width = gain_ref.shape[1]
+    slice_width = gain_rows.shape[1]
     heads = rate_ref.shape[0]
     value_columns = values.shape[2]
     me = lax.axis_index("dp")
@@ -119,14 +119,28 @@
             {"dp": 6 * (line - 1) + side},
         )
 
+    tail = slice_width // 8 // 16 * 16
+    most = slice_width - tail
+
     def side_copy(w, step):
         place = side * lines + lax.rem(line + lines - step, lines)
         return remote(
-            wholes[w].at[place],
-            wholes[w].at[place],
+            wholes[w].at[place, pl.ds(0, most)],
+            wholes[w].at[place, pl.ds(0, most)],
             side_send.at[w, step],
             side_recv.at[w, step],
             opposite,
+        )
+
+    there = (1 - side) * lines + line
+
+    def tail_copy(w, step):
+        return remote(
+            wholes[w].at[there, pl.ds(most, tail)],
+            wholes[w].at[there, pl.ds(most, tail)],
+            tail_send.at[w, step],
+            tail_recv.at[w, step],
+            {"dp": 2 * lax.rem(line + step, lines) + side},
         )
 
     def on_line(w, step, act):
@@ -155,6 +169,10 @@
             if inner:
                 late = 3 - 2 * ((3 - line) // 3)
                 step = [2, 4 - late, late][at]
+            if tail and at == 0:
+                across[w, 0].wait_recv()
+                for hop in range(1, lines):
+                    tail_copy(w, hop).start()
             line_copy(w, step).wait_recv()
             if inner and at == 0:
 
@@ -165,9 +183,12 @@
             side_copy(w, step).start()
 
     def complete(w):
-        across[w, 0].wait_recv()
+        if not tail:
+            across[w, 0].wait_recv()
         for step in range(1, lines):
             side_copy(w, step).wait_recv()
+            if tail:
+                tail_copy(w, step).wait_recv()
         finish(ours[w])
 
     def load(w, target, sem):
@@ -177,26 +198,27 @@
 
     def stage(w, target, body):
         if w + 1 < WEIGHTS:
-            pass_on(w + 1, 0)
+            for third in range(3):
+                pass_on(w + 1, third)
+        if w + 3 < WEIGHTS:
+            start_lines(w + 3)
         complete(w)
         load(w, target, home.at[home.shape[0] - 1 - w])
-        lax.fori_loop(0, members // 2, body, 0)
-        if w + 1 < WEIGHTS:
-            pass_on(w + 1, 1)
-        lax.fori_loop(members // 2, members, body, 0)
-        if w + 1 < WEIGHTS:
-            pass_on(w + 1, 2)
-        if w + 3 < WEIGHTS:
-            start_lines(w + 3)
-
+        lax.fori_loop(0, members, body, 0)
+
+    gain_rows[...] = jnp.where(
+        lax.broadcasted_iota(jnp.int32, gain_rows.shape, 0) == 0,
+        gain_ref[0:1, :].astype(WIDE),
+        gain_ref[1:2, :].astype(WIDE),
+    )
     gains = []
     for k in range(1, parts):
         copy = remote(
-            gain_ref, gain_all.at[here], gain_send.at[k], gain_recv.at[k], others[k - 1]
+            gain_rows, gain_all.at[here], gain_send.at[k], gain_recv.at[k], others[k - 1]
         )
         copy.start()
         gains.append(copy)
-    gain_all[here] = gain_ref[...]
+    gain_all[here] = gain_rows[...]
     for w in range(3):
         start_lines(w)
 
@@ -440,6 +462,8 @@
         for step in sends:
             on_line(w, step, lambda copy: copy.wait_send())
             side_copy(w, step).wait_send()
+            if tail:
+                tail_copy(w, step).wait_send()
         across[w, 0].wait_send()
         if inner:
 
@@ -466,7 +490,7 @@
     outs = [
         (turned, LOW),
         (blocks + (width,), LOW),
-        ((parts,) + gains.shape, WIDE),
+        ((parts, 8, gains.shape[1]), WIDE),
     ]
     outs += [((parts,) + shard.shape, LOW) for shard in shards]
     outs += [
@@ -519,6 +543,9 @@
             pltpu.SemaphoreType.DMA((parts,)),
             pltpu.SemaphoreType.DMA((parts,)),
             pltpu.SemaphoreType.DMA((40,)),
+            pltpu.SemaphoreType.DMA((WEIGHTS, lines)),
+            pltpu.SemaphoreType.DMA((WEIGHTS, lines)),
+            pltpu.VMEM((8, gains.shape[1]), WIDE),
         ],
         compiler_params=pltpu.CompilerParams(
             collective_id=0, has_side_effects=True, vmem_limit_bytes=ROOM
@@ -530,11 +557,20 @@
     )(hidden, grad, gains, cosine, sine, segments.T, segments, rates, *shards)
 
 
+def tail_rows(rows, lines):
+    return rows // 8 // 16 * 16 if lines == 4 else 0
+
+
 class Scatter:
-    def __init__(self, lines, held, far_got, near_got, spare, sems):
+    def __init__(self, lines, held, far_got, near_got, tail_got, spare, tails, sems):
         self.lines = lines
         self.held, self.far_got, self.near_got, self.spare = held, far_got, near_got, spare
-        self.side_send, self.side_recv, self.line_send, self.line_recv, self.home = sems
+        self.tail_got, self.tails = tail_got, tails
+        self.side_send, self.side_recv, self.line_send, self.line_recv = sems[:4]
+        self.tail_send, self.tail_recv, self.home = sems[4:]
+        self.rows = held[0].shape[1]
+        self.tail = tail_rows(self.rows, lines)
+        self.most = self.rows - self.tail
         me = lax.axis_index("dp")
         self.line, self.side = me // 2, lax.rem(me, 2)
         self.opposite = {"dp": 2 * self.line + (1 - self.side)}
@@ -547,8 +583,8 @@
 
     def far_copy(self, w, place):
         return remote(
-            self.held[w].at[place],
-            self.far_got[w].at[place],
+            self.held[w].at[place, pl.ds(0, self.most)],
+            self.far_got[w].at[place, pl.ds(0, self.most)],
             self.side_send.at[w, place],
             self.side_recv.at[w, place],
             self.opposite,
@@ -565,11 +601,40 @@
         )
 
     def fetch(self, source):
-        spare = self.spare[source.shape[-1]]
+        rows, columns = source.shape
+        spare = self.spare[columns].at[pl.ds(0, rows)]
         copy = pltpu.make_async_copy(source, spare, self.home)
         copy.start()
         copy.wait()
         return spare[...].astype(WIDE)
+
+
+    def tail_copy(self, w, step):
+        place = lax.rem(self.line + step, self.lines)
+        return remote(
+            self.held[w].at[place, pl.ds(self.most, self.tail)],
+            self.tail_got[w].at[step],
+            self.tail_send.at[w, step],
+            self.tail_recv.at[w, step],
+            self.peer(step),
+        )
+
+    def tail_across(self, w):
+        return remote(
+            self.tails[w],
+            self.tail_got[w].at[0],
+            self.tail_send.at[w, 0],
+            self.tail_recv.at[w, 0],
+            self.opposite,
+        )
+
+    def add_tails(self, w):
+        total = self.held[w][self.line, self.most :].astype(WIDE)
+        for step in range(1, self.lines):
+            self.tail_copy(w, step).wait_recv()
+            total = total + self.fetch(self.tail_got[w].at[step])
+        self.tails[w][...] = total.astype(LOW)
+        self.tail_across(w).start()
 
     def product(self, left, right, place):
         rows = self.held[0].shape[1]
@@ -601,21 +666,31 @@
             other = (1 - self.side) * self.lines + place
             self.held[w][place] = self.product(left, right, other).astype(LOW)
             self.far_copy(w, place).start()
+            if self.tail:
+
+                @pl.when(at < self.lines - 1)
+                def _():
+                    self.tail_copy(w, step).start()
+
             return carry
 
         lax.fori_loop(0, self.lines, body, 0)
 
     def near(self, w, left, right, quarter):
-        def add(place):
+        def put(place, step):
             part = self.product(left, right, self.side * self.lines + place)
             self.far_copy(w, place).wait_recv()
-            total = part + self.fetch(self.far_got[w].at[place])
+            got = self.fetch(self.far_got[w].at[place, pl.ds(0, self.most)])
             self.far_copy(w, place).wait_send()
-            return total
+            if self.tail and step is not None:
+                self.tail_copy(w, step).wait_send()
+            self.held[w][place, : self.most] = (part[: self.most] + got).astype(LOW)
+            if self.tail:
+                self.held[w][place, self.most :] = part[self.most :].astype(LOW)
 
         def body(step, carry):
             place = lax.rem(self.line + step, self.lines)
-            self.held[w][place] = add(place).astype(LOW)
+            put(place, step)
             self.near_copy(w, step).start()
             return carry
 
@@ -626,7 +701,7 @@
             step = 1 + 2 * quarter
             end = 3 - 3 * quarter
             place = lax.rem(self.line + step, self.lines)
-            self.held[w][place] = add(place).astype(LOW)
+            put(place, step)
 
             @pl.when(self.line == end)
             def _():
@@ -637,8 +712,7 @@
                 self.near_copy(w, step).start()
         elif quarter == 2:
             place = lax.rem(self.line + 2, self.lines)
-            total = add(place)
-            self.held[w][place] = total.astype(LOW)
+            put(place, 2)
 
             @pl.when((self.line == 1) | (self.line == 2))
             def _():
@@ -651,8 +725,11 @@
             self.near_copy(w, 2).start()
         if quarter < 3:
             return
-        self.held[w][self.line] = add(self.line).astype(LOW)
-        self.own_copy(w).start()
+        if self.tail:
+            self.add_tails(w)
+        put(self.line, None)
+        if not self.tail:
+            self.own_copy(w).start()
         if self.lines == 4:
 
             @pl.when((self.line == 0) | (self.line == 3))
@@ -689,6 +766,13 @@
                     def _():
                         copy.wait_recv()
 
+        if self.tail:
+            self.tail_across(w).wait()
+            self.held[w][self.line, self.most :] = (
+                self.held[w][self.line, self.most :].astype(WIDE)
+                + self.fetch(self.tail_got[w].at[0])
+            ).astype(LOW)
+            self.own_copy(w).start()
         self.own_copy(w).wait()
 
 
@@ -726,13 +810,13 @@
     later = refs[3:9]
     gate_hidden, up_hidden = refs[9:11]
     near_got, mid_all, mid_grad_out, hidden_out, gain_out = refs[11:14], *refs[14:18]
-    far_got = refs[18:21]
-    gate_low, up_low, pre, up = refs[21:25]
-    scatter_held = refs[25:28]
-    spare, held, got, last, base, mid = refs[28:34]
-    sems = refs[34:38]
-    near_send, near_recv, home = refs[38:41]
-    loaded = refs[41:]
+    far_got, tail_got = refs[18:21], refs[21:24]
+    gate_low, up_low, pre, up = refs[24:28]
+    scatter_held = refs[28:31]
+    spare, held, got, last, base, mid = refs[31:37]
+    sems = refs[37:43]
+    near_send, near_recv, home = refs[43:46]
+    loaded, tails = refs[46:52], refs[52:]
     grad_ref, mid_turned, resid_ref, gate_weight, up_weight, down_weight = loaded
     parts = 2 * lines
     rows, width = resid_ref.shape
@@ -746,7 +830,9 @@
         scatter_held,
         far_got,
         near_got,
+        tail_got,
         {spare.shape[1]: spare},
+        tails,
         sems + (home.at[0],),
     )
     near = Near(near_send, near_recv)
@@ -877,9 +963,12 @@
     own.wait()
     near.sent(3)
     near.sent(4)
-    mid[...] = (
-        base[...] + last[2].astype(WIDE) + last[1].astype(WIDE) + resid_ref[...]
-    ).astype(LOW)
+    for p in range(parts):
+        columns = slice(p * slice_width, (p + 1) * slice_width)
+        value = base[:, columns] + last[2, :, columns].astype(WIDE)
+        value = value + last[1, :, columns].astype(WIDE) + resid_ref[:, columns]
+        start = (2 * (p % lines) + p // lines) * slice_width
+        mid[:, start : start + slice_width] = value.astype(LOW)
     own = pltpu.make_async_copy(mid, hidden_out, home.at[3])
     own.start()
     for w in range(3):
@@ -909,11 +998,13 @@
         ((8, width), WIDE),
     ]
     outs += [((lines + 1,) + piece[1:], LOW)] * 3
+    tail = max(tail_rows(slice_width, lines), 16)
+    outs += [((lines, tail, columns), LOW)] * 3
     return pl.pallas_call(
         functools.partial(feed_kernel, lines, members),
         out_shape=[jax.ShapeDtypeStruct(shape, dtype) for shape, dtype in outs],
         in_specs=[INSIDE] * 3 + [ANY] * 8,
-        out_specs=[ANY] * 6 + [INSIDE] + [ANY] * 3,
+        out_specs=[ANY] * 6 + [INSIDE] + [ANY] * 6,
         scratch_shapes=[
             pltpu.VMEM(blocks + (columns,), LOW),
             pltpu.VMEM(blocks + (columns,), LOW),
@@ -932,11 +1023,14 @@
             pltpu.SemaphoreType.DMA((3, lines)),
             pltpu.SemaphoreType.DMA((3, lines)),
             pltpu.SemaphoreType.DMA((3, lines)),
+            pltpu.SemaphoreType.DMA((3, lines)),
+            pltpu.SemaphoreType.DMA((3, lines)),
             pltpu.SemaphoreType.DMA((9,)),
             pltpu.SemaphoreType.DMA((9,)),
             pltpu.SemaphoreType.DMA((10,)),
         ]
-        + [pltpu.VMEM(value.shape, value.dtype) for value in later],
+        + [pltpu.VMEM(value.shape, value.dtype) for value in later]
+        + [pltpu.VMEM((tail, columns), LOW)] * 3,
         compiler_params=pltpu.CompilerParams(
             collective_id=1, has_side_effects=True, vmem_limit_bytes=ROOM
         ),
@@ -952,15 +1046,15 @@
     mid_grad_ref, mid_all, retained_all, gate_all = refs[13:17]
     weights = refs[17:22]
     near_got, in_grad_out, gain_out = refs[22:27], refs[27], refs[28]
-    far_got = refs[29:34]
-    turned, wide_one, wide_two, short_one, short_two = refs[34:39]
-    gate_low, retained_low, query_low, key_low = refs[39:43]
-    scatter_held = refs[43:48]
-    spare_wide, spare_short, held, got, base, retained, gate = refs[48:55]
-    pieces, piece_got, total, total_got = refs[55:59]
-    sems = refs[59:63]
-    near_send, near_recv, gain_send, gain_recv, home = refs[63:68]
-    loaded = refs[68:]
+    far_got, tail_got = refs[29:34], refs[34:39]
+    turned, wide_one, wide_two, short_one, short_two = refs[39:44]
+    gate_low, retained_low, query_low, key_low = refs[44:48]
+    scatter_held = refs[48:53]
+    spare_wide, spare_short, held, got, base, retained, gate = refs[53:60]
+    pieces, piece_got, total, total_got = refs[60:64]
+    sems = refs[64:70]
+    near_send, near_recv, gain_send, gain_recv, home = refs[70:75]
+    loaded, tails = refs[75:80], refs[80:]
     mixed, normed_turned, query, keys, values = loaded
     value_low = mixed
     parts = 2 * lines
@@ -974,7 +1068,9 @@
         scatter_held,
         far_got,
         near_got,
+        tail_got,
         {spare_wide.shape[1]: spare_wide, spare_short.shape[1]: spare_short},
+        tails,
         sems + (home.at[0],),
     )
     near = Near(near_send, near_recv)
@@ -1215,9 +1311,14 @@
     for p in range(parts):
         columns = slice(p * slice_width, (p + 1) * slice_width)
         block = hidden_ref[:, columns].astype(WIDE) * scale
-        in_grad_out[:, columns] += scale * (
+        base[:, columns] = in_grad_out[:, columns] + scale * (
             base[:, columns] * gain_all[p][0:1] - block * dot
         )
+    for p in range(parts):
+        start = (2 * (p % lines) + p // lines) * slice_width
+        in_grad_out[:, start : start + slice_width] = base[
+            :, p * slice_width : (p + 1) * slice_width
+        ]
     value = pieces[here]
     for k in range(1, parts):
         gains[k - 1].wait_recv()
@@ -1249,11 +1350,13 @@
     outs = [(piece, LOW) for piece in pieces]
     outs += [((rows, width), WIDE), ((8, slice_width), WIDE)]
     outs += [((lines + 1,) + piece[1:], LOW) for piece in pieces]
+    tail = max(tail_rows(slice_width, lines), 16)
+    outs += [((lines, tail, columns), LOW) for columns in widths]
     return pl.pallas_call(
         functools.partial(retention_kernel, lines, members),
         out_shape=[jax.ShapeDtypeStruct(shape, dtype) for shape, dtype in outs],
         in_specs=[ANY] * 5 + [INSIDE] * 8 + [ANY] * 9,
-        out_specs=[ANY] * 5 + [INSIDE] * 2 + [ANY] * 5,
+        out_specs=[ANY] * 5 + [INSIDE] * 2 + [ANY] * 10,
         scratch_shapes=[
             pltpu.VMEM((width, rows * members), LOW),
             pltpu.VMEM(weights[0].shape, LOW),
@@ -1282,13 +1385,16 @@
             pltpu.SemaphoreType.DMA((5, lines)),
             pltpu.SemaphoreType.DMA((5, lines)),
             pltpu.SemaphoreType.DMA((5, lines)),
+            pltpu.SemaphoreType.DMA((5, lines)),
+            pltpu.SemaphoreType.DMA((5, lines)),
             pltpu.SemaphoreType.DMA((6,)),
             pltpu.SemaphoreType.DMA((6,)),
             pltpu.SemaphoreType.DMA((parts,)),
             pltpu.SemaphoreType.DMA((parts,)),
             pltpu.SemaphoreType.DMA((14,)),
         ]
-        + [pltpu.VMEM(value.shape, value.dtype) for value in inside[:5]],
+        + [pltpu.VMEM(value.shape, value.dtype) for value in inside[:5]]
+        + [pltpu.VMEM((tail, columns), LOW) for columns in widths],
         compiler_params=pltpu.CompilerParams(
             collective_id=2, has_side_effects=True, vmem_limit_bytes=ROOM
         ),
@@ -1324,16 +1430,10 @@
         blocks = [value[:, k * slice_width : (k + 1) * slice_width] for k in order]
         return jnp.concatenate(blocks, axis=1)
 
-    def from_places(value):
-        blocks = [value[:, k * slice_width : (k + 1) * slice_width] for k in range(parts)]
-        return jnp.concatenate([blocks[k // 2 + k % 2 * lines] for k in range(parts)], axis=1)
-
     heads_here = w_query.shape[1] // KEY
     resid_low = to_places(hidden_in.reshape(rows, width))
     grad_local = to_places(out_grad.reshape(rows, width))
-    gain_rows = jnp.concatenate(
-        [norm1_gain[None], norm2_gain[None], jnp.zeros((6, slice_width), LOW)]
-    ).astype(WIDE)
+    gain_rows = jnp.stack([norm1_gain, norm2_gain])
     position = jnp.concatenate(
         [(own ^ k) * rows + jnp.arange(rows, dtype=jnp.int32) for k in range(members)]
     )
@@ -1397,8 +1497,8 @@
         return jnp.sum(pieces.astype(WIDE), axis=0)
 
     return (
-        from_places(hidden_out).reshape(hidden_in.shape),
-        from_places(in_grad).reshape(hidden_in.shape),
+        hidden_out.reshape(hidden_in.shape),
+        in_grad.reshape(hidden_in.shape),
         gain_total[0],
         add_up(query_grad),
         add_up(key_grad),

time: 716 us -> 674 us (0.941)
  Pallas kernels: 658 us -> 622 us
    pallas_call x1, Pallas kernels: 307 us -> 289 us  [forward(): pl.pallas_call(functools.partial(forward_kernel, lines, members), out_sha...]
    pallas_call x1, Pallas kernels: 213 us -> 200 us  [retention_backward(): pl.pallas_call(functools.partial(retention_kernel, lines, members), out_s...]
    unnamed x72 -> x54, local copies, waits for them, and re-layouts: 26 us -> 22 us
where the time goes in v5:
time: 674 us; the launch traced here: 663 us
  Pallas kernels  622 us (92%)
  local copies, waits for them, and re-layouts  26.4 us (4%)
  other arithmetic  13.1 us (2%)
    pallas_call x1, Pallas kernels, forward(): pl.pallas_call(functools.partial(forward_kernel, lines, members), out_sha...  289 us
    pallas_call x1, Pallas kernels, retention_backward(): pl.pallas_call(functools.partial(retention_kernel, lines, members), out_s...  200 us
    pallas_call x1, Pallas kernels, feed_backward(): pl.pallas_call(functools.partial(feed_kernel, lines, members), out_shape=...  133 us
    unnamed x54, local copies, waits for them, and re-layouts  22 us

profile of v5, /device:TPU:8, one launch (start us, length us, event | category | flops | bytes accessed | tf_op | source)
XLA Modules:
  0.0 663.0 jit_solution(10424951623356904449)
XLA Ops:
  0.6 0.0 copy-start.9
  0.7 0.0 copy-start.8
  0.7 0.0 copy-start.7
  0.7 0.6 broadcast_in_dim.2.refs_7_.refs_9_
  1.4 0.7 stack.9
  2.0 0.7 stack.10
  2.7 0.6 pad_maximum_fusion.refs_2_
  3.3 2.0 copy.42.refs_10_
  5.3 0.0 copy-start.12
  5.3 2.0 copy.43.refs_11_
  7.3 2.0 copy.39
  9.2 0.0 copy-start.6
  9.2 0.0 copy-done.7
  9.2 1.0 copy.44.refs_13_
  10.2 0.0 copy-done.8
  10.2 1.0 copy.45.refs_14_
  11.2 0.0 copy-done.9
  11.2 0.0 copy-start.5
  11.2 1.0 copy.40
  12.2 0.0 copy-done.12
  12.2 1.0 copy.41.refs_5_.refs_7_
  13.2 3.0 multiply_sine_fusion
  16.2 0.0 copy-done.6
  16.4 0.0 copy-done.5
  16.7 0.0 copy-start.11
  16.7 1.0 copy-done.11
  17.6 0.0 copy-start.10
  17.6 1.0 copy-done.10
  18.6 288.7 %forward.1 = (bf16[2048,1024]{1,0:T(8,128)(2,1)}, bf16[4,256,2048]{2,1,0:T(8,128)(2,1)}, f32[8,8,256]{2,1,0:T(8,128)}, bf16[8,256,512]{2,1,0:T(8,128)(2,1)}, bf1...) custom-call(bf16[256,2048]{1,0:T(8,128)(2,1)} %copy-done.10, ...), custom_call_target="tpu_custom_call" | custom-call | flops 99999997952 | bytes 1000000000 | tf_op jit(solution)/shard_map/forward/pallas_call | solution.py:514
  307.3 133.2 %feed_backward.1 = (bf16[4,256,864]{2,1,0:T(8,128)(2,1)}, bf16[4,256,864]{2,1,0:T(8,128)(2,1)}, bf16[4,256,864]{2,1,0:T(8,128)(2,1)}, bf16[4,256,2048]{2,1,0:T(8...) custom-call(bf16[2048,1024]{1,0:T(8,128)(2,1)} %get-tuple-element.49, ...), custom_call_target="tpu_custom_call" | custom-call | flops 99999997952 | bytes 1000000000 | tf_op jit(solution)/shard_map/feed_backward/pallas_call | solution.py:1003
  440.6 200.1 %retention_backward.1 = (bf16[4,256,864]{2,1,0:T(8,128)(2,1)}, bf16[4,256,864]{2,1,0:T(8,128)(2,1)}, bf16[4,256,864]{2,1,0:T(8,128)(2,1)}, bf16[4,256,512]{2,1,0...) custom-call(bf16[4,256,864]{2,1,0:T(8,128)(2,1)} %get-tuple-element., ...), custom_call_target="tpu_custom_call" | custom-call | flops 99999997952 | bytes 1000000000 | tf_op jit(solution)/shard_map/retention_backward/pallas_call | solution.py:1355
  640.7 0.0 copy-start.4
  640.7 1.4 fusion
  642.1 2.2 convert_reduce_fusion.7
  644.4 2.2 convert_reduce_fusion.6
  646.6 0.0 copy-done.4
  646.6 0.0 copy-start.3
  646.6 0.3 convert_reduce_fusion.5
  646.9 1.2 copy.47
  648.1 0.0 copy-done.3
  648.1 0.3 convert_reduce_fusion.4
  648.3 1.2 copy.48
  649.5 0.0 copy-start.2
  649.5 2.0 convert_reduce_fusion.3
  651.5 1.2 copy.49
  652.7 0.0 copy-done.2
  652.7 0.3 convert_reduce_fusion.2
  653.0 1.2 copy.50
  654.2 0.0 copy-start.1
  654.2 2.0 convert_reduce_fusion.1
  656.2 1.2 copy.51
  657.4 0.0 copy-done.1
  657.4 0.3 convert_reduce_fusion
  657.7 0.0 copy-start
  657.7 1.2 copy.52
  658.9 2.3 copy.69
  661.2 0.0 copy-done
  661.2 1.3 copy.70
  (20 shorter events, 0.4 us)
Async XLA Ops:
  0.6 10.6 %copy-start.9 = (bf16[864,256]{1,0:T(8,128)(2,1)S(1)}, bf16[864,256]{1,0:T(8,128)(2,1)}, u32[]{:S(2)}) copy-start(bf16[864,256]{1,0:T(8,128)(2,1)} %param.25) | copy-start | bytes 1327108
  0.7 9.6 %copy-start.8 = (bf16[256,864]{0,1:T(8,128)(2,1)S(1)}, bf16[256,864]{0,1:T(8,128)(2,1)}, u32[]{:S(2)}) copy-start(bf16[256,864]{0,1:T(8,128)(2,1)} %param.24) | copy-start | bytes 1327108
  0.7 8.6 %copy-start.7 = (bf16[256,864]{0,1:T(8,128)(2,1)S(1)}, bf16[256,864]{0,1:T(8,128)(2,1)}, u32[]{:S(2)}) copy-start(bf16[256,864]{0,1:T(8,128)(2,1)} %param.23) | copy-start | bytes 1327108
  5.3 6.9 %copy-start.12 = (s32[1,1024]{1,0:T(1,128)S(1)}, s32[1,1024]{1,0:T(1,128)}, u32[]{:S(2)}) copy-start(s32[1,1024]{1,0:T(1,128)} %refs_8_.3) | copy-start | bytes 12292
  9.2 7.0 %copy-start.6 = (bf16[1,256,2048]{2,1,0:T(8,128)(2,1)S(1)}, bf16[1,256,2048]{2,1,0:T(8,128)(2,1)}, u32[]{:S(2)}) copy-start(bf16[1,256,2048]{2,1,0:T(8,128)(2,1)} %param.13) | copy-start | bytes 3145732
  11.2 5.2 copy-start.5
  16.7 1.0 copy-start.11
  17.6 1.0 copy-start.10
  640.7 5.9 copy-start.4
  646.6 1.5 copy-start.3
  649.5 3.2 copy-start.2
  654.2 3.2 copy-start.1
  657.7 3.5 copy-start

commit v6 on v5

--- a/solution.py
+++ b/solution.py
@@ -55,7 +55,7 @@
     query, keys, scores, values, retained, gate, mixed, hidden = refs[45:53]
     held, got, base = refs[53:56]
     line_send, line_recv, side_send, side_recv = refs[56:60]
-    near_send, near_recv, gain_send, gain_recv, home, tail_send, tail_recv, gain_rows = refs[60:]
+    near_send, near_recv, gain_send, gain_recv, home, tail_send, tail_recv, gain_rows, raw, flip = refs[60:]
 
     parts = 2 * lines
     rows, width = hidden_ref.shape
@@ -102,7 +102,7 @@
 
     def line_copy(w, step):
         return remote(
-            shards[w],
+            source(w),
             wholes[w].at[here],
             line_send.at[w, step],
             line_recv.at[w, step],
@@ -154,14 +154,32 @@
 
     sends = [2, 1, 3] if inner else list(range(1, lines))
 
+    def prepare(w):
+        if w < 2:
+            ours[w] = keep(shards[w], wholes[w].at[here])
+            return
+        copy = pltpu.make_async_copy(shards[w], raw, home.at[home.shape[0] - 1])
+        copy.start()
+        copy.wait()
+        columns = raw.shape[0]
+        for at in range(0, columns, 128):
+            block = slice(at, min(at + 128, columns))
+            flip[:, block] = raw[block, :].T
+        copy = pltpu.make_async_copy(flip, wholes[w].at[here], home.at[home.shape[0] - 1])
+        copy.start()
+        copy.wait()
+
+    def source(w):
+        return shards[w] if w < 2 else wholes[w].at[here]
+
     def start_lines(w):
+        prepare(w)
         for step in sends:
             on_line(w, step, lambda copy: copy.start())
         across[w, 0] = remote(
-            shards[w], wholes[w].at[here], side_send.at[w, 0], side_recv.at[w, 0], opposite
+            source(w), wholes[w].at[here], side_send.at[w, 0], side_recv.at[w, 0], opposite
         )
         across[w, 0].start()
-        ours[w] = keep(shards[w], wholes[w].at[here])
 
     def pass_on(w, third):
         for at in range(third * (lines - 1) // 3, (third + 1) * (lines - 1) // 3):
@@ -189,7 +207,8 @@
             side_copy(w, step).wait_recv()
             if tail:
                 tail_copy(w, step).wait_recv()
-        finish(ours[w])
+        if w in ours:
+            finish(ours[w])
 
     def load(w, target, sem):
         copy = pltpu.make_async_copy(wholes[w], target, sem)
@@ -483,7 +502,8 @@
     parts = 2 * lines
     rows, width = hidden.shape
     heads = rates.shape[0]
-    key_columns, value_columns = shards[0].shape[1], shards[2].shape[1]
+    key_columns, value_columns = shards[0].shape[1], shards[2].shape[0]
+    chunks = [shard.shape if k < 2 else shard.shape[::-1] for k, shard in enumerate(shards)]
     length = rows * members
     blocks = (members, rows)
     turned = (width, length)
@@ -492,7 +512,7 @@
         (blocks + (width,), LOW),
         ((parts, 8, gains.shape[1]), WIDE),
     ]
-    outs += [((parts,) + shard.shape, LOW) for shard in shards]
+    outs += [((parts,) + chunk, LOW) for chunk in chunks]
     outs += [
         (blocks + (key_columns,), LOW),
         (blocks + (key_columns,), LOW),
@@ -519,9 +539,9 @@
         scratch_shapes=[
             pltpu.VMEM(blocks + (width,), LOW),
             pltpu.VMEM(blocks + (width,), LOW),
-            pltpu.VMEM((parts,) + shards[0].shape, LOW),
-            pltpu.VMEM((parts,) + shards[2].shape, LOW),
-            pltpu.VMEM((parts,) + shards[2].shape, LOW),
+            pltpu.VMEM((parts,) + chunks[0], LOW),
+            pltpu.VMEM((parts,) + chunks[2], LOW),
+            pltpu.VMEM((parts,) + chunks[2], LOW),
             pltpu.VMEM(turned, LOW),
             pltpu.VMEM(blocks + (key_columns,), LOW),
             pltpu.VMEM(blocks + (key_columns,), LOW),
@@ -546,6 +566,8 @@
             pltpu.SemaphoreType.DMA((WEIGHTS, lines)),
             pltpu.SemaphoreType.DMA((WEIGHTS, lines)),
             pltpu.VMEM((8, gains.shape[1]), WIDE),
+            pltpu.VMEM(shards[2].shape, LOW),
+            pltpu.VMEM(shards[2].shape[::-1], LOW),
         ],
         compiler_params=pltpu.CompilerParams(
             collective_id=0, has_side_effects=True, vmem_limit_bytes=ROOM
@@ -810,13 +832,14 @@
     later = refs[3:9]
     gate_hidden, up_hidden = refs[9:11]
     near_got, mid_all, mid_grad_out, hidden_out, gain_out = refs[11:14], *refs[14:18]
-    far_got, tail_got = refs[18:21], refs[21:24]
-    gate_low, up_low, pre, up = refs[24:28]
-    scatter_held = refs[28:31]
-    spare, held, got, last, base, mid = refs[31:37]
-    sems = refs[37:43]
-    near_send, near_recv, home = refs[43:46]
-    loaded, tails = refs[46:52], refs[52:]
+    mid_low_turned = refs[18]
+    far_got, tail_got = refs[19:22], refs[22:25]
+    gate_low, up_low, pre, up = refs[25:29]
+    scatter_held = refs[29:32]
+    spare, held, got, last, base, mid = refs[32:38]
+    sems = refs[38:44]
+    near_send, near_recv, home, column = refs[44:48]
+    loaded, tails = refs[48:54], refs[54:]
     grad_ref, mid_turned, resid_ref, gate_weight, up_weight, down_weight = loaded
     parts = 2 * lines
     rows, width = resid_ref.shape
@@ -956,11 +979,27 @@
     near.start(8, held.at[1], last.at[2], 1)
     scatter.near(2, mid_turned, up_low, 1)
     down(0, put_sum)
+    own.wait()
+    near.wait(4)
+    near.wait(5)
+    for k in range(members):
+        copy = pltpu.make_async_copy(mid_all.at[k], got.at[0], home.at[9])
+        copy.start()
+        copy.wait()
+        if k:
+            turned_copy.wait()
+        for c in range(width // 256):
+            block = slice(c * 256, (c + 1) * 256)
+            column[block, :] = got[0, :, block].T
+        turned_copy = pltpu.make_async_copy(
+            column, mid_low_turned.at[:, pl.ds(k * rows, rows)], home.at[10]
+        )
+        turned_copy.start()
+    turned_copy.wait()
     scatter.near(2, mid_turned, up_low, 2)
     scatter.near(2, mid_turned, up_low, 3)
     near.wait(8)
     near.wait(7)
-    own.wait()
     near.sent(3)
     near.sent(4)
     for p in range(parts):
@@ -971,13 +1010,12 @@
         mid[:, start : start + slice_width] = value.astype(LOW)
     own = pltpu.make_async_copy(mid, hidden_out, home.at[3])
     own.start()
+    own.wait()
+    near.sent(5)
+    near.sent(7)
+    near.sent(8)
     for w in range(3):
         scatter.finish(w)
-    near.wait(4)
-    near.wait(5)
-    own.wait()
-    for tag in (5, 7, 8):
-        near.sent(tag)
 
 
 def feed_backward(
@@ -996,6 +1034,7 @@
         ((rows, width), WIDE),
         ((rows, width), LOW),
         ((8, width), WIDE),
+        ((width, rows * members), LOW),
     ]
     outs += [((lines + 1,) + piece[1:], LOW)] * 3
     tail = max(tail_rows(slice_width, lines), 16)
@@ -1004,7 +1043,7 @@
         functools.partial(feed_kernel, lines, members),
         out_shape=[jax.ShapeDtypeStruct(shape, dtype) for shape, dtype in outs],
         in_specs=[INSIDE] * 3 + [ANY] * 8,
-        out_specs=[ANY] * 6 + [INSIDE] + [ANY] * 6,
+        out_specs=[ANY] * 6 + [INSIDE] + [ANY] * 7,
         scratch_shapes=[
             pltpu.VMEM(blocks + (columns,), LOW),
             pltpu.VMEM(blocks + (columns,), LOW),
@@ -1027,7 +1066,8 @@
             pltpu.SemaphoreType.DMA((3, lines)),
             pltpu.SemaphoreType.DMA((9,)),
             pltpu.SemaphoreType.DMA((9,)),
-            pltpu.SemaphoreType.DMA((10,)),
+            pltpu.SemaphoreType.DMA((11,)),
+            pltpu.VMEM((width, rows), LOW),
         ]
         + [pltpu.VMEM(value.shape, value.dtype) for value in later]
         + [pltpu.VMEM((tail, columns), LOW)] * 3,
@@ -1036,26 +1076,26 @@
         ),
         cost_estimate=pl.CostEstimate(flops=10**11, bytes_accessed=10**9, transcendentals=0),
         name="feed_backward",
-    )(grad_turned, hidden, gains, *later, *pres)[:7]
+    )(grad_turned, hidden, gains, *later, *pres)[:8]
 
 
 def retention_kernel(lines, members, *refs):
-    later = refs[:5]
-    cos_ref, sin_ref, down_seg, along_seg, rate_ref = refs[5:10]
-    hidden_ref, gain_all, gain_part = refs[10:13]
-    mid_grad_ref, mid_all, retained_all, gate_all = refs[13:17]
-    weights = refs[17:22]
-    near_got, in_grad_out, gain_out = refs[22:27], refs[27], refs[28]
-    far_got, tail_got = refs[29:34], refs[34:39]
-    turned, wide_one, wide_two, short_one, short_two = refs[39:44]
+    later = refs[:6]
+    cos_ref, sin_ref, down_seg, along_seg, rate_ref = refs[6:11]
+    hidden_ref, gain_all, gain_part = refs[11:14]
+    mid_grad_ref, mid_all, retained_all, gate_all = refs[14:18]
+    weights = refs[18:23]
+    near_got, in_grad_out, gain_out = refs[23:28], refs[28], refs[29]
+    far_got, tail_got = refs[30:35], refs[35:40]
+    wide_one, wide_two, short_one, short_two = refs[40:44]
     gate_low, retained_low, query_low, key_low = refs[44:48]
     scatter_held = refs[48:53]
     spare_wide, spare_short, held, got, base, retained, gate = refs[53:60]
     pieces, piece_got, total, total_got = refs[60:64]
     sems = refs[64:70]
     near_send, near_recv, gain_send, gain_recv, home = refs[70:75]
-    loaded, tails = refs[75:80], refs[80:]
-    mixed, normed_turned, query, keys, values = loaded
+    loaded, tails = refs[75:81], refs[81:]
+    mixed, normed_turned, query, keys, values, turned = loaded
     value_low = mixed
     parts = 2 * lines
     rows, width = hidden_ref.shape
@@ -1084,26 +1124,18 @@
         copy.start()
         return copy
 
+    loads = [fetch(later[k], loaded[k], 9 + k) for k in (5, 0)]
     out_copy = fetch(weights[0], wide_one, 1)
+    loads += [fetch(later[k], loaded[k], 9 + k) for k in range(1, 5)]
     value_copy = fetch(weights[2], wide_two, 2)
     query_copy = fetch(weights[3], short_one, 3)
     key_copy = fetch(weights[4], short_two, 4)
     grad_copy = fetch(mid_grad_ref, in_grad_out, 7)
-    loads = [fetch(later[k], loaded[k], 9 + k) for k in range(5)]
-
-    def turn_over(k, carry):
-        fetch(mid_all.at[k], held.at[0], 8).wait()
-        at = pl.ds(pl.multiple_of(k * rows, rows), rows)
-        for c in range(width // 256):
-            columns = slice(c * 256, (c + 1) * 256)
-            turned[columns, at] = held[0, :, columns].T
-        return carry
-
-    lax.fori_loop(0, members, turn_over, 0)
     loads[0].wait()
+    loads[1].wait()
     scatter.far(0, turned, mixed)
     out_copy.wait()
-    for load in loads[1:]:
+    for load in loads[2:]:
         load.wait()
 
     column = lax.broadcasted_iota(jnp.int32, (rows, value_columns), 1)
@@ -1217,10 +1249,13 @@
     scatter.near(0, turned, mixed, 2)
     scatter.near(0, turned, mixed, 3)
     early_side(0, 0)
-    for m in range(1, members):
-        early_side(m, 0)
-        scatter.near(1, normed_turned, gate_low, m - 1)
+    early_side(1, 0)
+    scatter.near(1, normed_turned, gate_low, 0)
+    early_side(2, 0)
+    early_side(3, 0)
     scatter.far(2, normed_turned, value_low)
+    scatter.near(1, normed_turned, gate_low, 1)
+    scatter.near(1, normed_turned, gate_low, 2)
     scatter.far(4, normed_turned, key_low)
     scatter.near(1, normed_turned, gate_low, 3)
 
@@ -1342,7 +1377,7 @@
 
 def retention_backward(inside, streamed, weights, lines, members, slice_width):
     parts = 2 * lines
-    rows, width = inside[10].shape
+    rows, width = inside[11].shape
     blocks = (members, rows)
     wide, short = weights[0].shape[2], weights[3].shape[2]
     widths = [wide, wide, wide, short, short]
@@ -1355,10 +1390,9 @@
     return pl.pallas_call(
         functools.partial(retention_kernel, lines, members),
         out_shape=[jax.ShapeDtypeStruct(shape, dtype) for shape, dtype in outs],
-        in_specs=[ANY] * 5 + [INSIDE] * 8 + [ANY] * 9,
+        in_specs=[ANY] * 6 + [INSIDE] * 8 + [ANY] * 9,
         out_specs=[ANY] * 5 + [INSIDE] * 2 + [ANY] * 10,
         scratch_shapes=[
-            pltpu.VMEM((width, rows * members), LOW),
             pltpu.VMEM(weights[0].shape, LOW),
             pltpu.VMEM(weights[0].shape, LOW),
             pltpu.VMEM(weights[3].shape, LOW),
@@ -1391,9 +1425,9 @@
             pltpu.SemaphoreType.DMA((6,)),
             pltpu.SemaphoreType.DMA((parts,)),
             pltpu.SemaphoreType.DMA((parts,)),
-            pltpu.SemaphoreType.DMA((14,)),
+            pltpu.SemaphoreType.DMA((15,)),
         ]
-        + [pltpu.VMEM(value.shape, value.dtype) for value in inside[:5]]
+        + [pltpu.VMEM(value.shape, value.dtype) for value in inside[:6]]
         + [pltpu.VMEM((tail, columns), LOW) for columns in widths],
         compiler_params=pltpu.CompilerParams(
             collective_id=2, has_side_effects=True, vmem_limit_bytes=ROOM
@@ -1449,7 +1483,7 @@
         sine,
         segment_ids,
         rates,
-        [w_query, w_key, w_value, w_gate, w_out.T, w_mlp_gate, w_mlp_up, w_mlp_down.T],
+        [w_query, w_key, w_value.T, w_gate.T, w_out, w_mlp_gate.T, w_mlp_up.T, w_mlp_down],
         lines,
         members,
     )
@@ -1457,7 +1491,7 @@
     query_weight, key_weight, value_weight, gate_weight, out_weight = outs[3:8]
     query, keys, values, gate_pre, grad_turned = outs[11:16]
     retained, mixed, resid_mid, mid_turned, gate_hidden, up_hidden, hidden = outs[16:]
-    down_grad, mlp_gate_grad, mlp_up_grad, mid_all, mid_grad, hidden_out, gain_part = feed_backward(
+    feed_outs = feed_backward(
         grad_full,
         grad_turned,
         mid_turned,
@@ -1469,6 +1503,8 @@
         lines,
         members,
     )
+    down_grad, mlp_gate_grad, mlp_up_grad, mid_all, mid_grad = feed_outs[:5]
+    hidden_out, gain_part, mid_low_turned = feed_outs[5:]
     out_weight_grad, gate_grad, value_grad, query_grad, key_grad, in_grad, gain_total = (
         retention_backward(
             [
@@ -1477,6 +1513,7 @@
                 query,
                 keys,
                 values,
+                mid_low_turned,
                 cosine,
                 sine,
                 segment_ids.T,
@@ -1494,7 +1531,10 @@
         )
     )
     def add_up(pieces):
-        return jnp.sum(pieces.astype(WIDE), axis=0)
+        total = pieces[0].astype(WIDE)
+        for k in range(1, pieces.shape[0]):
+            total = total + pieces[k].astype(WIDE)
+        return total
 
     return (
         hidden_out.reshape(hidden_in.shape),

time: 674 us -> 656 us (0.973)
  Pallas kernels: 622 us -> 612 us
    pallas_call x1, Pallas kernels: 200 us -> 190 us  [retention_backward(): pl.pallas_call(functools.partial(retention_kernel, lines, members), out_s...]
    reduce_sum x8 -> x0, other arithmetic: 9.47 us -> none  [add_up(): return jnp.sum(pieces.astype(WIDE), axis=0)]
    unnamed x54 -> x40, local copies, waits for them, and re-layouts: 22 us -> 15 us
where the time goes in v6:
time: 656 us; the launch traced here: 646 us
  Pallas kernels  612 us (93%)
  local copies, waits for them, and re-layouts  20.2 us (3%)
  other arithmetic  12.3 us (2%)
    pallas_call x1, Pallas kernels, forward(): pl.pallas_call(functools.partial(forward_kernel, lines, members), out_sha...  289 us
    pallas_call x1, Pallas kernels, retention_backward(): pl.pallas_call(functools.partial(retention_kernel, lines, members), out_s...  190 us
    pallas_call x1, Pallas kernels, feed_backward(): pl.pallas_call(functools.partial(feed_kernel, lines, members), out_shape=...  133 us
    unnamed x40, local copies, waits for them, and re-layouts  15 us

profile of v6, /device:TPU:8, one launch (start us, length us, event | category | flops | bytes accessed | tf_op | source)
XLA Modules:
  0.0 645.8 jit_solution(15435602504489278001)
XLA Ops:
  0.6 0.0 copy-start.5
  0.7 0.0 copy-start.6
  0.7 0.6 broadcast_in_dim.2.refs_7_.refs_10_
  1.3 0.7 stack.9
  2.0 0.7 stack.10
  2.7 0.6 pad_maximum_fusion.refs_2_
  3.3 1.7 copy.31.refs_5_.refs_8_
  5.0 3.0 multiply_sine_fusion
  8.0 0.9 slice_dynamic-update-slice_fusion.15
  8.9 0.9 slice_dynamic-update-slice_fusion.14
  9.8 0.0 copy-done.6
  10.0 0.0 copy-done.5
  10.2 0.0 copy-start.8
  10.2 1.0 copy-done.8
  11.2 0.0 copy-start.7
  11.2 1.0 copy-done.7
  12.2 288.7 %forward.1 = (bf16[2048,1024]{1,0:T(8,128)(2,1)}, bf16[4,256,2048]{2,1,0:T(8,128)(2,1)}, f32[8,8,256]{2,1,0:T(8,128)}, bf16[8,256,512]{2,1,0:T(8,128)(2,1)}, bf1...) custom-call(bf16[256,2048]{1,0:T(8,128)(2,1)} %copy-done.7, ...), custom_call_target="tpu_custom_call" | custom-call | flops 99999997952 | bytes 1000000000 | tf_op jit(solution)/shard_map/forward/pallas_call | solution.py:534
  300.9 133.3 %feed_backward.1 = (bf16[4,256,864]{2,1,0:T(8,128)(2,1)}, bf16[4,256,864]{2,1,0:T(8,128)(2,1)}, bf16[4,256,864]{2,1,0:T(8,128)(2,1)}, bf16[4,256,2048]{2,1,0:T(8...) custom-call(bf16[2048,1024]{1,0:T(8,128)(2,1)} %get-tuple-element.50, ...), custom_call_target="tpu_custom_call" | custom-call | flops 99999997952 | bytes 1000000000 | tf_op jit(solution)/shard_map/feed_backward/pallas_call | solution.py:1042
  434.2 190.1 %retention_backward.1 = (bf16[4,256,864]{2,1,0:T(8,128)(2,1)}, bf16[4,256,864]{2,1,0:T(8,128)(2,1)}, bf16[4,256,864]{2,1,0:T(8,128)(2,1)}, bf16[4,256,512]{2,1,0...) custom-call(bf16[4,256,864]{2,1,0:T(8,128)(2,1)} %get-tuple-element., ...), custom_call_target="tpu_custom_call" | custom-call | flops 99999997952 | bytes 1000000000 | tf_op jit(solution)/shard_map/retention_backward/pallas_call | solution.py:1390
  624.3 0.0 copy-start.4
  624.3 1.4 fusion
  625.7 2.1 add_bitcast_fusion.7
  627.8 2.1 add_bitcast_fusion.6
  629.9 0.0 copy-done.4
  629.9 0.0 copy-start.3
  629.9 0.2 add_bitcast_fusion.5
  630.2 1.2 copy.33
  631.4 0.1 copy-done.3
  631.5 0.2 add_bitcast_fusion.4
  631.7 1.2 copy.34
  632.9 0.0 copy-start.2
  632.9 1.8 add_bitcast_fusion.3
  634.7 1.2 copy.35
  635.9 0.0 copy-done.2
  635.9 0.2 add_bitcast_fusion.2
  636.1 1.2 copy.36
  637.3 0.0 copy-start.1
  637.3 1.8 add_bitcast_fusion.1
  639.1 1.2 copy.37
  640.3 0.0 copy-done.1
  640.3 0.2 add_bitcast_fusion
  640.6 0.0 copy-start
  640.6 1.2 copy.38
  641.8 2.3 copy.55
  644.1 0.0 copy-done
  644.1 1.3 copy.56
  (18 shorter events, 0.3 us)
Async XLA Ops:
  0.6 9.3 %copy-start.5 = (bf16[1,256,2048]{2,1,0:T(8,128)(2,1)S(1)}, bf16[1,256,2048]{2,1,0:T(8,128)(2,1)}, u32[]{:S(2)}) copy-start(bf16[1,256,2048]{2,1,0:T(8,128)(2,1)} %param.14) | copy-start | bytes 3145732
  0.7 9.2 %copy-start.6 = (bf16[1,256,2048]{2,1,0:T(8,128)(2,1)S(1)}, bf16[1,256,2048]{2,1,0:T(8,128)(2,1)}, u32[]{:S(2)}) copy-start(bf16[1,256,2048]{2,1,0:T(8,128)(2,1)} %param.13) | copy-start | bytes 3145732
  10.2 1.0 copy-start.8
  11.2 1.0 copy-start.7
  624.3 5.6 copy-start.4
  629.9 1.6 copy-start.3
  632.9 3.0 copy-start.2
  637.3 3.0 copy-start.1
  640.6 3.5 copy-start

commit v7 on v6

--- a/solution.py
+++ b/solution.py
@@ -579,19 +579,19 @@
     )(hidden, grad, gains, cosine, sine, segments.T, segments, rates, *shards)
 
 
-def tail_rows(rows, lines):
-    return rows // 8 // 16 * 16 if lines == 4 else 0
+def tail_rows(rows, lines, sixteenths):
+    return rows * sixteenths // 16 // 16 * 16 if lines == 4 else 0
 
 
 class Scatter:
-    def __init__(self, lines, held, far_got, near_got, tail_got, spare, tails, sems):
+    def __init__(self, lines, held, far_got, near_got, tail_got, spare, tails, sixteenths, sems):
         self.lines = lines
         self.held, self.far_got, self.near_got, self.spare = held, far_got, near_got, spare
         self.tail_got, self.tails = tail_got, tails
         self.side_send, self.side_recv, self.line_send, self.line_recv = sems[:4]
         self.tail_send, self.tail_recv, self.home = sems[4:]
         self.rows = held[0].shape[1]
-        self.tail = tail_rows(self.rows, lines)
+        self.tail = tail_rows(self.rows, lines, sixteenths)
         self.most = self.rows - self.tail
         me = lax.axis_index("dp")
         self.line, self.side = me // 2, lax.rem(me, 2)
@@ -856,6 +856,7 @@
         tail_got,
         {spare.shape[1]: spare},
         tails,
+        3,
         sems + (home.at[0],),
     )
     near = Near(near_send, near_recv)
@@ -997,6 +998,7 @@
         turned_copy.start()
     turned_copy.wait()
     scatter.near(2, mid_turned, up_low, 2)
+    scatter.finish(0)
     scatter.near(2, mid_turned, up_low, 3)
     near.wait(8)
     near.wait(7)
@@ -1014,8 +1016,8 @@
     near.sent(5)
     near.sent(7)
     near.sent(8)
-    for w in range(3):
-        scatter.finish(w)
+    scatter.finish(1)
+    scatter.finish(2)
 
 
 def feed_backward(
@@ -1037,7 +1039,7 @@
         ((width, rows * members), LOW),
     ]
     outs += [((lines + 1,) + piece[1:], LOW)] * 3
-    tail = max(tail_rows(slice_width, lines), 16)
+    tail = max(tail_rows(slice_width, lines, 3), 16)
     outs += [((lines, tail, columns), LOW)] * 3
     return pl.pallas_call(
         functools.partial(feed_kernel, lines, members),
@@ -1111,6 +1113,7 @@
         tail_got,
         {spare_wide.shape[1]: spare_wide, spare_short.shape[1]: spare_short},
         tails,
+        2,
         sems + (home.at[0],),
     )
     near = Near(near_send, near_recv)
@@ -1361,10 +1364,15 @@
     total[...] = value
     for k in range(1, members):
         near.start(2 + k, total, total_got.at[k], k)
-    for quarter in range(4):
-        scatter.near(3, normed_turned, query_low, quarter)
-    for w in (0, 1, 2, 4, 3):
-        scatter.finish(w)
+    scatter.near(3, normed_turned, query_low, 0)
+    scatter.finish(0)
+    scatter.near(3, normed_turned, query_low, 1)
+    scatter.finish(1)
+    scatter.near(3, normed_turned, query_low, 2)
+    scatter.finish(2)
+    scatter.near(3, normed_turned, query_low, 3)
+    scatter.finish(4)
+    scatter.finish(3)
     for k in range(1, members):
         near.wait(2 + k)
         value = value + total_got[k]
@@ -1385,7 +1393,7 @@
     outs = [(piece, LOW) for piece in pieces]
     outs += [((rows, width), WIDE), ((8, slice_width), WIDE)]
     outs += [((lines + 1,) + piece[1:], LOW) for piece in pieces]
-    tail = max(tail_rows(slice_width, lines), 16)
+    tail = max(tail_rows(slice_width, lines, 2), 16)
     outs += [((lines, tail, columns), LOW) for columns in widths]
     return pl.pallas_call(
         functools.partial(retention_kernel, lines, members),

time: 656 us -> 653 us (level)
  no operation moved by 1% of the time
where the time goes in v7:
time: 653 us; the launch traced here: 642 us
  Pallas kernels  608 us (93%)
  local copies, waits for them, and re-layouts  20.2 us (3%)
  other arithmetic  12.3 us (2%)
    pallas_call x1, Pallas kernels, forward(): pl.pallas_call(functools.partial(forward_kernel, lines, members), out_sha...  289 us
    pallas_call x1, Pallas kernels, retention_backward(): pl.pallas_call(functools.partial(retention_kernel, lines, members), out_s...  186 us
    pallas_call x1, Pallas kernels, feed_backward(): pl.pallas_call(functools.partial(feed_kernel, lines, members), out_shape=...  134 us
    unnamed x40, local copies, waits for them, and re-layouts  15 us

profile of v7, /device:TPU:8, one launch (start us, length us, event | category | flops | bytes accessed | tf_op | source)
XLA Modules:
  0.0 642.2 jit_solution(2686740885874628575)
XLA Ops:
  0.6 0.0 copy-start.5
  0.7 0.0 copy-start.6
  0.7 0.6 broadcast_in_dim.2.refs_7_.refs_10_
  1.3 0.7 stack.9
  2.0 0.7 stack.10
  2.7 0.6 pad_maximum_fusion.refs_2_
  3.3 1.7 copy.31.refs_5_.refs_8_
  5.0 3.0 multiply_sine_fusion
  8.0 0.9 slice_dynamic-update-slice_fusion.15
  8.9 0.9 slice_dynamic-update-slice_fusion.14
  9.8 0.0 copy-done.6
  10.0 0.0 copy-done.5
  10.2 0.0 copy-start.8
  10.2 1.0 copy-done.8
  11.2 0.0 copy-start.7
  11.2 1.0 copy-done.7
  12.2 288.7 %forward.1 = (bf16[2048,1024]{1,0:T(8,128)(2,1)}, bf16[4,256,2048]{2,1,0:T(8,128)(2,1)}, f32[8,8,256]{2,1,0:T(8,128)}, bf16[8,256,512]{2,1,0:T(8,128)(2,1)}, bf1...) custom-call(bf16[256,2048]{1,0:T(8,128)(2,1)} %copy-done.7, ...), custom_call_target="tpu_custom_call" | custom-call | flops 99999997952 | bytes 1000000000 | tf_op jit(solution)/shard_map/forward/pallas_call | solution.py:534
  300.9 133.8 %feed_backward.1 = (bf16[4,256,864]{2,1,0:T(8,128)(2,1)}, bf16[4,256,864]{2,1,0:T(8,128)(2,1)}, bf16[4,256,864]{2,1,0:T(8,128)(2,1)}, bf16[4,256,2048]{2,1,0:T(8...) custom-call(bf16[2048,1024]{1,0:T(8,128)(2,1)} %get-tuple-element.50, ...), custom_call_target="tpu_custom_call" | custom-call | flops 99999997952 | bytes 1000000000 | tf_op jit(solution)/shard_map/feed_backward/pallas_call | solution.py:1044
  434.7 186.0 %retention_backward.1 = (bf16[4,256,864]{2,1,0:T(8,128)(2,1)}, bf16[4,256,864]{2,1,0:T(8,128)(2,1)}, bf16[4,256,864]{2,1,0:T(8,128)(2,1)}, bf16[4,256,512]{2,1,0...) custom-call(bf16[4,256,864]{2,1,0:T(8,128)(2,1)} %get-tuple-element., ...), custom_call_target="tpu_custom_call" | custom-call | flops 99999997952 | bytes 1000000000 | tf_op jit(solution)/shard_map/retention_backward/pallas_call | solution.py:1398
  620.6 0.0 copy-start.4
  620.6 1.4 fusion
  622.1 2.1 add_bitcast_fusion.7
  624.2 2.1 add_bitcast_fusion.6
  626.3 0.0 copy-done.4
  626.3 0.0 copy-start.3
  626.3 0.2 add_bitcast_fusion.5
  626.5 1.2 copy.33
  627.7 0.1 copy-done.3
  627.9 0.2 add_bitcast_fusion.4
  628.1 1.2 copy.34
  629.3 0.0 copy-start.2
  629.3 1.8 add_bitcast_fusion.3
  631.1 1.2 copy.35
  632.3 0.0 copy-done.2
  632.3 0.2 add_bitcast_fusion.2
  632.5 1.2 copy.36
  633.7 0.0 copy-start.1
  633.7 1.8 add_bitcast_fusion.1
  635.5 1.2 copy.37
  636.7 0.0 copy-done.1
  636.7 0.2 add_bitcast_fusion
  636.9 0.0 copy-start
  636.9 1.2 copy.38
  638.1 2.3 copy.55
  640.4 0.0 copy-done
  640.4 1.3 copy.56
  (18 shorter events, 0.3 us)
Async XLA Ops:
  0.6 9.3 %copy-start.5 = (bf16[1,256,2048]{2,1,0:T(8,128)(2,1)S(1)}, bf16[1,256,2048]{2,1,0:T(8,128)(2,1)}, u32[]{:S(2)}) copy-start(bf16[1,256,2048]{2,1,0:T(8,128)(2,1)} %param.14) | copy-start | bytes 3145732
  0.7 9.2 %copy-start.6 = (bf16[1,256,2048]{2,1,0:T(8,128)(2,1)S(1)}, bf16[1,256,2048]{2,1,0:T(8,128)(2,1)}, u32[]{:S(2)}) copy-start(bf16[1,256,2048]{2,1,0:T(8,128)(2,1)} %param.13) | copy-start | bytes 3145732
  10.2 1.0 copy-start.8
  11.2 1.0 copy-start.7
  620.6 5.6 copy-start.4
  626.3 1.6 copy-start.3
  629.3 3.0 copy-start.2
  633.7 3.0 copy-start.1
  636.9 3.5 copy-start

commit v8 on v7

--- a/solution.py
+++ b/solution.py
@@ -999,6 +999,7 @@
     turned_copy.wait()
     scatter.near(2, mid_turned, up_low, 2)
     scatter.finish(0)
+    scatter.finish(1)
     scatter.near(2, mid_turned, up_low, 3)
     near.wait(8)
     near.wait(7)
@@ -1016,7 +1017,6 @@
     near.sent(5)
     near.sent(7)
     near.sent(8)
-    scatter.finish(1)
     scatter.finish(2)
 
 
@@ -1370,8 +1370,8 @@
     scatter.finish(1)
     scatter.near(3, normed_turned, query_low, 2)
     scatter.finish(2)
+    scatter.finish(4)
     scatter.near(3, normed_turned, query_low, 3)
-    scatter.finish(4)
     scatter.finish(3)
     for k in range(1, members):
         near.wait(2 + k)

time: 653 us -> 654 us (level)
  no operation moved by 1% of the time
where the time goes in v8:
time: 654 us; the launch traced here: 644 us
  Pallas kernels  610 us (93%)
  local copies, waits for them, and re-layouts  20.2 us (3%)
  other arithmetic  12.3 us (2%)
    pallas_call x1, Pallas kernels, forward(): pl.pallas_call(functools.partial(forward_kernel, lines, members), out_sha...  289 us
    pallas_call x1, Pallas kernels, retention_backward(): pl.pallas_call(functools.partial(retention_kernel, lines, members), out_s...  187 us
    pallas_call x1, Pallas kernels, feed_backward(): pl.pallas_call(functools.partial(feed_kernel, lines, members), out_shape=...  134 us
    unnamed x40, local copies, waits for them, and re-layouts  15 us

profile of v8, /device:TPU:8, one launch (start us, length us, event | category | flops | bytes accessed | tf_op | source)
XLA Modules:
  0.0 643.5 jit_solution(1261720231315848009)
XLA Ops:
  0.6 0.0 copy-start.5
  0.7 0.0 copy-start.6
  0.7 0.6 broadcast_in_dim.2.refs_7_.refs_10_
  1.3 0.7 stack.9
  2.0 0.7 stack.10
  2.7 0.6 pad_maximum_fusion.refs_2_
  3.3 1.7 copy.31.refs_5_.refs_8_
  5.0 3.0 multiply_sine_fusion
  8.0 0.9 slice_dynamic-update-slice_fusion.15
  8.9 0.9 slice_dynamic-update-slice_fusion.14
  9.8 0.0 copy-done.6
  10.0 0.0 copy-done.5
  10.2 0.0 copy-start.8
  10.2 1.0 copy-done.8
  11.2 0.0 copy-start.7
  11.2 1.0 copy-done.7
  12.2 288.7 %forward.1 = (bf16[2048,1024]{1,0:T(8,128)(2,1)}, bf16[4,256,2048]{2,1,0:T(8,128)(2,1)}, f32[8,8,256]{2,1,0:T(8,128)}, bf16[8,256,512]{2,1,0:T(8,128)(2,1)}, bf1...) custom-call(bf16[256,2048]{1,0:T(8,128)(2,1)} %copy-done.7, ...), custom_call_target="tpu_custom_call" | custom-call | flops 99999997952 | bytes 1000000000 | tf_op jit(solution)/shard_map/forward/pallas_call | solution.py:534
  300.9 133.8 %feed_backward.1 = (bf16[4,256,864]{2,1,0:T(8,128)(2,1)}, bf16[4,256,864]{2,1,0:T(8,128)(2,1)}, bf16[4,256,864]{2,1,0:T(8,128)(2,1)}, bf16[4,256,2048]{2,1,0:T(8...) custom-call(bf16[2048,1024]{1,0:T(8,128)(2,1)} %get-tuple-element.50, ...), custom_call_target="tpu_custom_call" | custom-call | flops 99999997952 | bytes 1000000000 | tf_op jit(solution)/shard_map/feed_backward/pallas_call | solution.py:1044
  434.7 187.3 %retention_backward.1 = (bf16[4,256,864]{2,1,0:T(8,128)(2,1)}, bf16[4,256,864]{2,1,0:T(8,128)(2,1)}, bf16[4,256,864]{2,1,0:T(8,128)(2,1)}, bf16[4,256,512]{2,1,0...) custom-call(bf16[4,256,864]{2,1,0:T(8,128)(2,1)} %get-tuple-element., ...), custom_call_target="tpu_custom_call" | custom-call | flops 99999997952 | bytes 1000000000 | tf_op jit(solution)/shard_map/retention_backward/pallas_call | solution.py:1398
  622.0 0.0 copy-start.4
  622.0 1.4 fusion
  623.4 2.1 add_bitcast_fusion.7
  625.5 2.1 add_bitcast_fusion.6
  627.6 0.0 copy-done.4
  627.6 0.0 copy-start.3
  627.6 0.2 add_bitcast_fusion.5
  627.9 1.2 copy.33
  629.1 0.1 copy-done.3
  629.2 0.2 add_bitcast_fusion.4
  629.4 1.2 copy.34
  630.6 0.0 copy-start.2
  630.6 1.8 add_bitcast_fusion.3
  632.4 1.2 copy.35
  633.6 0.0 copy-done.2
  633.6 0.2 add_bitcast_fusion.2
  633.8 1.2 copy.36
  635.0 0.0 copy-start.1
  635.0 1.8 add_bitcast_fusion.1
  636.8 1.2 copy.37
  638.0 0.0 copy-done.1
  638.0 0.2 add_bitcast_fusion
  638.2 0.0 copy-start
  638.3 1.2 copy.38
  639.5 2.3 copy.55
  641.8 0.0 copy-done
  641.8 1.3 copy.56
  (18 shorter events, 0.3 us)
Async XLA Ops:
  0.6 9.3 %copy-start.5 = (bf16[1,256,2048]{2,1,0:T(8,128)(2,1)S(1)}, bf16[1,256,2048]{2,1,0:T(8,128)(2,1)}, u32[]{:S(2)}) copy-start(bf16[1,256,2048]{2,1,0:T(8,128)(2,1)} %param.14) | copy-start | bytes 3145732
  0.7 9.2 %copy-start.6 = (bf16[1,256,2048]{2,1,0:T(8,128)(2,1)S(1)}, bf16[1,256,2048]{2,1,0:T(8,128)(2,1)}, u32[]{:S(2)}) copy-start(bf16[1,256,2048]{2,1,0:T(8,128)(2,1)} %param.13) | copy-start | bytes 3145732
  10.2 1.0 copy-start.8
  11.2 1.0 copy-start.7
  622.0 5.6 copy-start.4
  627.6 1.6 copy-start.3
  630.6 3.0 copy-start.2
  635.0 3.0 copy-start.1
  638.2 3.5 copy-start
